TPU v7x, 32 devices: a whole 2x2x4 slice. The times are simulated.
32 devices in a mesh: band: 8 (over z, x), rep: 4 (over y, core).
Axes of the slice: x: 2, y: 2, z: 4, core: 2. Of those that a mesh axis runs over, the one named last changes fastest.
Arguments:
- feats: bfloat16 [131072, 128], P(('band', 'rep')), may hold values from -6 to 6
- tile_vals: bfloat16 [1024, 3, 128, 128], P(('band', 'rep')), may hold values from -0.3125 to 0.3125
- tile_offs: int32 [1024, 3], P(('band', 'rep')), may hold values from -16 to 16, as said below
- w_in: bfloat16 [2, 256, 128], replicated, may hold values from -0.375 to 0.375
- bias_in: float32 [2, 128], replicated, may hold values from -3 to 3
- w_out: bfloat16 [2, 128, 128], replicated, may hold values from -0.5 to 0.5
- gain: float32 [2, 128], replicated, may hold values from 0.1 to 1.9
- cot: bfloat16 [131072, 128], P(('band', 'rep')), may hold values from -6 to 6
Outputs:
- out_feats: bfloat16 [131072, 128], P(('band', 'rep'))
- grad_feats: float32 [131072, 128], P(('band', 'rep'))
- grad_w_in: float32 [2, 256, 128], replicated
- grad_bias_in: float32 [2, 128], replicated
- grad_w_out: float32 [2, 128, 128], replicated
- grad_gain: float32 [2, 128], replicated
Inputs may be any that keep to these rules, and one draw needn't show every extreme that they name: `tile_offs`: in every block row slot 0 is 0, slot 1 lies in -16 to -1 and slot 2 in 1 to 16; block rows whose index is a multiple of 16 have -16 and 16.
All inputs are finite; a program needn't handle non-finite values.
Results may differ from a plain program's by a relative error of at most 0.0085.
Values may be sent and summed in bfloat16 or wider, within the bound.
No kernel may reach another device: no remote copies, remote signals or barrier semaphores. Data moves between devices by JAX's collectives and lax.ppermute only.
A program may use at most 128 MiB of HBM per device.

v0:
```python
import math

import jax
import jax.numpy as jnp
from jax import lax
from jax.sharding import PartitionSpec as P

HALO_BLK = 16


def from_behind(x, axis, by):
    peers = lax.axis_size(axis)
    return lax.ppermute(x, axis, [(i, (i + by) % peers) for i in range(peers)])


def layer_forward(feats_now, agg_now, weight_in, bias_now, weight_out, gain_now):
    joined = jnp.concatenate([feats_now, agg_now], axis=1)
    pre_act = jnp.dot(joined, weight_in, preferred_element_type=jnp.float32) + bias_now
    act_now = jax.nn.silu(pre_act).astype(jnp.bfloat16)
    mixed = jnp.dot(act_now, weight_out, preferred_element_type=jnp.float32)
    centred = mixed - jnp.mean(mixed, axis=1, keepdims=True)
    inv_std = lax.rsqrt(jnp.mean(centred * centred, axis=1, keepdims=True) + 1e-05)
    normed = centred * inv_std
    feats_next = (feats_now.astype(jnp.float32) + normed * gain_now).astype(jnp.bfloat16)
    return (feats_next, (joined, pre_act, act_now, normed, inv_std))


def layer_backward(grad_now, saved, weight_in, weight_out, gain_now):
    joined, pre_act, act_now, normed, inv_std = saved
    feat_width = gain_now.shape[0]
    grad_gain = jnp.sum(grad_now * normed, axis=0)
    grad_norm = grad_now * gain_now
    grad_mix = inv_std * (
        grad_norm
        - jnp.mean(grad_norm, axis=1, keepdims=True)
        - normed * jnp.mean(grad_norm * normed, axis=1, keepdims=True)
    )
    grad_mix_b = grad_mix.astype(jnp.bfloat16)
    grad_wout = lax.dot_general(
        act_now, grad_mix_b, (((0,), (0,)), ((), ())), preferred_element_type=jnp.float32
    )
    grad_act = lax.dot_general(
        grad_mix_b, weight_out, (((1,), (1,)), ((), ())), preferred_element_type=jnp.float32
    )
    sigma = jax.nn.sigmoid(pre_act)
    grad_pre = grad_act * sigma * (1.0 + pre_act * (1.0 - sigma))
    grad_bias = jnp.sum(grad_pre, axis=0)
    grad_pre_b = grad_pre.astype(jnp.bfloat16)
    grad_win = lax.dot_general(
        joined, grad_pre_b, (((0,), (0,)), ((), ())), preferred_element_type=jnp.float32
    )
    grad_cat = lax.dot_general(
        grad_pre_b, weight_in, (((1,), (1,)), ((), ())), preferred_element_type=jnp.float32
    )
    grad_next = grad_now + grad_cat[:, :feat_width]
    grad_agg = grad_cat[:, feat_width:].astype(jnp.bfloat16)
    return (grad_next, grad_agg, grad_win, grad_bias, grad_wout, grad_gain)


def per_device(feats, tile_vals, tile_offs, w_in, bias_in, w_out, gain, cot):
    node_rows = feats.shape[0]
    feat_width = feats.shape[1]
    tile_width = tile_vals.shape[2]
    block_count = node_rows // tile_width
    rim_rows = HALO_BLK * tile_width
    columns = jnp.arange(block_count, dtype=jnp.int32)[:, None] + HALO_BLK + tile_offs
    flat_columns = columns.reshape(-1)
    rim_index = jnp.arange(HALO_BLK, dtype=jnp.int32)
    low_tiles, low_offs = from_behind(
        (tile_vals[block_count - HALO_BLK :, 2], tile_offs[block_count - HALO_BLK :, 2]),
        ("band", "rep"),
        1,
    )
    high_tiles, high_offs = from_behind(
        (tile_vals[:HALO_BLK, 1], tile_offs[:HALO_BLK, 1]), ("band", "rep"), -1
    )
    low_targets = rim_index + low_offs
    high_targets = block_count + HALO_BLK + rim_index + high_offs
    layer_count = w_in.shape[0]
    feats_now = feats
    stored = []
    for layer_idx in range(layer_count):
        from_below = from_behind(feats_now[node_rows - rim_rows :], ("band", "rep"), 1)
        from_above = from_behind(feats_now[:rim_rows], ("band", "rep"), -1)
        blocks = jnp.concatenate([from_below, feats_now, from_above], axis=0).reshape(
            block_count + 2 * HALO_BLK, tile_width, feat_width
        )
        pieces = blocks[columns]
        summed = jnp.einsum("bkij,bkjd->bid", tile_vals, pieces, preferred_element_type=jnp.float32)
        agg_now = summed.astype(jnp.bfloat16).reshape(node_rows, feat_width)
        feats_now, saved = layer_forward(
            feats_now,
            agg_now,
            w_in[layer_idx],
            bias_in[layer_idx],
            w_out[layer_idx],
            gain[layer_idx],
        )
        stored.append(saved)
    grad_now = cot.astype(jnp.float32)
    win_list, bias_list, wout_list, gain_list = ([], [], [], [])
    for layer_idx in reversed(range(layer_count)):
        grad_now, grad_agg, grad_win, grad_bias, grad_wout, grad_gain = layer_backward(
            grad_now, stored[layer_idx], w_in[layer_idx], w_out[layer_idx], gain[layer_idx]
        )
        grad_blocks = grad_agg.reshape(block_count, tile_width, feat_width)
        contrib = jnp.einsum(
            "bkij,bid->bkjd", tile_vals, grad_blocks, preferred_element_type=jnp.float32
        )
        extended = jnp.zeros((block_count + 2 * HALO_BLK, tile_width, feat_width), jnp.float32)
        extended = extended.at[flat_columns].add(contrib.reshape(-1, tile_width, feat_width))
        low_rim = from_behind(grad_agg[node_rows - rim_rows :], ("band", "rep"), 1)
        high_rim = from_behind(grad_agg[:rim_rows], ("band", "rep"), -1)
        low_contrib = jnp.einsum(
            "bij,bid->bjd",
            low_tiles,
            low_rim.reshape(HALO_BLK, tile_width, feat_width),
            preferred_element_type=jnp.float32,
        )
        high_contrib = jnp.einsum(
            "bij,bid->bjd",
            high_tiles,
            high_rim.reshape(HALO_BLK, tile_width, feat_width),
            preferred_element_type=jnp.float32,
        )
        extended = extended.at[low_targets].add(low_contrib)
        extended = extended.at[high_targets].add(high_contrib)
        grad_now = grad_now + extended.reshape(-1, feat_width)[rim_rows : rim_rows + node_rows]
        win_list.insert(0, grad_win)
        bias_list.insert(0, grad_bias)
        wout_list.insert(0, grad_wout)
        gain_list.insert(0, grad_gain)
    totals = lax.psum(
        (jnp.stack(win_list), jnp.stack(bias_list), jnp.stack(wout_list), jnp.stack(gain_list)),
        ("band", "rep"),
    )
    scale_factor = 1.0 / math.sqrt(node_rows * lax.axis_size("band") * lax.axis_size("rep"))
    return (
        feats_now,
        grad_now,
        totals[0] * scale_factor,
        totals[1] * scale_factor,
        totals[2] * scale_factor,
        totals[3] * scale_factor,
    )


def solution(mesh):
    placed = (
        P(("band", "rep"), None),
        P(("band", "rep"), None, None, None),
        P(("band", "rep"), None),
        P(),
        P(),
        P(),
        P(),
        P(("band", "rep"), None),
    )
    return jax.shard_map(
        per_device,
        mesh=mesh,
        in_specs=placed,
        out_specs=(P(("band", "rep"), None), P(("band", "rep"), None), P(), P(), P(), P()),
        check_vma=False,
    )
```

profile of v0, /device:TPU:1, one launch (start us, length us, event | category | flops | bytes accessed | tf_op | source)
XLA Modules:
  0.0 385.4 jit_solution(10275902553538116334)
XLA Ops:
  8.6 2.7 collective-permute-start
  19.4 9.2 %collective-permute-done = bf16[2048,128]{1,0:T(8,128)(2,1)S(1)} collective-permute-done((bf16[2048,128]{1,0:T(8,128)(2,1)S(1)}, bf16[2048,128]{1,0:T(8,128)(2,1)S(1)}, u32[]{:S(2)}, u32[]{:S(2)}) %collective-permute-start) | collective-permute-done | bytes 524320 | tf_op jit(solution)/shard_map/ppermute | solution.py:13
  32.6 4.4 %gather_fusion = bf16[96,128,128]{2,1,0:T(8,128)(2,1)} fusion(bf16[64,128,128]{2,1,0:T(8,128)(2,1)} %bitcast.146, s32[1024]{0:T(1024)S(1)} %pad_clamp_fusion), kind=kCustom, calls=%fused_computation | custom fusion | bytes 6291840 | tf_op jit(solution)/shard_map/gather | solution.py:88
  37.0 3.0 bitcast_convert_fusion.1
  48.7 8.3 %collective-permute-done.7 = s32[16]{0:T(128)S(1)} collective-permute-done((s32[16]{0:T(128)S(1)}, s32[16]{0:T(128)S(1)}, u32[]{:S(2)}, u32[]{:S(2)}) %collective-permute-start.7) | collective-permute-done | bytes 96 | tf_op jit(solution)/shard_map/ppermute | solution.py:13
  57.9 3.0 pad_maximum_fusion.2
  61.0 4.1 %copy.74 = bf16[8192,128]{1,0:T(8,128)(2,1)} copy(bf16[8192,128]{0,1:T(8,128)(2,1)} %pad_maximum_fusion.2) | data formatting | bytes 4194304 | tf_op jit(solution)/shard_map/reshape | solution.py:85
  65.0 4.3 %gather_fusion.1 = bf16[96,128,128]{2,1,0:T(8,128)(2,1)} fusion(bf16[64,128,128]{2,1,0:T(8,128)(2,1)} %bitcast.147, s32[1024]{0:T(1024)S(1)} %pad_clamp_fusion), kind=kCustom, calls=%fused_computation.1 | custom fusion | bytes 6291840 | tf_op jit(solution)/shard_map/gather | solution.py:88
  69.3 3.8 bitcast_convert_fusion
  83.3 2.6 fusion.51
  89.6 3.7 fusion.55
  93.3 6.6 %copy.48 = f32[96,128,128]{2,1,0:T(8,128)} copy(f32[96,128,128]{1,2,0:T(8,128)} %bitcast.145) | data formatting | bytes 12582912 | tf_op jit(solution)/shard_map/reshape | solution.py:111
  99.9 3.1 slice.130
  102.9 2.9 copy.82
  110.6 20.1 %scatter_fusion = f32[64,128,128]{2,1,0:T(8,128)} fusion(f32[64,128,128]{2,1,0:T(8,128)} %broadcast.118.clone, s32[96]{0:T(128)S(1)} %fusion.39, f32[96,128,128]{2,1,0:T(8,128)} %copy.48), kind=kCustom, calls=%fused_computation.2 | custom fusion | flops 1572864 | bytes 18874752 | tf_op jit(solution)/shard_map/scatter-add | solution.py:111
  145.8 3.8 scatter_fusion.1
  149.6 3.7 scatter_fusion.2
  153.3 3.1 slice.134
  156.5 2.9 copy.78
  159.4 4.2 %multiply_reduce_fusion = (f32[128]{0:T(128)S(1)}, f32[4096]{0:T(1024)S(1)}, f32[4096]{0:T(1024)S(1)}, f32[4096,128]{0,1:T(8,128)S(1)}) fusion(f32[4096,128]{0,1:T(8,128)} %copy-done.1, f32[4096]{0:T(1024)S(1)} %add_rsqrt_fusion.1, f32[4096]{0:T(1024)S(1)} %broadcast_multiply_fusion.7, f32[128]{0:T(128)S(1)} %get-tuple-element.46, f32[4096,128]{0,1:T(8,128)} %copy.78, ...), kind=kLoop, calls=%fused_computation.32 | loop fusion | flops 5758848 | bytes 9503744 | tf_op jit(solution)/shard_map/reduce_sum | solution.py:31
  174.9 39.8 %all-reduce = (f32[2,128]{1,0:T(2,128)S(1)}, f32[2,128]{1,0:T(2,128)S(1)}) all-reduce(f32[2,128]{1,0:T(2,128)S(1)} %pad_maximum_fusion.14, f32[2,128]{1,0:T(2,128)S(1)} %pad_maximum_fusion.15), channel_id=1, replica_groups=mesh['band'=8,'rep'=4] {'band','rep'}, use_global_device_ids=true, to_apply=%region_17.18 | all-reduce | flops 512 | bytes 4096 | tf_op jit(solution)/shard_map/psum | solution.py:133
  215.3 4.9 %fusion.56 = f32[32,128,3,128]{3,1,2,0:T(8,128)} fusion(bf16[32,128,128,1]{2,1,3,0:T(8,128)(2,1)} %bitcast.152, bf16[32,3,128,128]{3,2,1,0:T(8,128)(2,1)S(1)} %copy-done), kind=kOutput, calls=%fused_computation.128 | convolution fusion | flops 402653184 | bytes 10485760 | tf_op jit(solution)/shard_map/bkij,bid->bkjd/dot_general | solution.py:107
  220.2 3.4 collective-permute-start.10
  225.6 6.6 %copy.58 = f32[96,128,128]{2,1,0:T(8,128)} copy(f32[96,128,128]{1,2,0:T(8,128)} %bitcast.144) | data formatting | bytes 12582912 | tf_op jit(solution)/shard_map/reshape | solution.py:111
  238.3 20.2 %scatter_fusion.3 = f32[64,128,128]{2,1,0:T(8,128)} fusion(f32[64,128,128]{2,1,0:T(8,128)} %broadcast.118, s32[96]{0:T(128)S(1)} %fusion.39, f32[96,128,128]{2,1,0:T(8,128)} %copy.58), kind=kCustom, calls=%fused_computation.5 | custom fusion | flops 1572864 | bytes 18874752 | tf_op jit(solution)/shard_map/scatter-add | solution.py:111
  258.5 93.6 %all-reduce.4.cloned.1.call-done = (f32[2,256,128]{2,1,0:T(8,128)}, f32[2,128,128]{2,1,0:T(8,128)}) async-done(((f32[2,256,128]{2,1,0:T(8,128)}, f32[2,128,128]{2,1,0:T(8,128)}), (f32[2,256,128]{2,1,0:T(8,128)}, f32[2,128,128]{2,1,0:T(8,128)})) %all-reduce.4.cloned.1.call-update) | async-done | bytes 393232 | tf_op jit(solution)/shard_map/psum | solution.py:133
  359.0 3.4 scatter_fusion.4
  362.3 3.3 scatter_fusion.5
  365.6 3.1 slice.139
  368.8 3.1 copy.81
  371.8 3.9 %add_add_fusion = f32[4096,128]{0,1:T(8,128)} fusion(f32[4096,128]{0,1:T(8,128)} %copy.81, f32[4096,128]{0,1:T(8,128)S(1)} %copy-done.4, f32[4096,128]{0,1:T(8,128)} %copy.85), kind=kLoop, calls=%fused_computation.33 | loop fusion | flops 1048576 | bytes 8388608 | tf_op jit(solution)/shard_map/add | solution.py:128
  375.7 2.9 copy.65
  (151 shorter events, 83.3 us)
Async XLA Ops:
  7.2 10.5 %copy-start.9 = (bf16[4096,128]{1,0:T(8,128)(2,1)S(1)}, bf16[4096,128]{1,0:T(8,128)(2,1)}, u32[]{:S(2)}) copy-start(bf16[4096,128]{1,0:T(8,128)(2,1)} %param.8) | copy-start | bytes 3145732
  7.2 8.2 %copy-start.26 = (s32[32,3]{0,1:T(4,128)S(1)}, s32[32,3]{0,1:T(4,128)}, u32[]{:S(2)}) copy-start(s32[32,3]{0,1:T(4,128)} %param.10) | copy-start | bytes 1156
  7.2 344.9 %all-reduce.4.cloned.1.call-start = ((), (), s32[]{:S(2)}) async-start(), calls=%async_computation | async-start | bytes 786432 | tf_op jit(solution)/shard_map/psum | solution.py:133
  8.6 20.0 %collective-permute-start = (bf16[2048,128]{1,0:T(8,128)(2,1)S(1)}, bf16[2048,128]{1,0:T(8,128)(2,1)S(1)}, u32[]{:S(2)}, u32[]{:S(2)}) collective-permute-start(bf16[2048,128]{1,0:T(8,128)(2,1)S(1)} %get-tuple-element.41), channel_id=1, source_target_pairs={{0,1},{1,2},{2,3},{3,4},{4,5},{5,6},{6,7},{7,8},{8,9},{9,10},{10,1... | collective-permute-start | bytes 1572872 | tf_op jit(solution)/shard_map/ppermute | solution.py:13
  11.3 8.1 %copy-start.27 = (f32[2,128]{1,0:T(2,128)S(1)}, f32[2,128]{1,0:T(2,128)}, u32[]{:S(2)}) copy-start(f32[2,128]{1,0:T(2,128)} %param.12) | copy-start | bytes 3076
  11.3 8.1 %copy-start.28 = (f32[2,128]{1,0:T(2,128)S(1)}, f32[2,128]{1,0:T(2,128)}, u32[]{:S(2)}) copy-start(f32[2,128]{1,0:T(2,128)} %param.14) | copy-start | bytes 3076
  11.3 19.8 %collective-permute-start.1 = (bf16[2048,128]{1,0:T(8,128)(2,1)S(1)}, bf16[2048,128]{1,0:T(8,128)(2,1)S(1)}, u32[]{:S(2)}, u32[]{:S(2)}) collective-permute-start(bf16[2048,128]{1,0:T(8,128)(2,1)S(1)} %get-tuple-element.42), channel_id=1, source_target_pairs={{0,31},{1,0},{2,1},{3,2},{4,3},{5,4},{6,5},{7,6},{8,7},{9,8},{10,9... | collective-permute-start | bytes 1572872 | tf_op jit(solution)/shard_map/ppermute | solution.py:13
  13.6 121.9 %collective-permute-start.6 = (bf16[16,128,128]{2,1,0:T(8,128)(2,1)}, bf16[16,128,128]{2,1,0:T(8,128)(2,1)}, u32[]{:S(2)}, u32[]{:S(2)}) collective-permute-start(bf16[16,128,128]{2,1,0:T(8,128)(2,1)} %get-tuple-element.32), channel_id=1, source_target_pairs={{0,1},{1,2},{2,3},{3,4},{4,5},{5,6},{6,7},{7,8},{8,9},{9,10},{10,1... | collective-permute-start | bytes 1572872 | tf_op jit(solution)/shard_map/ppermute | solution.py:13
  15.4 33.2 %collective-permute-start.4 = (s32[16]{0:T(128)S(1)}, s32[16]{0:T(128)S(1)}, u32[]{:S(2)}, u32[]{:S(2)}) collective-permute-start(s32[16]{0:T(128)S(1)} %get-tuple-element.44), channel_id=1, source_target_pairs={{0,1},{1,2},{2,3},{3,4},{4,5},{5,6},{6,7},{7,8},{8,9},{9,10},{10,1... | collective-permute-start | bytes 200 | tf_op jit(solution)/shard_map/ppermute | solution.py:13
  15.4 125.2 %collective-permute-start.9 = (bf16[16,128,128]{2,1,0:T(8,128)(2,1)}, bf16[16,128,128]{2,1,0:T(8,128)(2,1)}, u32[]{:S(2)}, u32[]{:S(2)}) collective-permute-start(bf16[16,128,128]{2,1,0:T(8,128)(2,1)} %get-tuple-element.31), channel_id=1, source_target_pairs={{0,31},{1,0},{2,1},{3,2},{4,3},{5,4},{6,5},{7,6},{8,7},{9,8},{10,9... | collective-permute-start | bytes 1572872 | tf_op jit(solution)/shard_map/ppermute | solution.py:13
  32.6 4.4 %copy-start = (bf16[32,3,128,128]{3,2,1,0:T(8,128)(2,1)S(1)}, bf16[32,3,128,128]{3,2,1,0:T(8,128)(2,1)}, u32[]{:S(2)}) copy-start(bf16[32,3,128,128]{3,2,1,0:T(8,128)(2,1)} %param.9) | copy-start | bytes 9437188
  37.0 3.0 copy-start.10
  37.0 3.0 copy-start.22
  40.0 2.1 copy-start.17
  40.0 2.1 copy-start.25
  42.1 2.0 copy-start.15
  45.8 12.1 %collective-permute-start.2 = (bf16[2048,128]{0,1:T(8,128)(2,1)}, bf16[2048,128]{0,1:T(8,128)(2,1)}, u32[]{:S(2)}, u32[]{:S(2)}) collective-permute-start(bf16[2048,128]{0,1:T(8,128)(2,1)} %get-tuple-element.39), channel_id=1, source_target_pairs={{0,1},{1,2},{2,3},{3,4},{4,5},{5,6},{6,7},{7,8},{8,9},{9,10},{10,1... | collective-permute-start | bytes 1572872 | tf_op jit(solution)/shard_map/ppermute | solution.py:13
  45.8 12.1 %collective-permute-start.3 = (bf16[2048,128]{0,1:T(8,128)(2,1)}, bf16[2048,128]{0,1:T(8,128)(2,1)}, u32[]{:S(2)}, u32[]{:S(2)}) collective-permute-start(bf16[2048,128]{0,1:T(8,128)(2,1)} %get-tuple-element.40), channel_id=1, source_target_pairs={{0,31},{1,0},{2,1},{3,2},{4,3},{5,4},{6,5},{7,6},{8,7},{9,8},{10,9... | collective-permute-start | bytes 1572872 | tf_op jit(solution)/shard_map/ppermute | solution.py:13
  48.6 8.3 %collective-permute-start.7 = (s32[16]{0:T(128)S(1)}, s32[16]{0:T(128)S(1)}, u32[]{:S(2)}, u32[]{:S(2)}) collective-permute-start(s32[16]{0:T(128)S(1)} %get-tuple-element.43), channel_id=1, source_target_pairs={{0,31},{1,0},{2,1},{3,2},{4,3},{5,4},{6,5},{7,6},{8,7},{9,8},{10,9... | collective-permute-start | bytes 200 | tf_op jit(solution)/shard_map/ppermute | solution.py:13
  83.3 2.6 copy-start.19
  87.1 48.4 %collective-permute-start.5 = (bf16[2048,128]{1,0:T(8,128)(2,1)}, bf16[2048,128]{1,0:T(8,128)(2,1)}, u32[]{:S(2)}, u32[]{:S(2)}) collective-permute-start(bf16[2048,128]{1,0:T(8,128)(2,1)} %get-tuple-element.38), channel_id=1, source_target_pairs={{0,1},{1,2},{2,3},{3,4},{4,5},{5,6},{6,7},{7,8},{8,9},{9,10},{10,1... | collective-permute-start | bytes 1572872 | tf_op jit(solution)/shard_map/ppermute | solution.py:13
  99.9 40.8 %collective-permute-start.8 = (bf16[2048,128]{1,0:T(8,128)(2,1)}, bf16[2048,128]{1,0:T(8,128)(2,1)}, u32[]{:S(2)}, u32[]{:S(2)}) collective-permute-start(bf16[2048,128]{1,0:T(8,128)(2,1)} %get-tuple-element.37), channel_id=1, source_target_pairs={{0,31},{1,0},{2,1},{3,2},{4,3},{5,4},{6,5},{7,6},{8,7},{9,8},{10,9... | collective-permute-start | bytes 1572872 | tf_op jit(solution)/shard_map/ppermute | solution.py:13
  130.7 2.2 copy-start.8
  130.7 2.2 copy-start.20
  159.4 4.3 %copy-start.2 = (f32[4096,128]{0,1:T(8,128)S(1)}, f32[4096,128]{0,1:T(8,128)}, u32[]{:S(2)}) copy-start(f32[4096,128]{0,1:T(8,128)} %copy-done.1) | copy-start | bytes 6291460
  163.7 2.0 copy-start.13
  215.3 9.0 %copy-start.23 = (f32[1,256,128]{2,1,0:T(8,128)S(1)}, f32[1,256,128]{2,1,0:T(8,128)}, u32[]{:S(2)}) copy-start(f32[1,256,128]{2,1,0:T(8,128)} %fusion.14) | copy-start | bytes 393220
  215.3 9.0 %copy-start.24 = (f32[1,256,128]{2,1,0:T(8,128)S(1)}, f32[1,256,128]{2,1,0:T(8,128)}, u32[]{:S(2)}) copy-start(f32[1,256,128]{2,1,0:T(8,128)} %fusion.13) | copy-start | bytes 393220
  220.2 135.1 %collective-permute-start.10 = (bf16[2048,128]{1,0:T(8,128)(2,1)}, bf16[2048,128]{1,0:T(8,128)(2,1)S(1)}, u32[]{:S(2)}, u32[]{:S(2)}) collective-permute-start(bf16[2048,128]{1,0:T(8,128)(2,1)} %get-tuple-element.36), channel_id=1, source_target_pairs={{0,1},{1,2},{2,3},{3,4},{4,5},{5,6},{6,7},{7,8},{8,9},{9,10},{10,1... | collective-permute-start | bytes 1572872 | tf_op jit(solution)/shard_map/ppermute | solution.py:13
  225.6 6.7 %copy-start.21 = (bf16[2048,128]{1,0:T(8,128)(2,1)S(1)}, bf16[2048,128]{1,0:T(8,128)(2,1)}, u32[]{:S(2)}) copy-start(bf16[2048,128]{1,0:T(8,128)(2,1)} %get-tuple-element.35) | copy-start | bytes 1572868
  232.2 124.8 %collective-permute-start.11 = (bf16[2048,128]{1,0:T(8,128)(2,1)S(1)}, bf16[2048,128]{1,0:T(8,128)(2,1)}, u32[]{:S(2)}, u32[]{:S(2)}) collective-permute-start(bf16[2048,128]{1,0:T(8,128)(2,1)S(1)} %copy-done.21), channel_id=1, source_target_pairs={{0,31},{1,0},{2,1},{3,2},{4,3},{5,4},{6,5},{7,6},{8,7},{9,8},{10,9... | collective-permute-start | bytes 1572872 | tf_op jit(solution)/shard_map/ppermute | solution.py:13
  368.8 3.1 copy-start.4
  (11 other events, 15.1 us)
Sparse Core Ops, SparseCore 0:
  225.1 126.8 all-reduce.3
where the time goes:
time: 389 us; the launch traced here: 385 us
  waiting for transfers between devices  115 us (30%)
  local copies, waits for them, and re-layouts  83.5 us (21%)
  other arithmetic  77.2 us (20%)
  matrix products  42.9 us (11%)
  blocking collectives  39.8 us (10%)
  between operations  14.5 us (4%)
  starting transfers between devices  13 us (3%)
    psum x1, waiting for transfers between devices, per_device(): lax.psum((jnp.stack(win_list), jnp.stack(bias_list), jnp.stack(wout_list)...  93.6 us
    scatter-add x2, other arithmetic, per_device(): extended.at[flat_columns].add(contrib.reshape(-1, tile_width, feat_width))  40.3 us
    psum x1, blocking collectives, per_device(): lax.psum((jnp.stack(win_list), jnp.stack(bias_list), jnp.stack(wout_list)...  39.8 us
    ppermute x12, waiting for transfers between devices, from_behind(): return lax.ppermute(x, axis, [(i, (i + by) % peers) for i in range(peers)])  21 us
    unnamed x66, local copies, waits for them, and re-layouts  18.8 us
    reshape x2, local copies, waits for them, and re-layouts, per_device(): contrib.reshape(-1, tile_width, feat_width)  13.2 us
    ppermute x12, starting transfers between devices, from_behind(): return lax.ppermute(x, axis, [(i, (i + by) % peers) for i in range(peers)])  13 us
    slice x4, local copies, waits for them, and re-layouts, per_device(): extended.reshape(-1, feat_width)[rim_rows:rim_rows + node_rows]  12.2 us
  transfers between devices with their start and end apart: 13, of which 5 were waited for; matrix products, arithmetic and copies ran while one was open for 36% of the time, Pallas kernels for 0%

commit v1 on v0

v1 whole, which is shorter than its diff:
```python
import math

import jax
import jax.numpy as jnp
from jax import lax
from jax.experimental import pallas as pl
from jax.experimental.pallas import tpu as pltpu
from jax.sharding import PartitionSpec as P

HALO = 16
EPS = 1e-05
AXES = ("band", "rep")
F32 = jnp.float32
BF16 = jnp.bfloat16
CH = 4
ANY = pl.BlockSpec(memory_space=pl.ANY)
SMEM = pl.BlockSpec(memory_space=pltpu.SMEM)
VMEM = pl.BlockSpec(memory_space=pltpu.VMEM)


def nt(a, b):
    return lax.dot_general(a, b, (((1,), (1,)), ((), ())), preferred_element_type=F32)


def nn(a, b):
    return jnp.dot(a, b, preferred_element_type=F32)


def eye(n):
    rows = lax.broadcasted_iota(jnp.int32, (n, n), 0)
    cols = lax.broadcasted_iota(jnp.int32, (n, n), 1)
    return (rows == cols).astype(BF16)


def column(row, width):
    return jnp.transpose(jnp.broadcast_to(row, (width, row.shape[1])))


def lanes(parts):
    return jnp.concatenate(parts, axis=1)


def widen(block, times):
    return lanes([block] * times)


def sigmoid(v):
    return 0.5 + 0.5 * jnp.tanh(0.5 * v)


def parity():
    place = lax.axis_index("band") * lax.axis_size("rep") + lax.axis_index("rep")
    return lax.rem(place, 2)


def start_all(copies):
    for c in copies:
        c.start()


def wait_all(copies):
    for c in copies:
        c.wait()


def swap(x, far):
    n = lax.axis_size("band") * lax.axis_size("rep")
    pairs = []
    for c in range(n // 2):
        a, b = (2 * c, 2 * c + 1) if not far else (2 * c + 1, (2 * c + 2) % n)
        pairs += [(a, b), (b, a)]
    return lax.ppermute(x, AXES, pairs)


def routed(even, start_even, start_odd):
    @pl.when(even)
    def _():
        start_all(start_even)

    @pl.when(jnp.logical_not(even))
    def _():
        start_all(start_odd)


def inner_tiles(ext, tiles, offs, part, it, first):
    slot = jnp.where(it * CH < HALO, 2, 1)
    for s in range(CH):
        b = it * CH + s
        col = b + offs[b, slot]
        left = lanes([ext[first + b], ext[first + col]])
        right = lanes([tiles[b, 0], tiles[b, slot]])
        part[b] = nt(left, right)


def load_tiles(tiles_hbm, tiles, sem, steps):
    return [
        pltpu.make_async_copy(
            tiles_hbm.at[pl.ds(i * CH, CH)], tiles.at[pl.ds(i * CH, CH)], sem.at[i]
        )
        for i in range(steps)
    ]


def inner0_kernel(nb, offs, x_hbm, tiles_hbm, h_hbm, part_hbm, x, tiles, h, part, sem, tsem):
    steps = nb // CH
    blk = tiles.shape[2]
    get_x = pltpu.make_async_copy(x_hbm, x, sem.at[0])
    get_t = load_tiles(tiles_hbm, tiles, tsem, steps)
    get_x.start()
    start_all(get_t)
    one = eye(blk)
    get_x.wait()

    def turn(it, c):
        for s in range(CH):
            b = it * CH + s
            h[b] = nt(one, x[pl.ds(b * blk, blk)]).astype(BF16)
        return c

    lax.fori_loop(0, steps, turn, 0)
    put_h = pltpu.make_async_copy(h, h_hbm, sem.at[1])
    put_h.start()

    def step(it, c):
        pltpu.make_async_copy(
            tiles_hbm.at[pl.ds(it * CH, CH)], tiles.at[pl.ds(it * CH, CH)], tsem.at[it]
        ).wait()
        inner_tiles(h, tiles, offs, part, it, 0)
        return c

    lax.fori_loop(0, steps, step, 0)
    put_p = pltpu.make_async_copy(part, part_hbm, sem.at[2])
    put_p.start()
    put_h.wait()
    put_p.wait()


def inner1_kernel(
    nb, offs, h_hbm, tiles_hbm, cot_hbm, part_hbm, cott_hbm, h, tiles, cot, cott, part, sem, tsem
):
    steps = nb // CH
    blk = tiles.shape[2]
    get_h = pltpu.make_async_copy(h_hbm, h, sem.at[0])
    get_t = load_tiles(tiles_hbm, tiles, tsem, steps)
    get_c = pltpu.make_async_copy(cot_hbm, cot, sem.at[1])
    get_h.start()
    start_all(get_t)
    get_c.start()
    get_h.wait()

    def step(it, c):
        pltpu.make_async_copy(
            tiles_hbm.at[pl.ds(it * CH, CH)], tiles.at[pl.ds(it * CH, CH)], tsem.at[it]
        ).wait()
        inner_tiles(h, tiles, offs, part, it, 0)
        return c

    lax.fori_loop(0, steps, step, 0)
    put_p = pltpu.make_async_copy(part, part_hbm, sem.at[2])
    put_p.start()
    get_c.wait()
    one = eye(blk)

    def turn(it, c):
        for s in range(CH):
            b = it * CH + s
            cott[b] = nt(one, cot[pl.ds(b * blk, blk)]).astype(BF16)
        return c

    lax.fori_loop(0, steps, turn, 0)
    put_c = pltpu.make_async_copy(cott, cott_hbm, sem.at[3])
    put_c.start()
    put_p.wait()
    put_c.wait()


def edge_tiles(tiles_hbm, rim, sem):
    return [
        pltpu.make_async_copy(tiles_hbm.at[pl.ds(0, HALO), 1], rim.at[pl.ds(0, HALO)], sem.at[0]),
        pltpu.make_async_copy(
            tiles_hbm.at[pl.ds(HALO, HALO), 2], rim.at[pl.ds(HALO, HALO)], sem.at[1]
        ),
    ]


def edge_column(offs, it, s):
    b = it * CH + s
    return b + HALO + offs[b, jnp.where(it * CH < HALO, 1, 2)]


def forward_step(it, ext, part, rim, offs, w1t, w2t, bias, gain):
    agg = []
    for s in range(CH):
        b = it * CH + s
        agg.append((part[b] + nt(ext[edge_column(offs, it, s)], rim[b])).astype(BF16))
    agg = lanes(agg)
    feats = lanes([ext[HALO + it * CH + s] for s in range(CH)])
    joined = jnp.concatenate([feats, agg], axis=0)
    pre = nn(w1t, joined) + widen(bias[...], CH)
    sig = sigmoid(pre)
    act = (pre * sig).astype(BF16)
    mix = nn(w2t, act)
    centred = mix - jnp.mean(mix, axis=0, keepdims=True)
    inv = lax.rsqrt(jnp.mean(centred * centred, axis=0, keepdims=True) + EPS)
    xhat = centred * inv
    after = (feats.astype(F32) + xhat * widen(gain[...], CH)).astype(BF16)
    return agg, pre, sig, act, xhat, inv, after


def backward_step(grad, xhat, inv, slope, w1, w2, gain):
    gx = grad * widen(gain[...], CH)
    gmix = inv * (
        gx
        - jnp.mean(gx, axis=0, keepdims=True)
        - xhat * jnp.mean(gx * xhat, axis=0, keepdims=True)
    )
    gmix = gmix.astype(BF16)
    gpre = nn(w2, gmix) * slope
    gpre_b = gpre.astype(BF16)
    gcat = nn(w1, gpre_b)
    width = grad.shape[0]
    return gmix, gpre, gpre_b, gcat[:width], gcat[width:].astype(BF16)


def cut(wide, s, blk):
    return wide[:, s * blk : (s + 1) * blk]


def fold(wide, blk):
    total = cut(wide, 0, blk)
    for s in range(1, CH):
        total = total + cut(wide, s, blk)
    return total


def push_edge(it, gagg, acc, rim, offs, blk):
    for s in range(CH):
        col = edge_column(offs, it, s)
        acc[col] += nn(cut(gagg, s, blk), rim[it * CH + s])


def outgoing(acc, send, nb, near_hbm, far_hbm, sem):
    for b in range(HALO):
        send[b] = acc[b].astype(BF16)
        send[HALO + b] = acc[HALO + nb + b].astype(BF16)
    send_rims(send, 0, HALO, near_hbm, far_hbm, sem)


def send_rims(buf, low, high, near_hbm, far_hbm, sem):
    even = parity() == 0
    lo, hi = buf.at[pl.ds(low, HALO)], buf.at[pl.ds(high, HALO)]
    routed(
        even,
        [
            pltpu.make_async_copy(lo, far_hbm, sem.at[0]),
            pltpu.make_async_copy(hi, near_hbm, sem.at[1]),
        ],
        [
            pltpu.make_async_copy(hi, far_hbm, sem.at[0]),
            pltpu.make_async_copy(lo, near_hbm, sem.at[1]),
        ],
    )
    pltpu.make_async_copy(lo, far_hbm, sem.at[0]).wait()
    pltpu.make_async_copy(hi, near_hbm, sem.at[1]).wait()


def fetch_rims(near_hbm, far_hbm, lo, hi, sem):
    routed(
        parity() == 0,
        [
            pltpu.make_async_copy(far_hbm, lo, sem.at[0]),
            pltpu.make_async_copy(near_hbm, hi, sem.at[1]),
        ],
        [
            pltpu.make_async_copy(near_hbm, lo, sem.at[0]),
            pltpu.make_async_copy(far_hbm, hi, sem.at[1]),
        ],
    )
    return [
        pltpu.make_async_copy(near_hbm, lo, sem.at[0]),
        pltpu.make_async_copy(far_hbm, hi, sem.at[1]),
    ]


def node0_kernel(
    nb, offs, near, far, h_hbm, part_hbm, tiles_hbm, w1t, w2t, bias, gain,
    near_out, far_out, h1_hbm, agg_hbm, act_hbm, slope_hbm, xhat_hbm, inv_hbm,
    halo, ext, part, rim, h1, agg, act, slope, xhat, inv, bcol, gcol, insem, outsem, edgesem,
):
    blk = rim.shape[1]
    steps = nb // CH
    rows = HALO * blk
    get = fetch_rims(near, far, halo.at[pl.ds(0, rows)], halo.at[pl.ds(rows, rows)], insem)
    get_h = pltpu.make_async_copy(h_hbm, ext.at[pl.ds(HALO, nb)], insem.at[2])
    get_p = pltpu.make_async_copy(part_hbm, part, insem.at[3])
    get_t = edge_tiles(tiles_hbm, rim, edgesem)
    start_all([get_h, get_p, *get_t])
    one = eye(blk)
    bcol[...] = column(bias[...], blk)
    gcol[...] = column(gain[...], blk)
    wait_all(get)

    def turn(it, c):
        for s in range(CH):
            b = it * CH + s
            ext[b] = nt(one, halo[pl.ds(b * blk, blk)]).astype(BF16)
            ext[HALO + nb + b] = nt(one, halo[pl.ds(rows + b * blk, blk)]).astype(BF16)
        return c

    lax.fori_loop(0, HALO // CH, turn, 0)
    wait_all([get_h, get_p, *get_t])

    def step(it, c):
        agg_w, pre, sig, act_w, xhat_w, inv_w, after = forward_step(
            it, ext, part, rim, offs, w1t[...], w2t[...], bcol, gcol
        )
        slope_w = (sig * (1.0 + pre * (1.0 - sig))).astype(BF16)
        xhat_b = xhat_w.astype(BF16)
        for s in range(CH):
            b = it * CH + s
            agg[b] = cut(agg_w, s, blk)
            act[b] = cut(act_w, s, blk)
            slope[b] = cut(slope_w, s, blk)
            xhat[b] = cut(xhat_b, s, blk)
            inv[b] = cut(inv_w, s, blk)
            h1[b] = cut(after, s, blk)
        return c

    lax.fori_loop(0, steps, step, 0)
    puts = [
        pltpu.make_async_copy(v, v_hbm, outsem.at[2 + i])
        for i, (v, v_hbm) in enumerate(
            [(h1, h1_hbm), (agg, agg_hbm), (act, act_hbm), (slope, slope_hbm), (xhat, xhat_hbm), (inv, inv_hbm)]
        )
    ]
    start_all(puts)
    send_rims(h1, 0, nb - HALO, near_out, far_out, outsem)
    wait_all(puts)


def node1_kernel(
    nb, offs, near, far, h_hbm, part_hbm, tiles_hbm, cott_hbm, w1t, w2t, w1, w2, bias, gain,
    near_out, far_out, h2_hbm, agg_hbm, act_hbm, gmix_hbm, gpre_hbm, gagg_hbm, acc_hbm, gb, gg,
    ext, part, rim, cott, h2, agg, act, gmix, gpre, gagg, acc, send, bcol, gcol, insem, outsem, edgesem,
):
    blk = rim.shape[1]
    steps = nb // CH
    get = fetch_rims(near, far, ext.at[pl.ds(0, HALO)], ext.at[pl.ds(HALO + nb, HALO)], insem)
    get_h = pltpu.make_async_copy(h_hbm, ext.at[pl.ds(HALO, nb)], insem.at[2])
    get_p = pltpu.make_async_copy(part_hbm, part, insem.at[3])
    get_c = pltpu.make_async_copy(cott_hbm, cott, insem.at[4])
    get_t = edge_tiles(tiles_hbm, rim, edgesem)
    start_all([get_h, get_p, get_c, *get_t])
    bcol[...] = column(bias[...], blk)
    gcol[...] = column(gain[...], blk)
    gb[...] = jnp.zeros_like(gb)
    gg[...] = jnp.zeros_like(gg)

    def clear(it, c):
        for s in range(CH):
            acc[it * CH + s] = jnp.zeros(acc.shape[1:], F32)
        return c

    lax.fori_loop(0, acc.shape[0] // CH, clear, 0)
    wait_all([*get, get_h, get_p, get_c, *get_t])

    def step(it, c):
        agg_w, pre, sig, act_w, xhat, inv, after = forward_step(
            it, ext, part, rim, offs, w1t[...], w2t[...], bcol, gcol
        )
        slope = sig * (1.0 + pre * (1.0 - sig))
        grad = lanes([cott[it * CH + s] for s in range(CH)]).astype(F32)
        gg[...] += fold(grad * xhat, blk)
        gmix_w, gpre_f, gpre_w, gh, gagg_w = backward_step(
            grad, xhat, inv, slope, w1[...], w2[...], gcol
        )
        gb[...] += fold(gpre_f, blk)
        rest = grad + gh
        for s in range(CH):
            b = it * CH + s
            agg[b] = cut(agg_w, s, blk)
            act[b] = cut(act_w, s, blk)
            h2[b] = cut(after, s, blk)
            gmix[b] = cut(gmix_w, s, blk)
            gpre[b] = cut(gpre_w, s, blk)
            gagg[b] = cut(gagg_w, s, blk)
            acc[HALO + b] += cut(rest, s, blk)
        push_edge(it, gagg_w, acc, rim, offs, blk)
        return c

    lax.fori_loop(0, steps, step, 0)
    puts = [
        pltpu.make_async_copy(v, v_hbm, outsem.at[2 + i])
        for i, (v, v_hbm) in enumerate(
            [(h2, h2_hbm), (agg, agg_hbm), (act, act_hbm), (gmix, gmix_hbm), (gpre, gpre_hbm),
             (gagg, gagg_hbm), (acc.at[pl.ds(HALO, nb)], acc_hbm)]
        )
    ]
    start_all(puts)
    outgoing(acc, send, nb, near_out, far_out, outsem)
    wait_all(puts)


def node2_kernel(
    nb, offs, near, far, acc_in, tiles_hbm, slope_hbm, xhat_hbm, inv_hbm, w1, w2, gain,
    near_out, far_out, gmix_hbm, gpre_hbm, gagg_hbm, acc_hbm, gb, gg,
    halo, before, rim, slope, xhat, inv, gmix, gpre, gagg, acc, send, gcol, insem, outsem, edgesem,
):
    blk = rim.shape[1]
    steps = nb // CH
    get = fetch_rims(near, far, halo.at[pl.ds(0, HALO)], halo.at[pl.ds(HALO, HALO)], insem)
    gets = [
        pltpu.make_async_copy(acc_in, before, insem.at[2]),
        pltpu.make_async_copy(slope_hbm, slope, insem.at[3]),
        pltpu.make_async_copy(xhat_hbm, xhat, insem.at[4]),
        pltpu.make_async_copy(inv_hbm, inv, insem.at[5]),
        *edge_tiles(tiles_hbm, rim, edgesem),
    ]
    start_all(gets)
    gcol[...] = column(gain[...], blk)
    gb[...] = jnp.zeros_like(gb)
    gg[...] = jnp.zeros_like(gg)

    def clear(it, c):
        for s in range(CH):
            acc[it * CH + s] = jnp.zeros(acc.shape[1:], F32)
        return c

    lax.fori_loop(0, acc.shape[0] // CH, clear, 0)
    wait_all([*get, *gets])

    def step(it, c):
        blocks = [it * CH + s for s in range(CH)]
        grad = lanes([before[b] + halo[b].astype(F32) for b in blocks])
        xhat_w = lanes([xhat[b] for b in blocks]).astype(F32)
        slope_w = lanes([slope[b] for b in blocks]).astype(F32)
        inv_w = lanes([inv[b] for b in blocks])
        gg[...] += fold(grad * xhat_w, blk)
        gmix_w, gpre_f, gpre_w, gh, gagg_w = backward_step(
            grad, xhat_w, inv_w, slope_w, w1[...], w2[...], gcol
        )
        gb[...] += fold(gpre_f, blk)
        rest = grad + gh
        for s, b in enumerate(blocks):
            gmix[b] = cut(gmix_w, s, blk)
            gpre[b] = cut(gpre_w, s, blk)
            gagg[b] = cut(gagg_w, s, blk)
            acc[HALO + b] += cut(rest, s, blk)
        push_edge(it, gagg_w, acc, rim, offs, blk)
        return c

    lax.fori_loop(0, steps, step, 0)
    puts = [
        pltpu.make_async_copy(v, v_hbm, outsem.at[2 + i])
        for i, (v, v_hbm) in enumerate(
            [(gmix, gmix_hbm), (gpre, gpre_hbm), (gagg, gagg_hbm), (acc.at[pl.ds(HALO, nb)], acc_hbm)]
        )
    ]
    start_all(puts)
    outgoing(acc, send, nb, near_out, far_out, outsem)
    wait_all(puts)


def weights_kernel(
    nb, with_out, *refs
):
    if with_out:
        (offs, gagg_hbm, acc_in, tiles_hbm, h_hbm, agg_hbm, act_hbm, gmix_hbm, gpre_hbm, gb, gg, h2_hbm,
         acc_hbm, gw, gv, out_hbm,
         gagg, acc, tiles, h, agg, act, gmix, gpre, h2, out, insem, tsem) = refs
    else:
        (offs, gagg_hbm, acc_in, tiles_hbm, h_hbm, agg_hbm, act_hbm, gmix_hbm, gpre_hbm, gb, gg,
         acc_hbm, gw, gv,
         gagg, acc, tiles, h, agg, act, gmix, gpre, insem, tsem) = refs
    blk = tiles.shape[2]
    width = h.shape[1]
    steps = nb // CH
    first = [
        pltpu.make_async_copy(gagg_hbm, gagg, insem.at[0]),
        pltpu.make_async_copy(acc_in, acc, insem.at[1]),
    ]
    then = [
        pltpu.make_async_copy(src, dst, insem.at[2 + i])
        for i, (src, dst) in enumerate(
            [(h_hbm, h), (agg_hbm, agg), (act_hbm, act), (gmix_hbm, gmix), (gpre_hbm, gpre)]
        )
    ]
    start_all(first)
    start_all(load_tiles(tiles_hbm, tiles, tsem, steps))
    start_all(then)
    if with_out:
        get_h2 = pltpu.make_async_copy(h2_hbm, h2, insem.at[7])
        get_h2.start()
    gv[0:1] = jnp.sum(jnp.transpose(gb[...]), axis=0, keepdims=True)
    gv[1:2] = jnp.sum(jnp.transpose(gg[...]), axis=0, keepdims=True)
    gw[...] = jnp.zeros_like(gw)
    wait_all(first)

    def push(it, c):
        pltpu.make_async_copy(
            tiles_hbm.at[pl.ds(it * CH, CH)], tiles.at[pl.ds(it * CH, CH)], tsem.at[it]
        ).wait()
        slot = jnp.where(it * CH < HALO, 2, 1)
        for s in range(CH):
            b = it * CH + s
            both = nn(gagg[b], lanes([tiles[b, 0], tiles[b, slot]]))
            acc[b] += both[:, :blk]
            acc[b + offs[b, slot]] += both[:, blk:]
        return c

    lax.fori_loop(0, steps, push, 0)
    put_a = pltpu.make_async_copy(acc, acc_hbm, insem.at[0])
    put_a.start()
    wait_all(then)

    def outer(it, c):
        blocks = [it * CH + s for s in range(CH)]
        gpre_w = lanes([gpre[b] for b in blocks])
        gw[0:width] += nt(lanes([h[b] for b in blocks]), gpre_w)
        gw[width : 2 * width] += nt(lanes([agg[b] for b in blocks]), gpre_w)
        gw[2 * width :] += nt(lanes([act[b] for b in blocks]), lanes([gmix[b] for b in blocks]))
        return c

    lax.fori_loop(0, steps, outer, 0)
    if with_out:
        get_h2.wait()
        one = eye(blk)

        def turn(it, c):
            for s in range(CH):
                b = it * CH + s
                out[pl.ds(b * blk, blk)] = nt(one, h2[b]).astype(BF16)
            return c

        lax.fori_loop(0, steps, turn, 0)
        put_o = pltpu.make_async_copy(out, out_hbm, insem.at[1])
        put_o.start()
        put_o.wait()
    put_a.wait()


def final_kernel(nb, near, far, acc_in, out_hbm, halo, acc, out, insem, outsem):
    blk = acc.shape[2]
    steps = nb // CH
    get = fetch_rims(near, far, halo.at[pl.ds(0, HALO)], halo.at[pl.ds(HALO, HALO)], insem)
    get_a = pltpu.make_async_copy(acc_in, acc, insem.at[2])
    get_a.start()
    wait_all([*get, get_a])

    def step(it, c):
        for s in range(CH):
            b = it * CH + s
            out[pl.ds(b * blk, blk)] = jnp.transpose(acc[b] + halo[b].astype(F32))
        pltpu.make_async_copy(
            out.at[pl.ds(it * CH * blk, CH * blk)],
            out_hbm.at[pl.ds(it * CH * blk, CH * blk)],
            outsem.at[it],
        ).start()
        return c

    lax.fori_loop(0, steps, step, 0)
    for i in range(steps):
        pltpu.make_async_copy(
            out.at[pl.ds(i * CH * blk, CH * blk)],
            out_hbm.at[pl.ds(i * CH * blk, CH * blk)],
            outsem.at[i],
        ).wait()


def call(body, name, specs, args, outs, out_specs, scratch, flops, moved):
    return pl.pallas_call(
        body,
        name=name,
        in_specs=specs,
        out_specs=out_specs,
        out_shape=[jax.ShapeDtypeStruct(s, t) for s, t in outs],
        scratch_shapes=scratch,
        compiler_params=pltpu.CompilerParams(vmem_limit_bytes=48 << 20),
        cost_estimate=pl.CostEstimate(flops=flops, bytes_accessed=moved, transcendentals=0),
    )(*args)


def dma(*n):
    return pltpu.SemaphoreType.DMA(n)


def per_device(feats, tile_vals, tile_offs, w_in, bias_in, w_out, gain, cot):
    import functools

    nodes, width = feats.shape
    nb, _, blk, _ = tile_vals.shape
    hid = w_out.shape[1]
    assert nb == 2 * HALO and width == blk and hid == width
    devices = lax.axis_size("band") * lax.axis_size("rep")
    steps = nb // CH
    rows = HALO * blk
    block = (width, blk)
    full = (nb, *block)
    rim = (HALO, *block)
    ext = (nb + 2 * HALO, *block)
    v = pltpu.VMEM
    tile_flops = 2 * blk * blk * width
    mlp_flops = 2 * nodes * (2 * width * hid + hid * width)
    mib = 2 * nodes * width

    w1t = jnp.swapaxes(w_in, 1, 2)
    w2t = jnp.swapaxes(w_out, 1, 2)
    odd = parity()
    far = swap(lax.dynamic_slice_in_dim(feats, odd * rows, rows), True)
    near = swap(lax.dynamic_slice_in_dim(feats, (1 - odd) * rows, rows), False)

    h0, part = call(
        functools.partial(inner0_kernel, nb), "inner0",
        [SMEM, ANY, ANY], (tile_offs, feats, tile_vals),
        [(full, BF16), (full, F32)], [ANY, ANY],
        [v((nodes, width), BF16), v(tile_vals.shape, BF16), v(full, BF16), v(full, F32), dma(3), dma(steps)],
        2 * nb * tile_flops, 7 * mib,
    )

    near, far, h1, agg0, act0, slope0, xhat0, inv0 = call(
        functools.partial(node0_kernel, nb), "node0",
        [SMEM, ANY, ANY, ANY, ANY, ANY, VMEM, VMEM, VMEM, VMEM],
        (tile_offs, near, far, h0, part, tile_vals, w1t[0], w2t[0], bias_in[0:1], gain[0:1]),
        [(rim, BF16), (rim, BF16), (full, BF16), (full, BF16), (full, BF16), (full, BF16), (full, BF16), ((nb, 1, blk), F32)],
        [ANY] * 8,
        [v((2 * rows, width), BF16), v(ext, BF16), v(full, F32), v(full, BF16)]
        + [v(full, BF16)] * 5
        + [v((nb, 1, blk), F32), v((hid, blk), F32), v(block, F32), dma(4), dma(8), dma(2)],
        nb * tile_flops + mlp_flops, 11 * mib,
    )

    near, far = swap(near, False), swap(far, True)
    part, cott = call(
        functools.partial(inner1_kernel, nb), "inner1",
        [SMEM, ANY, ANY, ANY], (tile_offs, h1, tile_vals, cot),
        [(full, F32), (full, BF16)], [ANY, ANY],
        [v(full, BF16), v(tile_vals.shape, BF16), v((nodes, width), BF16), v(full, BF16), v(full, F32), dma(4), dma(steps)],
        2 * nb * tile_flops, 8 * mib,
    )

    near, far, h2, agg1, act1, gmix1, gpre1, gagg, acc, gb1, gg1 = call(
        functools.partial(node1_kernel, nb), "node1",
        [SMEM, ANY, ANY, ANY, ANY, ANY, ANY] + [VMEM] * 6,
        (tile_offs, near, far, h1, part, tile_vals, cott, w1t[1], w2t[1], w_in[1], w_out[1], bias_in[1:2], gain[1:2]),
        [(rim, BF16), (rim, BF16)] + [(full, BF16)] * 6 + [(full, F32), (block, F32), (block, F32)],
        [ANY] * 9 + [VMEM] * 2,
        [v(ext, BF16), v(full, F32), v(full, BF16), v(full, BF16)]
        + [v(full, BF16)] * 6
        + [v(ext, F32), v(full, BF16), v(block, F32), v(block, F32), dma(5), dma(9), dma(2)],
        2 * nb * tile_flops + 2 * mlp_flops, 16 * mib,
    )

    near, far = swap(near, False), swap(far, True)
    acc, gw1, gv1, out_feats = call(
        functools.partial(weights_kernel, nb, True), "weights1",
        [SMEM] + [ANY] * 8 + [VMEM, VMEM, ANY],
        (tile_offs, gagg, acc, tile_vals, h1, agg1, act1, gmix1, gpre1, gb1, gg1, h2),
        [(full, F32), ((2 * width + hid, hid), F32), ((2, blk), F32), ((nodes, width), BF16)],
        [ANY, VMEM, VMEM, ANY],
        [v(full, BF16), v(full, F32), v(tile_vals.shape, BF16)]
        + [v(full, BF16)] * 6
        + [v((nodes, width), BF16), dma(8), dma(steps)],
        2 * nb * tile_flops + mlp_flops, 16 * mib,
    )

    near, far, gmix0, gpre0, gagg, acc, gb0, gg0 = call(
        functools.partial(node2_kernel, nb), "node2",
        [SMEM] + [ANY] * 7 + [VMEM] * 3 ,
        (tile_offs, near, far, acc, tile_vals, slope0, xhat0, inv0, w_in[0], w_out[0], gain[0:1]),
        [(rim, BF16), (rim, BF16)] + [(full, BF16)] * 3 + [(full, F32), (block, F32), (block, F32)],
        [ANY] * 6 + [VMEM] * 2,
        [v(full, BF16), v(full, F32), v(full, BF16), v(full, BF16), v(full, BF16), v((nb, 1, blk), F32)]
        + [v(full, BF16)] * 3
        + [v(ext, F32), v(full, BF16), v(block, F32), dma(6), dma(6), dma(2)],
        nb * tile_flops + mlp_flops, 14 * mib,
    )

    near, far = swap(near, False), swap(far, True)
    acc, gw0, gv0 = call(
        functools.partial(weights_kernel, nb, False), "weights0",
        [SMEM] + [ANY] * 8 + [VMEM, VMEM],
        (tile_offs, gagg, acc, tile_vals, h0, agg0, act0, gmix0, gpre0, gb0, gg0),
        [(full, F32), ((2 * width + hid, hid), F32), ((2, blk), F32)],
        [ANY, VMEM, VMEM],
        [v(full, BF16), v(full, F32), v(tile_vals.shape, BF16)] + [v(full, BF16)] * 5 + [dma(7), dma(steps)],
        2 * nb * tile_flops + mlp_flops, 14 * mib,
    )

    scale = 1.0 / math.sqrt(nodes * devices)
    big = jnp.concatenate([gw0, gw1], axis=0).reshape(devices, -1, hid)
    share = big.shape[1]
    small = jnp.concatenate([gv0, gv1, jnp.zeros((4, hid), F32)], axis=0)
    bundle = jnp.concatenate([big, jnp.broadcast_to(small, (devices, 8, hid))], axis=1).astype(BF16)
    parts = lax.all_to_all(bundle, AXES, 0, 0, tiled=True)
    sums = jnp.sum(parts.astype(F32), axis=0) * scale
    mine = jnp.broadcast_to(sums[:share].astype(BF16), (devices, share, hid))
    whole = lax.all_to_all(mine, AXES, 0, 0, tiled=True).astype(F32).reshape(2, -1, hid)
    vectors = sums[share:]

    (grad_feats,) = call(
        functools.partial(final_kernel, nb), "final",
        [ANY] * 3, (near, far, acc), [((nodes, width), F32)], [ANY],
        [v(full, BF16), v(full, F32), v((nodes, width), F32), dma(3), dma(steps)],
        nodes * width, 5 * mib,
    )
    return (
        out_feats,
        grad_feats,
        whole[:, : 2 * width],
        jnp.stack([vectors[0], vectors[2]]),
        whole[:, 2 * width :],
        jnp.stack([vectors[1], vectors[3]]),
    )


def solution(mesh):
    placed = (
        P(AXES, None),
        P(AXES, None, None, None),
        P(AXES, None),
        P(),
        P(),
        P(),
        P(),
        P(AXES, None),
    )
    return jax.shard_map(
        per_device,
        mesh=mesh,
        in_specs=placed,
        out_specs=(P(AXES, None), P(AXES, None), P(), P(), P(), P()),
        check_vma=False,
    )
```

time: 389 us -> 129 us (0.33)
  waiting for transfers between devices: 115 us -> 23.9 us
  other arithmetic: 77.2 us -> 2.07 us
  local copies, waits for them, and re-layouts: 83.5 us -> 13.6 us
  Pallas kernels: 0 us -> 66.2 us
  matrix products: 42.9 us -> 0 us
  blocking collectives: 39.8 us -> 0 us
  between operations: 14.5 us -> 1 us
  starting transfers between devices: 13 us -> 21.6 us
    psum x1 -> x0, waiting for transfers between devices: 93.6 us -> none  [per_device(): lax.psum((jnp.stack(win_list), jnp.stack(bias_list), jnp.stack(wout_list)...]
    pallas_call x0 -> x8, Pallas kernels: none -> 66.2 us  [call(): pl.pallas_call(body, name=name, in_specs=specs, out_specs=out_specs, out_...]
    scatter-add x6 -> x0, other arithmetic: 54.5 us -> none  [the longest x2 40.3 us: per_device(): extended.at[flat_columns].add(contrib.reshape(-1, tile_width, feat_width))]
    dot_general x20 -> x0, matrix products: 42.9 us -> none  [the longest x2 8.61 us: per_device(): jnp.einsum('bkij,bid->bkjd', tile_vals, grad_blocks, preferred_element_ty...]
    psum x1 -> x0, blocking collectives: 39.8 us -> none  [per_device(): lax.psum((jnp.stack(win_list), jnp.stack(bias_list), jnp.stack(wout_list)...]
    slice x12 -> x5, local copies, waits for them, and re-layouts: 22.7 us -> 1.4 us  [the longest x1 0.72 us: per_device(): whole[:, :2 * width]]
    reshape x5 -> x0, local copies, waits for them, and re-layouts: 19.7 us -> none  [the longest x2 13.2 us: per_device(): contrib.reshape(-1, tile_width, feat_width)]
    all_to_all x0 -> x2, waiting for transfers between devices: none -> 15.2 us  [the longest x1 9.3 us: per_device(): parts = lax.all_to_all(bundle, AXES, 0, 0, tiled=True)]
  transfers between devices with their start and end apart: 13 -> 10, of which waited for: 5 -> 4; matrix products, arithmetic and copies ran while one was open for 36% -> 2% of each run, Pallas kernels for 0% -> 18%
where the time goes in v1:
time: 129 us; the launch traced here: 128 us
  Pallas kernels  66.2 us (51%)
  waiting for transfers between devices  23.9 us (19%)
  starting transfers between devices  21.6 us (17%)
  local copies, waits for them, and re-layouts  13.6 us (11%)
  other arithmetic  2.07 us (2%)
    pallas_call x8, Pallas kernels, call(): pl.pallas_call(body, name=name, in_specs=specs, out_specs=out_specs, out_...  66.2 us
    unnamed x45, local copies, waits for them, and re-layouts  9.98 us
    all_to_all x1, waiting for transfers between devices, per_device(): parts = lax.all_to_all(bundle, AXES, 0, 0, tiled=True)  9.3 us
    ppermute x8, waiting for transfers between devices, swap(): return lax.ppermute(x, AXES, pairs)  8.73 us
    ppermute x8, starting transfers between devices, swap(): return lax.ppermute(x, AXES, pairs)  8.23 us
    all_to_all x1, starting transfers between devices, per_device(): lax.all_to_all(mine, AXES, 0, 0, tiled=True).astype(F32).reshape(2, -1, hid)  6.73 us
    all_to_all x1, starting transfers between devices, per_device(): parts = lax.all_to_all(bundle, AXES, 0, 0, tiled=True)  6.65 us
    all_to_all x1, waiting for transfers between devices, per_device(): lax.all_to_all(mine, AXES, 0, 0, tiled=True).astype(F32).reshape(2, -1, hid)  5.89 us
  transfers between devices with their start and end apart: 10, of which 4 were waited for; matrix products, arithmetic and copies ran while one was open for 2% of the time, Pallas kernels for 18%

profile of v1, /device:TPU:1, one launch (start us, length us, event | category | flops | bytes accessed | tf_op | source)
XLA Modules:
  0.0 128.4 jit_solution(12750289034878271140)
XLA Ops:
  0.7 1.4 %constant_dynamic-slice_fusion = (bf16[2048,128]{1,0:T(8,128)(2,1)S(1)}, bf16[2048,128]{1,0:T(8,128)(2,1)S(1)}) fusion(bf16[4096,128]{1,0:T(8,128)(2,1)} %x_hbm.1, s32[]{:T(128)S(6)} %select_n.7, s32[]{:T(128)S(6)} %select_n.6), kind=kLoop, calls=%fused_computation.17 | loop fusion | bytes 2097160 | tf_op jit(solution)/shard_map/dynamic_slice | solution.py:609
  2.2 2.7 %collective-permute-start.1 = (bf16[2048,128]{1,0:T(8,128)(2,1)S(1)}, bf16[2048,128]{1,0:T(8,128)(2,1)S(1)}, u32[]{:S(2)}, u32[]{:S(2)}) collective-permute-start(bf16[2048,128]{1,0:T(8,128)(2,1)S(1)} %get-tuple-element.82), channel_id=1, source_target_pairs={{1,2},{2,1},{3,4},{4,3},{5,6},{6,5},{7,8},{8,7},{9,10},{10,9},{11,... | collective-permute-start | bytes 1572872 | tf_op jit(solution)/shard_map/ppermute | solution.py:72
  5.1 0.7 copy.16
  5.8 4.8 %inner0.1 = (bf16[32,128,128]{2,1,0:T(8,128)(2,1)S(1)}, f32[32,128,128]{2,1,0:T(8,128)S(1)}) custom-call(s32[32,3]{1,0:T(8,128)S(1)} %copy.20.offs.refs_0_, bf16[4096,128]{1,0:T(8,128)(2,1)S(1)} %copy-done.4, bf16[32,3,128,128]{3,2,1,0:T(8,128)(2,1)} %refs_3_.3), custom_call_target="tpu_custom_call" | custom-call | flops 268435456 | bytes 7340032 | tf_op jit(solution)/shard_map/inner0/pallas_call | solution.py:571
  10.6 1.0 copy-done.2
  11.6 1.3 %copy-done.7 = f32[32,128,128]{2,1,0:T(8,128)} copy-done((f32[32,128,128]{2,1,0:T(8,128)}, f32[32,128,128]{2,1,0:T(8,128)S(1)}, u32[]{:S(2)}) %copy-start.7) | copy-done | bytes 2097176
  13.0 4.4 %collective-permute-done.1.far = bf16[2048,128]{1,0:T(8,128)(2,1)S(1)} collective-permute-done((bf16[2048,128]{1,0:T(8,128)(2,1)S(1)}, bf16[2048,128]{1,0:T(8,128)(2,1)S(1)}, u32[]{:S(2)}, u32[]{:S(2)}) %collective-permute-start.1) | collective-permute-done | bytes 524320 | tf_op jit(solution)/shard_map/ppermute | solution.py:72
  17.3 9.7 %node0.1 = (bf16[16,128,128]{2,1,0:T(8,128)(2,1)S(1)}, bf16[16,128,128]{2,1,0:T(8,128)(2,1)S(1)}, bf16[32,128,128]{2,1,0:T(8,128)(2,1)S(1)}, bf16[32,128,128]{2,...) custom-call(s32[32,3]{1,0:T(8,128)S(1)} %copy.20.offs.refs_0_, ...), custom_call_target="tpu_custom_call" | custom-call | flops 536870912 | bytes 11534336 | tf_op jit(solution)/shard_map/node0/pallas_call | solution.py:571
  27.2 1.7 %collective-permute-start.3 = (bf16[16,128,128]{2,1,0:T(8,128)(2,1)S(1)}, bf16[16,128,128]{2,1,0:T(8,128)(2,1)S(1)}, u32[]{:S(2)}, u32[]{:S(2)}) collective-permute-start(bf16[16,128,128]{2,1,0:T(8,128)(2,1)S(1)} %get-tuple-element.47), channel_id=1, source_target_pairs={{1,2},{2,1},{3,4},{4,3},{5,6},{6,5},{7,8},{8,7},{9,10},{10,9},{11,... | collective-permute-start | bytes 1572872 | tf_op jit(solution)/shard_map/ppermute | solution.py:72
  29.0 5.8 %inner1.1 = (f32[32,128,128]{2,1,0:T(8,128)S(1)}, bf16[32,128,128]{2,1,0:T(8,128)(2,1)S(1)}) custom-call(s32[32,3]{1,0:T(8,128)S(1)} %copy.20.offs.refs_0_, bf16[32,128,128]{2,1,0:T(8,128)(2,1)S(1)} %get-tuple-element.48.h_hbm.refs_4_, bf16[32,3,128,128]{3,2,1,0:T(8,128)(2,1)} %refs_3_.3, bf16[4096,128]{1,0:T(8,128)(2,1)S(1)} %copy-done.8), custom_call_target="tpu_custom_call" | custom-call | flops 268435456 | bytes 8388608 | tf_op jit(solution)/shard_map/inner1/pallas_call | solution.py:571
  34.8 1.3 %copy-done.5 = f32[32,128,128]{2,1,0:T(8,128)} copy-done((f32[32,128,128]{2,1,0:T(8,128)}, f32[32,128,128]{2,1,0:T(8,128)S(1)}, u32[]{:S(2)}) %copy-start.5) | copy-done | bytes 2097176
  36.1 1.0 copy-done.12
  37.1 4.3 %collective-permute-done.3.far = bf16[16,128,128]{2,1,0:T(8,128)(2,1)S(1)} collective-permute-done((bf16[16,128,128]{2,1,0:T(8,128)(2,1)S(1)}, bf16[16,128,128]{2,1,0:T(8,128)(2,1)S(1)}, u32[]{:S(2)}, u32[]{:S(2)}) %collective-permute-start.3) | collective-permute-done | bytes 524320 | tf_op jit(solution)/shard_map/ppermute | solution.py:72
  41.4 15.5 %node1.1 = (bf16[16,128,128]{2,1,0:T(8,128)(2,1)S(1)}, bf16[16,128,128]{2,1,0:T(8,128)(2,1)S(1)}, bf16[32,128,128]{2,1,0:T(8,128)(2,1)S(1)}, bf16[32,128,128]{2,...) custom-call(s32[32,3]{1,0:T(8,128)S(1)} %copy.20.offs.refs_0_, ...), custom_call_target="tpu_custom_call" | custom-call | flops 1073741824 | bytes 16777216 | tf_op jit(solution)/shard_map/node1/pallas_call | solution.py:571
  57.0 1.0 copy-done.9
  58.0 1.7 %collective-permute-start.5 = (bf16[16,128,128]{2,1,0:T(8,128)(2,1)S(1)}, bf16[16,128,128]{2,1,0:T(8,128)(2,1)S(1)}, u32[]{:S(2)}, u32[]{:S(2)}) collective-permute-start(bf16[16,128,128]{2,1,0:T(8,128)(2,1)S(1)} %get-tuple-element.62), channel_id=1, source_target_pairs={{1,2},{2,1},{3,4},{4,3},{5,6},{6,5},{7,8},{8,7},{9,10},{10,9},{11,... | collective-permute-start | bytes 1572872 | tf_op jit(solution)/shard_map/ppermute | solution.py:72
  59.8 1.2 copy-done.10
  61.0 1.2 copy-done.11
  62.2 10.2 %weights1.1 = (f32[32,128,128]{2,1,0:T(8,128)}, f32[384,128]{1,0:T(8,128)S(1)}, f32[2,128]{1,0:T(2,128)S(1)}, bf16[4096,128]{1,0:T(8,128)(2,1)}) custom-call(s32[32,3]{1,0:T(8,128)S(1)} %copy.20.offs.refs_0_, bf16[32,128,128]{2,1,0:T(8,128)(2,1)S(1)} %copy-done.11, f32[32,128,128]{2,1,0:T(8,128)} %get-tuple-element.52.refs_2_, ...), custom_call_target="tpu_custom_call" | custom-call | flops 671088640 | bytes 16777216 | tf_op jit(solution)/shard_map/weights1/pallas_call | solution.py:571
  72.5 10.5 %node2.1 = (bf16[16,128,128]{2,1,0:T(8,128)(2,1)}, bf16[16,128,128]{2,1,0:T(8,128)(2,1)S(1)}, bf16[32,128,128]{2,1,0:T(8,128)(2,1)S(1)}, bf16[32,128,128]{2,1,0:...) custom-call(s32[32,3]{1,0:T(8,128)S(1)} %copy.20.offs.refs_0_, ...), custom_call_target="tpu_custom_call" | custom-call | flops 536870912 | bytes 14680064 | tf_op jit(solution)/shard_map/node2/pallas_call | solution.py:571
  83.0 1.0 copy-done.13
  84.0 7.5 %weights0.1 = (f32[32,128,128]{2,1,0:T(8,128)}, f32[384,128]{1,0:T(8,128)S(1)}, f32[2,128]{1,0:T(2,128)S(1)}) custom-call(s32[32,3]{1,0:T(8,128)S(1)} %copy.20.offs.refs_0_, bf16[32,128,128]{2,1,0:T(8,128)(2,1)S(1)} %get-tuple-element.69.refs_1_, f32[32,128,128]{2,1,0:T(8,128)} %get-tuple-element.70.refs_2_, bf16[32,3,128,128]{3,2,1,0:T(8,128)(2,1)} %refs_3_.3, ...), custom_call_target="tpu_custom_call" | custom-call | flops 671088640 | bytes 14680064 | tf_op jit(solution)/shard_map/weights0/pallas_call | solution.py:571
  91.7 0.7 pad_maximum_fusion
  92.4 6.7 %all-to-all-start = ((bf16[32,32,128]{2,1,0:T(8,128)(2,1)}), bf16[32,32,128]{2,1,0:T(8,128)(2,1)S(1)}, u32[]{:S(2)}, u32[]{:S(2)}) async-start(bf16[32,32,128]{2,1,0:T(8,128)(2,1)} %pad_maximum_fusion), calls=%async_computation | async-start | bytes 524288 | tf_op jit(solution)/shard_map/all_to_all | solution.py:694
  99.5 1.4 %collective-permute-start.7 = (bf16[16,128,128]{2,1,0:T(8,128)(2,1)}, bf16[16,128,128]{2,1,0:T(8,128)(2,1)S(1)}, u32[]{:S(2)}, u32[]{:S(2)}) collective-permute-start(bf16[16,128,128]{2,1,0:T(8,128)(2,1)} %copy-done.14), channel_id=1, source_target_pairs={{1,2},{2,1},{3,4},{4,3},{5,6},{6,5},{7,8},{8,7},{9,10},{10,9},{11,... | collective-permute-start | bytes 1572872 | tf_op jit(solution)/shard_map/ppermute | solution.py:72
  100.9 9.3 %all-to-all-done = bf16[32,32,128]{2,1,0:T(8,128)(2,1)S(1)} async-done(((bf16[32,32,128]{2,1,0:T(8,128)(2,1)}), bf16[32,32,128]{2,1,0:T(8,128)(2,1)S(1)}, u32[]{:S(2)}, u32[]{:S(2)}) %all-to-all-start) | async-done | bytes 262176 | tf_op jit(solution)/shard_map/all_to_all | solution.py:694
  110.3 0.7 broadcast_in_dim.11
  111.0 6.7 %all-to-all-start.1 = ((bf16[32,24,128]{2,1,0:T(8,128)(2,1)}), bf16[32,24,128]{2,1,0:T(8,128)(2,1)S(1)}, u32[]{:S(2)}, u32[]{:S(2)}) async-start(bf16[32,24,128]{2,1,0:T(8,128)(2,1)} %broadcast_in_dim.11), calls=%async_computation.1 | async-start | bytes 393216 | tf_op jit(solution)/shard_map/all_to_all | solution.py:697
  118.9 2.1 %final.1 = f32[4096,128]{1,0:T(8,128)} custom-call(bf16[16,128,128]{2,1,0:T(8,128)(2,1)S(1)} %collective-permute-done.6.near, bf16[16,128,128]{2,1,0:T(8,128)(2,1)S(1)} %collective-permute-done.7.far, f32[32,128,128]{2,1,0:T(8,128)S(1)} %copy-done.6), custom_call_target="tpu_custom_call" | custom-call | flops 524288 | bytes 5242880 | tf_op jit(solution)/shard_map/final/pallas_call | solution.py:571
  121.0 5.9 %all-to-all-done.1 = bf16[32,24,128]{2,1,0:T(8,128)(2,1)S(1)} async-done(((bf16[32,24,128]{2,1,0:T(8,128)(2,1)}), bf16[32,24,128]{2,1,0:T(8,128)(2,1)S(1)}, u32[]{:S(2)}, u32[]{:S(2)}) %all-to-all-start.1) | async-done | bytes 196640 | tf_op jit(solution)/shard_map/all_to_all | solution.py:697
  127.0 0.7 slice.88
  127.7 0.7 slice.91
  (65 shorter events, 2.5 us)
Async XLA Ops:
  0.6 5.2 %copy-start.4 = (bf16[4096,128]{1,0:T(8,128)(2,1)S(1)}, bf16[4096,128]{1,0:T(8,128)(2,1)}, u32[]{:S(2)}) copy-start(bf16[4096,128]{1,0:T(8,128)(2,1)} %x_hbm.1) | copy-start | bytes 3145732
  0.6 4.2 %copy-start.20 = (f32[2,128]{1,0:T(2,128)S(1)}, f32[2,128]{1,0:T(2,128)}, u32[]{:S(2)}) copy-start(f32[2,128]{1,0:T(2,128)} %param.12) | copy-start | bytes 3076
  0.7 4.2 %copy-start.19 = (f32[2,128]{1,0:T(2,128)S(1)}, f32[2,128]{1,0:T(2,128)}, u32[]{:S(2)}) copy-start(f32[2,128]{1,0:T(2,128)} %param.14) | copy-start | bytes 3076
  0.7 4.2 %copy-start.18 = (s32[32,3]{0,1:T(4,128)S(1)}, s32[32,3]{0,1:T(4,128)}, u32[]{:S(2)}) copy-start(s32[32,3]{0,1:T(4,128)} %param.10) | copy-start | bytes 1156
  0.7 4.3 %copy-start.15 = (bf16[2,256,128]{2,1,0:T(8,128)(2,1)S(1)}, bf16[2,256,128]{2,1,0:T(8,128)(2,1)}, u32[]{:S(2)}) copy-start(bf16[2,256,128]{2,1,0:T(8,128)(2,1)} %param.11) | copy-start | bytes 393220
  0.7 4.4 %copy-start.16 = (bf16[2,128,128]{2,1,0:T(8,128)(2,1)S(1)}, bf16[2,128,128]{2,1,0:T(8,128)(2,1)}, u32[]{:S(2)}) copy-start(bf16[2,128,128]{2,1,0:T(8,128)(2,1)} %param.13) | copy-start | bytes 196612
  2.1 10.9 %collective-permute-start = (bf16[2048,128]{1,0:T(8,128)(2,1)S(1)}, bf16[2048,128]{1,0:T(8,128)(2,1)S(1)}, u32[]{:S(2)}, u32[]{:S(2)}) collective-permute-start(bf16[2048,128]{1,0:T(8,128)(2,1)S(1)} %get-tuple-element.83), channel_id=1, source_target_pairs={{0,1},{1,0},{2,3},{3,2},{4,5},{5,4},{6,7},{7,6},{8,9},{9,8},{10,11... | collective-permute-start | bytes 1572872 | tf_op jit(solution)/shard_map/ppermute | solution.py:72
  2.2 15.2 %collective-permute-start.1 = (bf16[2048,128]{1,0:T(8,128)(2,1)S(1)}, bf16[2048,128]{1,0:T(8,128)(2,1)S(1)}, u32[]{:S(2)}, u32[]{:S(2)}) collective-permute-start(bf16[2048,128]{1,0:T(8,128)(2,1)S(1)} %get-tuple-element.82), channel_id=1, source_target_pairs={{1,2},{2,1},{3,4},{4,3},{5,6},{6,5},{7,8},{8,7},{9,10},{10,9},{11,... | collective-permute-start | bytes 1572872 | tf_op jit(solution)/shard_map/ppermute | solution.py:72
  5.8 7.1 %copy-start.17 = (bf16[2,128,128]{1,2,0:T(8,128)(2,1)S(1)}, bf16[2,128,128]{1,2,0:T(8,128)(2,1)}, u32[]{:S(2)}) copy-start(bf16[2,128,128]{1,2,0:T(8,128)(2,1)} %copy.16) | copy-start | bytes 196612
  10.6 1.0 copy-start.2
  11.6 1.3 %copy-start.7 = (f32[32,128,128]{2,1,0:T(8,128)}, f32[32,128,128]{2,1,0:T(8,128)S(1)}, u32[]{:S(2)}) copy-start(f32[32,128,128]{2,1,0:T(8,128)S(1)} %get-tuple-element.45.part_hbm) | copy-start | bytes 6291460
  17.3 11.6 %copy-start.8 = (bf16[4096,128]{1,0:T(8,128)(2,1)S(1)}, bf16[4096,128]{1,0:T(8,128)(2,1)}, u32[]{:S(2)}) copy-start(bf16[4096,128]{1,0:T(8,128)(2,1)} %cot_hbm.1) | copy-start | bytes 3145732
  27.1 7.7 %copy-start = (bf16[32,128,128]{2,1,0:T(8,128)(2,1)}, bf16[32,128,128]{2,1,0:T(8,128)(2,1)S(1)}, u32[]{:S(2)}) copy-start(bf16[32,128,128]{2,1,0:T(8,128)(2,1)S(1)} %get-tuple-element.48.h_hbm.refs_4_) | copy-start | bytes 3145732
  27.1 10.0 %collective-permute-start.2 = (bf16[16,128,128]{2,1,0:T(8,128)(2,1)S(1)}, bf16[16,128,128]{2,1,0:T(8,128)(2,1)S(1)}, u32[]{:S(2)}, u32[]{:S(2)}) collective-permute-start(bf16[16,128,128]{2,1,0:T(8,128)(2,1)S(1)} %get-tuple-element.46), channel_id=1, source_target_pairs={{0,1},{1,0},{2,3},{3,2},{4,5},{5,4},{6,7},{7,6},{8,9},{9,8},{10,11... | collective-permute-start | bytes 1572872 | tf_op jit(solution)/shard_map/ppermute | solution.py:72
  27.2 14.2 %collective-permute-start.3 = (bf16[16,128,128]{2,1,0:T(8,128)(2,1)S(1)}, bf16[16,128,128]{2,1,0:T(8,128)(2,1)S(1)}, u32[]{:S(2)}, u32[]{:S(2)}) collective-permute-start(bf16[16,128,128]{2,1,0:T(8,128)(2,1)S(1)} %get-tuple-element.47), channel_id=1, source_target_pairs={{1,2},{2,1},{3,4},{4,3},{5,6},{6,5},{7,8},{8,7},{9,10},{10,9},{11,... | collective-permute-start | bytes 1572872 | tf_op jit(solution)/shard_map/ppermute | solution.py:72
  34.8 1.3 %copy-start.5 = (f32[32,128,128]{2,1,0:T(8,128)}, f32[32,128,128]{2,1,0:T(8,128)S(1)}, u32[]{:S(2)}) copy-start(f32[32,128,128]{2,1,0:T(8,128)S(1)} %get-tuple-element.49.part_hbm) | copy-start | bytes 6291460
  36.1 1.0 copy-start.12
  41.4 18.3 %copy-start.1 = (bf16[32,128,128]{2,1,0:T(8,128)(2,1)S(1)}, bf16[32,128,128]{2,1,0:T(8,128)(2,1)}, u32[]{:S(2)}) copy-start(bf16[32,128,128]{2,1,0:T(8,128)(2,1)} %copy-done) | copy-start | bytes 3145732
  57.0 1.0 copy-start.9
  57.9 14.5 %collective-permute-start.4 = (bf16[16,128,128]{2,1,0:T(8,128)(2,1)S(1)}, bf16[16,128,128]{2,1,0:T(8,128)(2,1)S(1)}, u32[]{:S(2)}, u32[]{:S(2)}) collective-permute-start(bf16[16,128,128]{2,1,0:T(8,128)(2,1)S(1)} %get-tuple-element.61), channel_id=1, source_target_pairs={{0,1},{1,0},{2,3},{3,2},{4,5},{5,4},{6,7},{7,6},{8,9},{9,8},{10,11... | collective-permute-start | bytes 1572872 | tf_op jit(solution)/shard_map/ppermute | solution.py:72
  58.0 14.5 %collective-permute-start.5 = (bf16[16,128,128]{2,1,0:T(8,128)(2,1)S(1)}, bf16[16,128,128]{2,1,0:T(8,128)(2,1)S(1)}, u32[]{:S(2)}, u32[]{:S(2)}) collective-permute-start(bf16[16,128,128]{2,1,0:T(8,128)(2,1)S(1)} %get-tuple-element.62), channel_id=1, source_target_pairs={{1,2},{2,1},{3,4},{4,3},{5,6},{6,5},{7,8},{8,7},{9,10},{10,9},{11,... | collective-permute-start | bytes 1572872 | tf_op jit(solution)/shard_map/ppermute | solution.py:72
  59.8 1.2 copy-start.10
  61.0 1.2 copy-start.11
  72.5 11.5 %copy-start.3 = (bf16[32,128,128]{2,1,0:T(8,128)(2,1)S(1)}, bf16[32,128,128]{2,1,0:T(8,128)(2,1)}, u32[]{:S(2)}) copy-start(bf16[32,128,128]{2,1,0:T(8,128)(2,1)} %copy-done.2) | copy-start | bytes 3145732
  83.0 1.0 copy-start.13
  84.0 7.6 %copy-start.14 = (bf16[16,128,128]{2,1,0:T(8,128)(2,1)}, bf16[16,128,128]{2,1,0:T(8,128)(2,1)S(1)}, u32[]{:S(2)}) copy-start(bf16[16,128,128]{2,1,0:T(8,128)(2,1)S(1)} %get-tuple-element.68) | copy-start | bytes 1572868
  91.5 27.4 %copy-start.6 = (f32[32,128,128]{2,1,0:T(8,128)S(1)}, f32[32,128,128]{2,1,0:T(8,128)}, u32[]{:S(2)}) copy-start(f32[32,128,128]{2,1,0:T(8,128)} %get-tuple-element.77.acc_in) | copy-start | bytes 6291460
  92.4 17.8 %all-to-all-start = ((bf16[32,32,128]{2,1,0:T(8,128)(2,1)}), bf16[32,32,128]{2,1,0:T(8,128)(2,1)S(1)}, u32[]{:S(2)}, u32[]{:S(2)}) async-start(bf16[32,32,128]{2,1,0:T(8,128)(2,1)} %pad_maximum_fusion), calls=%async_computation | async-start | bytes 524288 | tf_op jit(solution)/shard_map/all_to_all | solution.py:694
  99.1 19.8 %collective-permute-start.6 = (bf16[16,128,128]{2,1,0:T(8,128)(2,1)}, bf16[16,128,128]{2,1,0:T(8,128)(2,1)S(1)}, u32[]{:S(2)}, u32[]{:S(2)}) collective-permute-start(bf16[16,128,128]{2,1,0:T(8,128)(2,1)} %get-tuple-element.67), channel_id=1, source_target_pairs={{0,1},{1,0},{2,3},{3,2},{4,5},{5,4},{6,7},{7,6},{8,9},{9,8},{10,11... | collective-permute-start | bytes 1572872 | tf_op jit(solution)/shard_map/ppermute | solution.py:72
  99.5 19.4 %collective-permute-start.7 = (bf16[16,128,128]{2,1,0:T(8,128)(2,1)}, bf16[16,128,128]{2,1,0:T(8,128)(2,1)S(1)}, u32[]{:S(2)}, u32[]{:S(2)}) collective-permute-start(bf16[16,128,128]{2,1,0:T(8,128)(2,1)} %copy-done.14), channel_id=1, source_target_pairs={{1,2},{2,1},{3,4},{4,3},{5,6},{6,5},{7,8},{8,7},{9,10},{10,9},{11,... | collective-permute-start | bytes 1572872 | tf_op jit(solution)/shard_map/ppermute | solution.py:72
  111.0 15.9 %all-to-all-start.1 = ((bf16[32,24,128]{2,1,0:T(8,128)(2,1)}), bf16[32,24,128]{2,1,0:T(8,128)(2,1)S(1)}, u32[]{:S(2)}, u32[]{:S(2)}) async-start(bf16[32,24,128]{2,1,0:T(8,128)(2,1)} %broadcast_in_dim.11), calls=%async_computation.1 | async-start | bytes 393216 | tf_op jit(solution)/shard_map/all_to_all | solution.py:697

commit v2 on v0

v2 whole, which is shorter than its diff:
```python
import functools
import math

import jax
import jax.numpy as jnp
from jax import lax
from jax.experimental import pallas as pl
from jax.experimental.pallas import tpu as pltpu
from jax.sharding import PartitionSpec as P

HALO = 16
EPS = 1e-05
AXES = ("band", "rep")
F32 = jnp.float32
BF16 = jnp.bfloat16
CH = 8
HBM = pl.BlockSpec(memory_space=pltpu.HBM)
ANY = pl.BlockSpec(memory_space=pl.ANY)
SMEM = pl.BlockSpec(memory_space=pltpu.SMEM)
VMEM = pl.BlockSpec(memory_space=pltpu.VMEM)


def nt(a, b):
    return lax.dot_general(a, b, (((1,), (1,)), ((), ())), preferred_element_type=F32)


def nn(a, b):
    return jnp.dot(a, b, preferred_element_type=F32)


def eye(n):
    rows = lax.broadcasted_iota(jnp.int32, (n, n), 0)
    cols = lax.broadcasted_iota(jnp.int32, (n, n), 1)
    return (rows == cols).astype(BF16)


def column(row, width):
    return jnp.transpose(jnp.broadcast_to(row, (width, row.shape[1])))


def lanes(parts):
    return jnp.concatenate(parts, axis=1)


def widen(block, times):
    return lanes([block] * times)


def parity():
    place = lax.axis_index("band") * lax.axis_size("rep") + lax.axis_index("rep")
    return lax.rem(place, 2)


def swap(x, far):
    n = lax.axis_size("band") * lax.axis_size("rep")
    pairs = []
    for c in range(n // 2):
        a, b = (2 * c, 2 * c + 1) if not far else (2 * c + 1, (2 * c + 2) % n)
        pairs += [(a, b), (b, a)]
    return lax.ppermute(x, AXES, pairs)


def by_side(near, far, move):
    even = parity() == 0

    @pl.when(even)
    def _():
        move(far, near)

    @pl.when(jnp.logical_not(even))
    def _():
        move(near, far)


def for_blocks(count, body, per=4):
    def step(it, c):
        for s in range(per):
            body(it * per + s)
        return c

    lax.fori_loop(0, count // per, step, 0)


def turn_kernel(nb, x_hbm, ext, near, far, x, sem):
    blk = ext.shape[2]
    one = eye(blk)
    parts = sem.shape[0]
    per = nb // parts

    def copy(i):
        rows = pl.ds(i * per * blk, per * blk)
        return pltpu.make_async_copy(x_hbm.at[rows], x.at[rows], sem.at[i])

    for i in range(parts):
        copy(i).start()

    def step(i, c):
        copy(i).wait()
        for s in range(per):
            b = i * per + s
            ext[HALO + b] = nt(one, x[pl.ds(b * blk, blk)]).astype(BF16)
        return c

    lax.fori_loop(0, parts, step, 0)
    give_rims(ext, HALO, nb, near, far)


def give_rims(buf, first, nb, near, far):
    def move(low, high):
        def one(b):
            low[b] = buf[first + b].astype(BF16)
            high[b] = buf[first + nb - HALO + b].astype(BF16)

        for_blocks(HALO, one)

    by_side(near, far, move)


def give_sums(acc, nb, near, far):
    def move(low, high):
        def one(b):
            low[b] = acc[b].astype(BF16)
            high[b] = acc[HALO + nb + b].astype(BF16)

        for_blocks(HALO, one)

    by_side(near, far, move)


def send_rims(rims, near_hbm, far_hbm, sem):
    low, high = rims.at[pl.ds(0, HALO)], rims.at[pl.ds(HALO, HALO)]

    def move(to_low, to_high):
        pltpu.make_async_copy(low, to_low, sem.at[0]).start()
        pltpu.make_async_copy(high, to_high, sem.at[1]).start()

    by_side(near_hbm, far_hbm, move)
    return [
        pltpu.make_async_copy(low, far_hbm, sem.at[0]),
        pltpu.make_async_copy(high, near_hbm, sem.at[1]),
    ]


def fetch_rims(near_hbm, far_hbm, rims, sem):
    low, high = rims.at[pl.ds(0, HALO)], rims.at[pl.ds(HALO, HALO)]

    def move(from_low, from_high):
        pltpu.make_async_copy(from_low, low, sem.at[0]).start()
        pltpu.make_async_copy(from_high, high, sem.at[1]).start()

    by_side(near_hbm, far_hbm, move)
    return [
        pltpu.make_async_copy(far_hbm, low, sem.at[0]),
        pltpu.make_async_copy(near_hbm, high, sem.at[1]),
    ]


def take_rims(near, far, buf, low_at, high_at):
    def move(low, high):
        def one(b):
            buf[low_at + b] = low[b]
            buf[high_at + b] = high[b]

        for_blocks(HALO, one)

    by_side(near, far, move)


def inner_tiles(nb, ext, tiles, offs, part):
    def one(b):
        slot = jnp.where(b < HALO, 2, 1)
        left = lanes([ext[HALO + b], ext[HALO + b + offs[slot, b]]])
        part[b] = nt(left, lanes([tiles[b, 0], tiles[b, slot]]))

    for_blocks(nb, one)


def inner0_kernel(nb, offs, ext, tiles, w_in, w_out, part, w1t, w2t, w2, kept, sem):
    keep = pltpu.make_async_copy(ext.at[pl.ds(HALO, nb)], kept, sem.at[0])
    keep.start()
    inner_tiles(nb, ext, tiles, offs, part)
    one = eye(tiles.shape[2])
    for layer in range(w_in.shape[0]):
        w1t[layer] = (0.5 * nt(one, w_in[layer])).astype(BF16)
        w2t[layer] = nt(one, w_out[layer]).astype(BF16)
        w2[layer] = (0.5 * w_out[layer].astype(F32)).astype(BF16)
    keep.wait()


def inner1_kernel(nb, offs, ext, tiles, cot, part, cott):
    inner_tiles(nb, ext, tiles, offs, part)
    blk = tiles.shape[2]
    one = eye(blk)

    def turn(b):
        cott[b] = nt(one, cot[pl.ds(b * blk, blk)]).astype(BF16)

    for_blocks(nb, turn)


def edge_slot(b):
    return jnp.where(b < HALO, 1, 2)


def forward_step(it, ext, part, tiles, offs, w1t, w2t, bias, gain):
    agg = []
    for s in range(CH):
        b = it * CH + s
        slot = edge_slot(b)
        agg.append((part[b] + nt(ext[HALO + b + offs[slot, b]], tiles[b, slot])).astype(BF16))
    agg = lanes(agg)
    feats = lanes([ext[HALO + it * CH + s] for s in range(CH)])
    joined = jnp.concatenate([feats, agg], axis=0)
    half = nn(w1t, joined) + widen(bias[...], CH)
    t = jnp.tanh(half)
    up = 1.0 + t
    act = (half * up).astype(BF16)
    slope = up * (1.0 + half * (1.0 - t))
    mix = nn(w2t, act)
    centred = mix - jnp.mean(mix, axis=0, keepdims=True)
    inv = lax.rsqrt(jnp.mean(centred * centred, axis=0, keepdims=True) + EPS)
    xhat = centred * inv
    after = (feats.astype(F32) + xhat * widen(gain[...], CH)).astype(BF16)
    return agg, act, slope, xhat, inv, after


def backward_step(grad, xhat, inv, slope, w1, w2, gain):
    wide = widen(gain[...], CH)
    prod = grad * xhat
    gx = grad * wide
    gmix = inv * (
        gx - jnp.mean(gx, axis=0, keepdims=True) - xhat * jnp.mean(prod * wide, axis=0, keepdims=True)
    )
    gmix = gmix.astype(BF16)
    gpre = nn(w2, gmix) * slope
    gpre_b = gpre.astype(BF16)
    gcat = nn(w1, gpre_b)
    width = grad.shape[0]
    return prod, gmix, gpre, gpre_b, gcat[:width], gcat[width:].astype(BF16)


def cut(wide, s, blk):
    return wide[:, s * blk : (s + 1) * blk]


def fold(wide, blk):
    total = cut(wide, 0, blk)
    for s in range(1, CH):
        total = total + cut(wide, s, blk)
    return total


def push_edge(it, gagg, acc, tiles, offs, blk):
    for s in range(CH):
        b = it * CH + s
        slot = edge_slot(b)
        acc[HALO + b + offs[slot, b]] += nn(cut(gagg, s, blk), tiles[b, slot])


def push_inner(b, gagg, acc, first, tiles, offs, blk):
    slot = jnp.where(b < HALO, 2, 1)
    both = nn(gagg[b], lanes([tiles[b, 0], tiles[b, slot]]))
    acc[first + b] += both[:, :blk]
    acc[first + b + offs[slot, b]] += both[:, blk:]


def clear(ref):
    def one(b):
        ref[b] = jnp.zeros(ref.shape[1:], ref.dtype)

    for_blocks(ref.shape[0], one)


def node0_kernel(
    nb, offs, near, far, ext_in, part, tiles, w1t, w2t, bias, gain,
    near_out, far_out, ext, after_ext, agg, act, slope, xhat, inv, bcol, gcol,
):
    blk = tiles.shape[2]
    bcol[...] = column(0.5 * bias[0:1], blk)
    gcol[...] = column(gain[0:1], blk)
    take_rims(near, far, ext, 0, HALO + nb)

    def step(it, c):
        agg_w, act_w, slope_w, xhat_w, inv_w, after = forward_step(
            it, ext, part, tiles, offs, w1t[0], w2t[0], bcol, gcol
        )
        slope_w = slope_w.astype(BF16)
        xhat_b = xhat_w.astype(BF16)
        for s in range(CH):
            b = it * CH + s
            agg[b] = cut(agg_w, s, blk)
            act[b] = cut(act_w, s, blk)
            slope[b] = cut(slope_w, s, blk)
            xhat[b] = cut(xhat_b, s, blk)
            inv[b] = cut(inv_w, s, blk)
            after_ext[HALO + b] = cut(after, s, blk)
        return c

    lax.fori_loop(0, nb // CH, step, 0)
    give_rims(after_ext, HALO, nb, near_out, far_out)


def node1_kernel(
    nb, offs, near, far, ext_in, part, tiles, cott, w1t, w2t, w_in, w2, bias, gain,
    near_out, far_out, ext, h2, agg, act, gmix, gpre, gagg, acc, gb, gg, bcol, gcol,
):
    blk = tiles.shape[2]
    bcol[...] = column(0.5 * bias[1:2], blk)
    gcol[...] = column(gain[1:2], blk)
    gb[...] = jnp.zeros_like(gb)
    gg[...] = jnp.zeros_like(gg)
    clear(acc)
    take_rims(near, far, ext, 0, HALO + nb)

    def step(it, c):
        agg_w, act_w, slope, xhat, inv, after = forward_step(
            it, ext, part, tiles, offs, w1t[1], w2t[1], bcol, gcol
        )
        grad = lanes([cott[it * CH + s] for s in range(CH)]).astype(F32)
        prod, gmix_w, gpre_f, gpre_w, gh, gagg_w = backward_step(
            grad, xhat, inv, slope, w_in[1], w2[1], gcol
        )
        gg[...] += fold(prod, blk)
        gb[...] += fold(gpre_f, blk)
        rest = grad + gh
        for s in range(CH):
            b = it * CH + s
            agg[b] = cut(agg_w, s, blk)
            act[b] = cut(act_w, s, blk)
            h2[b] = cut(after, s, blk)
            gmix[b] = cut(gmix_w, s, blk)
            gpre[b] = cut(gpre_w, s, blk)
            gagg[b] = cut(gagg_w, s, blk)
            acc[HALO + b] += cut(rest, s, blk)
        push_edge(it, gagg_w, acc, tiles, offs, blk)
        return c

    lax.fori_loop(0, nb // CH, step, 0)
    give_sums(acc, nb, near_out, far_out)


def outer_step(blocks, feats, first, agg, act, gmix, gpre, gw):
    width = feats.shape[1]
    gpre_w = lanes([gpre[b] for b in blocks])
    gw[0:width] += nt(lanes([feats[first + b] for b in blocks]), gpre_w)
    gw[width : 2 * width] += nt(lanes([agg[b] for b in blocks]), gpre_w)
    gw[2 * width :] += nt(lanes([act[b] for b in blocks]), lanes([gmix[b] for b in blocks]))


def row_sum(block):
    return jnp.sum(jnp.transpose(block), axis=0, keepdims=True)


def weights_kernel(
    nb, offs, gagg, acc_in, tiles, ext, agg, act, gmix, gpre, gb, gg, h2, acc, gw, gv, out_hbm, out, sem,
):
    blk = tiles.shape[2]
    one = eye(blk)

    def turn(b):
        out[pl.ds(b * blk, blk)] = nt(one, h2[b]).astype(BF16)

    for_blocks(nb, turn)
    put = pltpu.make_async_copy(out, out_hbm, sem.at[0])
    put.start()
    gv[0:1] = row_sum(gb[...])
    gv[1:2] = row_sum(gg[...])
    for_blocks(nb, lambda b: push_inner(b, gagg, acc, HALO, tiles, offs, blk))
    gw[...] = jnp.zeros_like(gw)

    def outer(it, c):
        outer_step([it * CH + s for s in range(CH)], ext, HALO, agg, act, gmix, gpre, gw)
        return c

    lax.fori_loop(0, nb // CH, outer, 0)
    put.wait()


def node2_kernel(
    nb, offs, near, far, acc_in, tiles, slope, xhat, inv, w_in, w2, gain, kept, agg, act, gw1, gv1,
    near_hbm, far_hbm, bundle_hbm, gagg_hbm, acc_hbm,
    gagg, acc, halo, gmix, gpre, gb, gg, gw, gcol, bundle, sem,
):
    blk = tiles.shape[2]
    gcol[...] = column(gain[0:1], blk)
    gb[...] = jnp.zeros_like(gb)
    gg[...] = jnp.zeros_like(gg)
    gw[...] = jnp.zeros_like(gw)
    clear(acc)
    take_rims(near, far, halo, 0, HALO)

    def step(it, c):
        blocks = [it * CH + s for s in range(CH)]
        grad = lanes([acc_in[HALO + b] + halo[b].astype(F32) for b in blocks])
        xhat_w = lanes([xhat[b] for b in blocks]).astype(F32)
        slope_w = lanes([slope[b] for b in blocks]).astype(F32)
        inv_w = lanes([inv[b] for b in blocks])
        prod, gmix_w, gpre_f, gpre_w, gh, gagg_w = backward_step(
            grad, xhat_w, inv_w, slope_w, w_in[0], w2[0], gcol
        )
        gg[...] += fold(prod, blk)
        gb[...] += fold(gpre_f, blk)
        rest = grad + gh
        for s, b in enumerate(blocks):
            gmix[b] = cut(gmix_w, s, blk)
            gpre[b] = cut(gpre_w, s, blk)
            gagg[b] = cut(gagg_w, s, blk)
            acc[HALO + b] += cut(rest, s, blk)
        some = pl.ds(it * CH, CH)
        pltpu.make_async_copy(gagg.at[some], gagg_hbm.at[some], sem.at[1]).start()
        push_edge(it, gagg_w, acc, tiles, offs, blk)
        outer_step(blocks, kept, 0, agg, act, gmix, gpre, gw)
        return c

    lax.fori_loop(0, nb // CH, step, 0)
    put = pltpu.make_async_copy(acc.at[pl.ds(HALO, nb)], acc_hbm, sem.at[0])
    put.start()

    def rim_sum(b):
        halo[b] = acc[b].astype(BF16)
        halo[HALO + b] = acc[HALO + nb + b].astype(BF16)

    for_blocks(HALO, rim_sum)
    sent = send_rims(halo, near_hbm, far_hbm, sem.at[pl.ds(2, 2)])
    devices = bundle.shape[0]
    rows = gw.shape[0]
    share = 2 * rows // devices
    vectors = jnp.concatenate([row_sum(gb[...]), row_sum(gg[...]), gv1[...]], axis=0)
    vectors = jnp.concatenate([vectors, jnp.zeros_like(vectors)], axis=0).astype(BF16)
    for p in range(devices):
        bundle[p, 0:8] = vectors
        at = p * share
        if at + share <= rows:
            mine = gw[at : at + share]
        elif at >= rows:
            mine = gw1[at - rows : at - rows + share]
        else:
            mine = jnp.concatenate([gw[at:rows], gw1[0 : at + share - rows]], axis=0)
        bundle[p, 8 : 8 + share] = mine.astype(BF16)
    out = pltpu.make_async_copy(bundle, bundle_hbm, sem.at[4])
    out.start()
    pltpu.make_async_copy(gagg, gagg_hbm, sem.at[1]).wait()
    for c in [*sent, put, out]:
        c.wait()


def total_kernel(scale, parts, mine_hbm, gbias, ggain, mine, sem):
    total = jnp.sum(parts[...].astype(F32), axis=0) * scale
    mine[...] = jnp.broadcast_to(total[8:][None], mine.shape).astype(BF16)
    put = pltpu.make_async_copy(mine, mine_hbm, sem.at[0])
    put.start()
    gbias[0:1] = total[0:1]
    ggain[0:1] = total[1:2]
    gbias[1:2] = total[2:3]
    ggain[1:2] = total[3:4]
    put.wait()


def final_kernel(
    nb, offs, near, far, acc_hbm, gagg_hbm, tiles_hbm, out_hbm, acc, gagg, tiles, halo, out, sem, tsem
):
    blk = tiles.shape[2]
    per = nb // tsem.shape[0]
    get_a = pltpu.make_async_copy(acc_hbm, acc, sem.at[0])
    get_g = pltpu.make_async_copy(gagg_hbm, gagg, sem.at[1])

    def get_t(it):
        some = pl.ds(it * per, per)
        return pltpu.make_async_copy(tiles_hbm.at[some], tiles.at[some], tsem.at[it])

    get_g.start()
    get_a.start()
    for it in range(nb // per):
        get_t(it).start()
    rims = fetch_rims(near, far, halo, sem.at[pl.ds(2, 2)])
    get_g.wait()
    get_a.wait()

    def push(it, c):
        get_t(it).wait()
        for s in range(per):
            push_inner(it * per + s, gagg, acc, 0, tiles, offs, blk)
        return c

    lax.fori_loop(0, nb // per, push, 0)

    for c in rims:
        c.wait()

    def put(it):
        rows = pl.ds(it * per * blk, per * blk)
        return pltpu.make_async_copy(out.at[rows], out_hbm.at[rows], tsem.at[it])

    def step(it, c):
        for s in range(per):
            b = it * per + s
            out[pl.ds(b * blk, blk)] = jnp.transpose(acc[b] + halo[b].astype(F32))
        put(it).start()
        return c

    lax.fori_loop(0, nb // per, step, 0)
    for it in range(nb // per):
        put(it).wait()


def unpack_kernel(sums, out1_hbm, out2_hbm, out1, out2, sem):
    devices, share, _ = sums.shape
    layers, upper, _ = out1.shape
    rows = upper + out2.shape[1]
    for p in range(devices):
        mine = sums[p].astype(F32)
        at = p * share
        while at < (p + 1) * share:
            layer, row = divmod(at, rows)
            end = min((p + 1) * share, layer * rows + (upper if row < upper else rows))
            piece = mine[at - p * share : end - p * share]
            if row < upper:
                out1[layer, row : row + end - at] = piece
            else:
                out2[layer, row - upper : row - upper + end - at] = piece
            at = end
    puts = [
        pltpu.make_async_copy(out1, out1_hbm, sem.at[0]),
        pltpu.make_async_copy(out2, out2_hbm, sem.at[1]),
    ]
    for p in puts:
        p.start()
    for p in puts:
        p.wait()


def call(
    body, name, args, outs, scratch=(), alias=None, far_args=(), any_args=(), flops=0, moved=0
):
    args = [
        pltpu.with_memory_space_constraint(a, pltpu.HBM) if i in far_args else a
        for i, a in enumerate(args)
    ]
    return pl.pallas_call(
        body,
        name=name,
        in_specs=[
            HBM if i in far_args else ANY if i in any_args else SMEM if a.dtype == jnp.int32 else VMEM
            for i, a in enumerate(args)
        ],
        out_specs=[HBM if len(o) == 3 else VMEM for o in outs],
        out_shape=[
            pltpu.HBM(o[0], o[1]) if len(o) == 3 else jax.ShapeDtypeStruct(o[0], o[1]) for o in outs
        ],
        scratch_shapes=list(scratch),
        input_output_aliases=alias or {},
        compiler_params=pltpu.CompilerParams(vmem_limit_bytes=24 << 20),
        cost_estimate=pl.CostEstimate(flops=flops, bytes_accessed=moved, transcendentals=0),
    )(*args)


def dma(n):
    return pltpu.SemaphoreType.DMA((n,))


def per_device(feats, tile_vals, tile_offs, w_in, bias_in, w_out, gain, cot):
    nodes, width = feats.shape
    nb, slots, blk, _ = tile_vals.shape
    hid = w_out.shape[1]
    layers = w_in.shape[0]
    assert nb == 2 * HALO and width == blk and hid == width and layers == 2
    devices = lax.axis_size("band") * lax.axis_size("rep")
    block = (width, blk)
    full, rim, ext = ((n, *block) for n in (nb, HALO, nb + 2 * HALO))
    whole = (2 * width + hid, hid)
    share = layers * whole[0] // devices
    assert share * devices == layers * whole[0]
    rims = [(rim, BF16), (rim, BF16)]
    v = pltpu.VMEM
    part_of = functools.partial
    tile_flops = 2 * blk * blk * width
    mlp_flops = 2 * nodes * (2 * width * hid + hid * width)
    mib = 2 * nodes * width
    offs = tile_offs.T

    h0, near, far = call(
        part_of(turn_kernel, nb), "turn", (feats,), [(ext, BF16), *rims],
        [v((nodes, width), BF16), dma(4)], far_args=(0,),
        flops=nb * tile_flops, moved=3 * mib,
    )
    near, far = swap(near, False), swap(far, True)
    part, w1t, w2t, w2, kept = call(
        part_of(inner0_kernel, nb), "inner0", (offs, h0, tile_vals, w_in, w_out),
        [(full, F32), ((layers, hid, 2 * width), BF16), ((layers, width, hid), BF16), (w_out.shape, BF16), (full, BF16, True)],
        [dma(1)],
        flops=2 * nb * tile_flops, moved=6 * mib,
    )
    near, far, h0, h1, agg0, act0, slope0, xhat0, inv0 = call(
        part_of(node0_kernel, nb), "node0",
        (offs, near, far, h0, part, tile_vals, w1t, w2t, bias_in, gain),
        [*rims, (ext, BF16), (ext, BF16), (full, BF16), (full, BF16), (full, BF16), (full, BF16), ((nb, 1, blk), F32)],
        [v(block, F32), v(block, F32)], {3: 2},
        flops=nb * tile_flops + mlp_flops, moved=11 * mib,
    )
    near, far = swap(near, False), swap(far, True)
    part, cott = call(
        part_of(inner1_kernel, nb), "inner1", (offs, h1, tile_vals, cot), [(full, F32), (full, BF16)],
        flops=2 * nb * tile_flops, moved=8 * mib,
    )
    near, far, h1, h2, agg1, act1, gmix1, gpre1, gagg, acc, gb1, gg1 = call(
        part_of(node1_kernel, nb), "node1",
        (offs, near, far, h1, part, tile_vals, cott, w1t, w2t, w_in, w2, bias_in, gain),
        [*rims, (ext, BF16), *[(full, BF16)] * 6, (ext, F32), (block, F32), (block, F32)],
        [v(block, F32), v(block, F32)], {3: 2},
        flops=2 * nb * tile_flops + 2 * mlp_flops, moved=16 * mib,
    )
    near, far = swap(near, False), swap(far, True)
    acc, gw1, gv1, out_feats = call(
        part_of(weights_kernel, nb), "weights1",
        (offs, gagg, acc, tile_vals, h1, agg1, act1, gmix1, gpre1, gb1, gg1, h2),
        [(ext, F32), (whole, F32), ((2, hid), F32), ((nodes, width), BF16, True)],
        [v((nodes, width), BF16), dma(1)], {2: 0},
        flops=2 * nb * tile_flops + mlp_flops, moved=16 * mib,
    )
    near, far, bundle, gagg, acc = call(
        part_of(node2_kernel, nb), "node2",
        (offs, near, far, acc, tile_vals, slope0, xhat0, inv0, w_in, w2, gain, kept, agg0, act0, gw1, gv1),
        [(rim, BF16, True), (rim, BF16, True), ((devices, 8 + share, hid), BF16, True), (full, BF16, True), (full, F32, True)],
        [v(full, BF16), v(ext, F32), v(full, BF16), v(full, BF16), v(full, BF16)]
        + [v(block, F32), v(block, F32), v(whole, F32), v(block, F32), v((devices, 8 + share, hid), BF16), dma(5)],
        flops=nb * tile_flops + 2 * mlp_flops, moved=14 * mib,
    )

    parts = lax.all_to_all(bundle, AXES, 0, 0, tiled=True)
    near, far = swap(near, False), swap(far, True)
    mine, grad_bias, grad_gain = call(
        part_of(total_kernel, 1.0 / math.sqrt(nodes * devices)), "total", (parts,),
        [((devices, share, hid), BF16, True), ((layers, hid), F32), ((layers, width), F32)],
        [v((devices, share, hid), BF16), dma(1)],
        flops=nodes * width, moved=mib,
    )
    sums = lax.all_to_all(mine, AXES, 0, 0, tiled=True)
    (grad_feats,) = call(
        part_of(final_kernel, nb), "final", (offs, near, far, acc, gagg, tile_vals),
        [((nodes, width), F32, True)],
        [v(full, F32), v(full, BF16), v((nb, slots, blk, blk), BF16), v(full, BF16), v((nodes, width), F32), dma(4), dma(8)],
        far_args=(3, 4, 5), any_args=(1, 2),
        flops=2 * nb * tile_flops, moved=9 * mib,
    )
    grad_w_in, grad_w_out = call(
        unpack_kernel, "unpack", (sums,),
        [((layers, 2 * width, hid), F32, True), ((layers, hid, width), F32, True)],
        [v((layers, 2 * width, hid), F32), v((layers, hid, width), F32), dma(2)],
        flops=nodes * width, moved=mib,
    )
    return out_feats, grad_feats, grad_w_in, grad_bias, grad_w_out, grad_gain


def solution(mesh):
    placed = (
        P(AXES, None),
        P(AXES, None, None, None),
        P(AXES, None),
        P(),
        P(),
        P(),
        P(),
        P(AXES, None),
    )
    return jax.shard_map(
        per_device,
        mesh=mesh,
        in_specs=placed,
        out_specs=(P(AXES, None), P(AXES, None), P(), P(), P(), P()),
        check_vma=False,
    )
```

time: 389 us -> 101 us (0.26)
  waiting for transfers between devices: 115 us -> 31.7 us
  local copies, waits for them, and re-layouts: 83.5 us -> 4.34 us
  other arithmetic: 77.2 us -> 0 us
  matrix products: 42.9 us -> 0 us
  Pallas kernels: 0 us -> 42.3 us
  blocking collectives: 39.8 us -> 0 us
  between operations: 14.5 us -> 0.81 us
  starting transfers between devices: 13 us -> 21.3 us
    psum x1 -> x0, waiting for transfers between devices: 93.6 us -> none  [per_device(): lax.psum((jnp.stack(win_list), jnp.stack(bias_list), jnp.stack(wout_list)...]
    scatter-add x6 -> x0, other arithmetic: 54.5 us -> none  [the longest x2 40.3 us: per_device(): extended.at[flat_columns].add(contrib.reshape(-1, tile_width, feat_width))]
    dot_general x20 -> x0, matrix products: 42.9 us -> none  [the longest x2 8.61 us: per_device(): jnp.einsum('bkij,bid->bkjd', tile_vals, grad_blocks, preferred_element_ty...]
    pallas_call x0 -> x10, Pallas kernels: none -> 42.3 us  [call(): pl.pallas_call(body, name=name, in_specs=[HBM if i in far_args else ANY i...]
    psum x1 -> x0, blocking collectives: 39.8 us -> none  [per_device(): lax.psum((jnp.stack(win_list), jnp.stack(bias_list), jnp.stack(wout_list)...]
    slice x12 -> x0, local copies, waits for them, and re-layouts: 22.7 us -> none  [the longest x4 12.2 us: per_device(): extended.reshape(-1, feat_width)[rim_rows:rim_rows + node_rows]]
    reshape x5 -> x0, local copies, waits for them, and re-layouts: 19.7 us -> none  [the longest x2 13.2 us: per_device(): contrib.reshape(-1, tile_width, feat_width)]
    unnamed x66 -> x22, local copies, waits for them, and re-layouts: 18.8 us -> 4.34 us
  transfers between devices with their start and end apart: 13 -> 10, of which waited for: 5 -> 5; matrix products, arithmetic and copies ran while one was open for 36% -> 0% of each run, Pallas kernels for 0% -> 21%
where the time goes in v2:
time: 101 us; the launch traced here: 100 us
  Pallas kernels  42.3 us (42%)
  waiting for transfers between devices  31.7 us (31%)
  starting transfers between devices  21.3 us (21%)
  local copies, waits for them, and re-layouts  4.34 us (4%)
    pallas_call x10, Pallas kernels, call(): pl.pallas_call(body, name=name, in_specs=[HBM if i in far_args else ANY i...  42.3 us
    ppermute x8, waiting for transfers between devices, swap(): return lax.ppermute(x, AXES, pairs)  20.5 us
    all_to_all x1, waiting for transfers between devices, per_device(): parts = lax.all_to_all(bundle, AXES, 0, 0, tiled=True)  9.19 us
    ppermute x8, starting transfers between devices, swap(): return lax.ppermute(x, AXES, pairs)  8.33 us
    all_to_all x1, starting transfers between devices, per_device(): sums = lax.all_to_all(mine, AXES, 0, 0, tiled=True)  6.74 us
    all_to_all x1, starting transfers between devices, per_device(): parts = lax.all_to_all(bundle, AXES, 0, 0, tiled=True)  6.21 us
    unnamed x22, local copies, waits for them, and re-layouts  4.34 us
  transfers between devices with their start and end apart: 10, of which 5 were waited for; matrix products, arithmetic and copies ran while one was open for 0% of the time, Pallas kernels for 21%

profile of v2, /device:TPU:1, one launch (start us, length us, event | category | flops | bytes accessed | tf_op | source)
XLA Modules:
  0.0 100.5 jit_solution(6328865810066099462)
XLA Ops:
  0.6 2.3 %turn.1 = (bf16[64,128,128]{2,1,0:T(8,128)(2,1)S(1)}, bf16[16,128,128]{2,1,0:T(8,128)(2,1)S(1)}, bf16[16,128,128]{2,1,0:T(8,128)(2,1)S(1)}) custom-call(bf16[4096,128]{1,0:T(8,128)(2,1)} %x_hbm.1), custom_call_target="tpu_custom_call" | custom-call | flops 134217728 | bytes 3145728 | tf_op jit(solution)/shard_map/turn/pallas_call | solution.py:539
  2.9 0.1 collective-permute-start
  3.0 2.7 %collective-permute-start.1 = (bf16[16,128,128]{2,1,0:T(8,128)(2,1)S(1)}, bf16[16,128,128]{2,1,0:T(8,128)(2,1)S(1)}, u32[]{:S(2)}, u32[]{:S(2)}) collective-permute-start(bf16[16,128,128]{2,1,0:T(8,128)(2,1)S(1)} %get-tuple-element.51), channel_id=1, source_target_pairs={{1,2},{2,1},{3,4},{4,3},{5,6},{6,5},{7,8},{8,7},{9,10},{10,9},{11,... | collective-permute-start | bytes 1572872 | tf_op jit(solution)/shard_map/ppermute | solution.py:60
  5.7 1.9 %copy-done = bf16[32,3,128,128]{3,2,1,0:T(8,128)(2,1)S(1)} copy-done((bf16[32,3,128,128]{3,2,1,0:T(8,128)(2,1)S(1)}, bf16[32,3,128,128]{3,2,1,0:T(8,128)(2,1)}, u32[]{:S(2)}) %copy-start) | copy-done | bytes 3145752
  7.6 0.9 copy-done.2
  8.5 0.7 copy-done.6
  9.2 0.8 copy-done.8
  10.0 2.6 %inner0.1 = (f32[32,128,128]{2,1,0:T(8,128)S(1)}, bf16[2,128,256]{2,1,0:T(8,128)(2,1)S(1)}, bf16[2,128,128]{2,1,0:T(8,128)(2,1)S(1)}, bf16[2,128,128]{2,1,0:T(8,128)(2,1)S(1)}, bf16[32,128,128]{2,1,0:T(8,128)(2,1)}) custom-call(s32[3,32]{1,0:T(4,128)S(1)} %bitcast.1, bf16[64,128,128]{2,1,0:T(8,128)(2,1)S(1)} %get-tuple-element.52.ext.ext_in, ...), custom_call_target="tpu_custom_call" | custom-call | flops 268435456 | bytes 6291456 | tf_op jit(solution)/shard_map/inner0/pallas_call | solution.py:539
  12.7 5.5 %collective-permute-done.1.far = bf16[16,128,128]{2,1,0:T(8,128)(2,1)S(1)} collective-permute-done((bf16[16,128,128]{2,1,0:T(8,128)(2,1)S(1)}, bf16[16,128,128]{2,1,0:T(8,128)(2,1)S(1)}, u32[]{:S(2)}, u32[]{:S(2)}) %collective-permute-start.1) | collective-permute-done | bytes 524320 | tf_op jit(solution)/shard_map/ppermute | solution.py:60
  18.2 0.0 copy-start.7
  18.2 3.9 %node0.1 = (bf16[16,128,128]{2,1,0:T(8,128)(2,1)S(1)}, bf16[16,128,128]{2,1,0:T(8,128)(2,1)S(1)}, bf16[64,128,128]{2,1,0:T(8,128)(2,1)S(1)}, bf16[64,128,128]{2,...) custom-call(s32[3,32]{1,0:T(4,128)S(1)} %bitcast.2, ...), custom_call_target="tpu_custom_call", output_to_operand_aliasing={{2}: (3, {})} | custom-call | flops 536870912 | bytes 11534336 | tf_op jit(solution)/shard_map/node0/pallas_call | solution.py:539
  22.1 0.1 collective-permute-start.2
  22.2 1.8 %collective-permute-start.3 = (bf16[16,128,128]{2,1,0:T(8,128)(2,1)S(1)}, bf16[16,128,128]{2,1,0:T(8,128)(2,1)S(1)}, u32[]{:S(2)}, u32[]{:S(2)}) collective-permute-start(bf16[16,128,128]{2,1,0:T(8,128)(2,1)S(1)} %get-tuple-element.57), channel_id=1, source_target_pairs={{1,2},{2,1},{3,4},{4,3},{5,6},{6,5},{7,8},{8,7},{9,10},{10,9},{11,... | collective-permute-start | bytes 1572872 | tf_op jit(solution)/shard_map/ppermute | solution.py:60
  24.0 4.1 %inner1.1 = (f32[32,128,128]{2,1,0:T(8,128)S(1)}, bf16[32,128,128]{2,1,0:T(8,128)(2,1)S(1)}) custom-call(s32[3,32]{1,0:T(4,128)S(1)} %bitcast.3, bf16[64,128,128]{2,1,0:T(8,128)(2,1)S(1)} %get-tuple-element.58.ext.ext_in, bf16[32,3,128,128]{3,2,1,0:T(8,128)(2,1)S(1)} %copy-done.1, bf16[4096,128]{1,0:T(8,128)(2,1)S(1)} %copy-done.5), custom_call_target="tpu_custom_call" | custom-call | flops 268435456 | bytes 8388608 | tf_op jit(solution)/shard_map/inner1/pallas_call | solution.py:539
  28.2 0.0 collective-permute-done.2.near
  28.2 8.3 %collective-permute-done.3.far = bf16[16,128,128]{2,1,0:T(8,128)(2,1)S(1)} collective-permute-done((bf16[16,128,128]{2,1,0:T(8,128)(2,1)S(1)}, bf16[16,128,128]{2,1,0:T(8,128)(2,1)S(1)}, u32[]{:S(2)}, u32[]{:S(2)}) %collective-permute-start.3) | collective-permute-done | bytes 524320 | tf_op jit(solution)/shard_map/ppermute | solution.py:60
  36.5 7.2 %node1.1 = (bf16[16,128,128]{2,1,0:T(8,128)(2,1)S(1)}, bf16[16,128,128]{2,1,0:T(8,128)(2,1)S(1)}, bf16[64,128,128]{2,1,0:T(8,128)(2,1)S(1)}, bf16[32,128,128]{2,...) custom-call(s32[3,32]{1,0:T(4,128)S(1)} %bitcast.4, ...), custom_call_target="tpu_custom_call", output_to_operand_aliasing={{2}: (3, {})} | custom-call | flops 1073741824 | bytes 16777216 | tf_op jit(solution)/shard_map/node1/pallas_call | solution.py:539
  43.7 0.1 collective-permute-start.4
  43.7 1.8 %collective-permute-start.5 = (bf16[16,128,128]{2,1,0:T(8,128)(2,1)S(1)}, bf16[16,128,128]{2,1,0:T(8,128)(2,1)S(1)}, u32[]{:S(2)}, u32[]{:S(2)}) collective-permute-start(bf16[16,128,128]{2,1,0:T(8,128)(2,1)S(1)} %get-tuple-element.74), channel_id=1, source_target_pairs={{1,2},{2,1},{3,4},{4,3},{5,6},{6,5},{7,8},{8,7},{9,10},{10,9},{11,... | collective-permute-start | bytes 1572872 | tf_op jit(solution)/shard_map/ppermute | solution.py:60
  45.5 5.8 %weights1.1 = (f32[64,128,128]{2,1,0:T(8,128)S(1)}, f32[384,128]{1,0:T(8,128)S(1)}, f32[2,128]{1,0:T(2,128)S(1)}, bf16[4096,128]{1,0:T(8,128)(2,1)}) custom-call(s32[3,32]{1,0:T(4,128)S(1)} %bitcast.5, bf16[32,128,128]{2,1,0:T(8,128)(2,1)S(1)} %get-tuple-element.62.gagg, ...), custom_call_target="tpu_custom_call", output_to_operand_aliasing={{0}: (2, {})} | custom-call | flops 671088640 | bytes 16777216 | tf_op jit(solution)/shard_map/weights1/pallas_call | solution.py:539
  51.3 0.0 collective-permute-done.4.near
  51.3 6.7 %collective-permute-done.5.far = bf16[16,128,128]{2,1,0:T(8,128)(2,1)S(1)} collective-permute-done((bf16[16,128,128]{2,1,0:T(8,128)(2,1)S(1)}, bf16[16,128,128]{2,1,0:T(8,128)(2,1)S(1)}, u32[]{:S(2)}, u32[]{:S(2)}) %collective-permute-start.5) | collective-permute-done | bytes 524320 | tf_op jit(solution)/shard_map/ppermute | solution.py:60
  58.0 7.2 %node2.1 = (bf16[16,128,128]{2,1,0:T(8,128)(2,1)}, bf16[16,128,128]{2,1,0:T(8,128)(2,1)}, bf16[32,32,128]{2,1,0:T(8,128)(2,1)}, bf16[32,128,128]{2,1,0:T(8,128)(2,1)}, f32[32,128,128]{2,1,0:T(8,128)}) custom-call(s32[3,32]{1,0:T(4,128)S(1)} %bitcast.6, bf16[16,128,128]{2,1,0:T(8,128)(2,1)S(1)} %collective-permute-done.4.near, ...), custom_call_target="tpu_custom_call" | custom-call | flops 939524096 | bytes 14680064 | tf_op jit(solution)/shard_map/node2/pallas_call | solution.py:539
  65.2 6.2 %all-to-all-start = ((bf16[32,32,128]{2,1,0:T(8,128)(2,1)}), bf16[32,32,128]{2,1,0:T(8,128)(2,1)S(1)}, u32[]{:S(2)}, u32[]{:S(2)}) async-start(bf16[32,32,128]{2,1,0:T(8,128)(2,1)} %get-tuple-element.88), calls=%async_computation | async-start | bytes 524288 | tf_op jit(solution)/shard_map/all_to_all | solution.py:629
  71.4 0.3 collective-permute-start.6
  71.8 1.5 %collective-permute-start.7 = (bf16[16,128,128]{2,1,0:T(8,128)(2,1)}, bf16[16,128,128]{2,1,0:T(8,128)(2,1)S(1)}, u32[]{:S(2)}, u32[]{:S(2)}) collective-permute-start(bf16[16,128,128]{2,1,0:T(8,128)(2,1)} %get-tuple-element.85), channel_id=1, source_target_pairs={{1,2},{2,1},{3,4},{4,3},{5,6},{6,5},{7,8},{8,7},{9,10},{10,9},{11,... | collective-permute-start | bytes 1572872 | tf_op jit(solution)/shard_map/ppermute | solution.py:60
  73.3 9.2 %all-to-all-done.parts = bf16[32,32,128]{2,1,0:T(8,128)(2,1)S(1)} async-done(((bf16[32,32,128]{2,1,0:T(8,128)(2,1)}), bf16[32,32,128]{2,1,0:T(8,128)(2,1)S(1)}, u32[]{:S(2)}, u32[]{:S(2)}) %all-to-all-start) | async-done | bytes 262176 | tf_op jit(solution)/shard_map/all_to_all | solution.py:629
  82.5 1.3 %total.1 = (bf16[32,24,128]{2,1,0:T(8,128)(2,1)}, f32[2,128]{1,0:T(2,128)}, f32[2,128]{1,0:T(2,128)}) custom-call(bf16[32,32,128]{2,1,0:T(8,128)(2,1)S(1)} %all-to-all-done.parts), custom_call_target="tpu_custom_call" | custom-call | flops 524288 | bytes 1048576 | tf_op jit(solution)/shard_map/total/pallas_call | solution.py:539
  83.8 6.7 %all-to-all-start.1 = ((bf16[32,24,128]{2,1,0:T(8,128)(2,1)}), bf16[32,24,128]{2,1,0:T(8,128)(2,1)S(1)}, u32[]{:S(2)}, u32[]{:S(2)}) async-start(bf16[32,24,128]{2,1,0:T(8,128)(2,1)} %get-tuple-element.89), calls=%async_computation.1 | async-start | bytes 393216 | tf_op jit(solution)/shard_map/all_to_all | solution.py:637
  90.5 7.2 %final.1 = f32[4096,128]{1,0:T(8,128)} custom-call(s32[3,32]{1,0:T(4,128)S(1)} %bitcast.7, bf16[16,128,128]{2,1,0:T(8,128)(2,1)S(1)} %collective-permute-done.6.near, bf16[16,128,128]{2,1,0:T(8,128)(2,1)S(1)} %collective-permute-done.7.far, f32[32,128,128]{2,1,0:T(8,128)} %get-tuple-element.86.acc_hbm, bf16[32,128,128]{2,1,0:T(8,128)(2,1)} %get-tuple-element.87.gagg_hbm, ...), custom_call_target="tpu_custom_call" | custom-call | flops 268435456 | bytes 9437184 | tf_op jit(solution)/shard_map/final/pallas_call | solution.py:539
  97.7 2.0 %all-to-all-done.1.sums = bf16[32,24,128]{2,1,0:T(8,128)(2,1)S(1)} async-done(((bf16[32,24,128]{2,1,0:T(8,128)(2,1)}), bf16[32,24,128]{2,1,0:T(8,128)(2,1)S(1)}, u32[]{:S(2)}, u32[]{:S(2)}) %all-to-all-start.1) | async-done | bytes 196640 | tf_op jit(solution)/shard_map/all_to_all | solution.py:637
  99.7 0.8 unpack.1
  (20 shorter events, 0.0 us)
Async XLA Ops:
  2.9 9.8 %collective-permute-start = (bf16[16,128,128]{2,1,0:T(8,128)(2,1)S(1)}, bf16[16,128,128]{2,1,0:T(8,128)(2,1)S(1)}, u32[]{:S(2)}, u32[]{:S(2)}) collective-permute-start(bf16[16,128,128]{2,1,0:T(8,128)(2,1)S(1)} %get-tuple-element.50), channel_id=1, source_target_pairs={{0,1},{1,0},{2,3},{3,2},{4,5},{5,4},{6,7},{7,6},{8,9},{9,8},{10,11... | collective-permute-start | bytes 1572872 | tf_op jit(solution)/shard_map/ppermute | solution.py:60
  3.0 15.2 %collective-permute-start.1 = (bf16[16,128,128]{2,1,0:T(8,128)(2,1)S(1)}, bf16[16,128,128]{2,1,0:T(8,128)(2,1)S(1)}, u32[]{:S(2)}, u32[]{:S(2)}) collective-permute-start(bf16[16,128,128]{2,1,0:T(8,128)(2,1)S(1)} %get-tuple-element.51), channel_id=1, source_target_pairs={{1,2},{2,1},{3,4},{4,3},{5,6},{6,5},{7,8},{8,7},{9,10},{10,9},{11,... | collective-permute-start | bytes 1572872 | tf_op jit(solution)/shard_map/ppermute | solution.py:60
  5.7 1.9 %copy-start = (bf16[32,3,128,128]{3,2,1,0:T(8,128)(2,1)S(1)}, bf16[32,3,128,128]{3,2,1,0:T(8,128)(2,1)}, u32[]{:S(2)}) copy-start(bf16[32,3,128,128]{3,2,1,0:T(8,128)(2,1)} %tiles_hbm.1) | copy-start | bytes 9437188
  7.6 0.9 copy-start.2
  8.5 0.7 copy-start.6
  9.2 0.8 copy-start.8
  10.0 8.2 %copy-start.9 = (f32[2,128]{1,0:T(2,128)S(1)}, f32[2,128]{1,0:T(2,128)}, u32[]{:S(2)}) copy-start(f32[2,128]{1,0:T(2,128)} %gain.5) | copy-start | bytes 3076
  10.0 8.2 %copy-start.10 = (f32[2,128]{1,0:T(2,128)S(1)}, f32[2,128]{1,0:T(2,128)}, u32[]{:S(2)}) copy-start(f32[2,128]{1,0:T(2,128)} %bias.3) | copy-start | bytes 3076
  18.2 5.8 %copy-start.1 = (bf16[32,3,128,128]{3,2,1,0:T(8,128)(2,1)S(1)}, bf16[32,3,128,128]{3,2,1,0:T(8,128)(2,1)}, u32[]{:S(2)}) copy-start(bf16[32,3,128,128]{3,2,1,0:T(8,128)(2,1)} %tiles_hbm.1) | copy-start | bytes 9437188
  18.2 5.8 %copy-start.5 = (bf16[4096,128]{1,0:T(8,128)(2,1)S(1)}, bf16[4096,128]{1,0:T(8,128)(2,1)}, u32[]{:S(2)}) copy-start(bf16[4096,128]{1,0:T(8,128)(2,1)} %cot.1) | copy-start | bytes 3145732
  18.2 5.8 %copy-start.7 = (s32[32,3]{0,1:T(4,128)S(1)}, s32[32,3]{0,1:T(4,128)}, u32[]{:S(2)}) copy-start(s32[32,3]{0,1:T(4,128)} %param.10) | copy-start | bytes 1156
  22.1 6.0 %collective-permute-start.2 = (bf16[16,128,128]{2,1,0:T(8,128)(2,1)S(1)}, bf16[16,128,128]{2,1,0:T(8,128)(2,1)S(1)}, u32[]{:S(2)}, u32[]{:S(2)}) collective-permute-start(bf16[16,128,128]{2,1,0:T(8,128)(2,1)S(1)} %get-tuple-element.56), channel_id=1, source_target_pairs={{0,1},{1,0},{2,3},{3,2},{4,5},{5,4},{6,7},{7,6},{8,9},{9,8},{10,11... | collective-permute-start | bytes 1572872 | tf_op jit(solution)/shard_map/ppermute | solution.py:60
  22.2 14.3 %collective-permute-start.3 = (bf16[16,128,128]{2,1,0:T(8,128)(2,1)S(1)}, bf16[16,128,128]{2,1,0:T(8,128)(2,1)S(1)}, u32[]{:S(2)}, u32[]{:S(2)}) collective-permute-start(bf16[16,128,128]{2,1,0:T(8,128)(2,1)S(1)} %get-tuple-element.57), channel_id=1, source_target_pairs={{1,2},{2,1},{3,4},{4,3},{5,6},{6,5},{7,8},{8,7},{9,10},{10,9},{11,... | collective-permute-start | bytes 1572872 | tf_op jit(solution)/shard_map/ppermute | solution.py:60
  24.0 12.5 %copy-start.3 = (bf16[2,256,128]{2,1,0:T(8,128)(2,1)S(1)}, bf16[2,256,128]{2,1,0:T(8,128)(2,1)}, u32[]{:S(2)}) copy-start(bf16[2,256,128]{2,1,0:T(8,128)(2,1)} %w_in.5) | copy-start | bytes 393220
  43.7 7.7 %collective-permute-start.4 = (bf16[16,128,128]{2,1,0:T(8,128)(2,1)S(1)}, bf16[16,128,128]{2,1,0:T(8,128)(2,1)S(1)}, u32[]{:S(2)}, u32[]{:S(2)}) collective-permute-start(bf16[16,128,128]{2,1,0:T(8,128)(2,1)S(1)} %get-tuple-element.73), channel_id=1, source_target_pairs={{0,1},{1,0},{2,3},{3,2},{4,5},{5,4},{6,7},{7,6},{8,9},{9,8},{10,11... | collective-permute-start | bytes 1572872 | tf_op jit(solution)/shard_map/ppermute | solution.py:60
  43.7 14.3 %collective-permute-start.5 = (bf16[16,128,128]{2,1,0:T(8,128)(2,1)S(1)}, bf16[16,128,128]{2,1,0:T(8,128)(2,1)S(1)}, u32[]{:S(2)}, u32[]{:S(2)}) collective-permute-start(bf16[16,128,128]{2,1,0:T(8,128)(2,1)S(1)} %get-tuple-element.74), channel_id=1, source_target_pairs={{1,2},{2,1},{3,4},{4,3},{5,6},{6,5},{7,8},{8,7},{9,10},{10,9},{11,... | collective-permute-start | bytes 1572872 | tf_op jit(solution)/shard_map/ppermute | solution.py:60
  45.5 12.5 %copy-start.4 = (bf16[32,128,128]{2,1,0:T(8,128)(2,1)S(1)}, bf16[32,128,128]{2,1,0:T(8,128)(2,1)}, u32[]{:S(2)}) copy-start(bf16[32,128,128]{2,1,0:T(8,128)(2,1)} %get-tuple-element.79.kept) | copy-start | bytes 3145732
  65.2 17.2 %all-to-all-start = ((bf16[32,32,128]{2,1,0:T(8,128)(2,1)}), bf16[32,32,128]{2,1,0:T(8,128)(2,1)S(1)}, u32[]{:S(2)}, u32[]{:S(2)}) async-start(bf16[32,32,128]{2,1,0:T(8,128)(2,1)} %get-tuple-element.88), calls=%async_computation | async-start | bytes 524288 | tf_op jit(solution)/shard_map/all_to_all | solution.py:629
  71.4 19.1 %collective-permute-start.6 = (bf16[16,128,128]{2,1,0:T(8,128)(2,1)}, bf16[16,128,128]{2,1,0:T(8,128)(2,1)S(1)}, u32[]{:S(2)}, u32[]{:S(2)}) collective-permute-start(bf16[16,128,128]{2,1,0:T(8,128)(2,1)} %get-tuple-element.84), channel_id=1, source_target_pairs={{0,1},{1,0},{2,3},{3,2},{4,5},{5,4},{6,7},{7,6},{8,9},{9,8},{10,11... | collective-permute-start | bytes 1572872 | tf_op jit(solution)/shard_map/ppermute | solution.py:60
  71.8 18.8 %collective-permute-start.7 = (bf16[16,128,128]{2,1,0:T(8,128)(2,1)}, bf16[16,128,128]{2,1,0:T(8,128)(2,1)S(1)}, u32[]{:S(2)}, u32[]{:S(2)}) collective-permute-start(bf16[16,128,128]{2,1,0:T(8,128)(2,1)} %get-tuple-element.85), channel_id=1, source_target_pairs={{1,2},{2,1},{3,4},{4,3},{5,6},{6,5},{7,8},{8,7},{9,10},{10,9},{11,... | collective-permute-start | bytes 1572872 | tf_op jit(solution)/shard_map/ppermute | solution.py:60
  83.8 15.9 %all-to-all-start.1 = ((bf16[32,24,128]{2,1,0:T(8,128)(2,1)}), bf16[32,24,128]{2,1,0:T(8,128)(2,1)S(1)}, u32[]{:S(2)}, u32[]{:S(2)}) async-start(bf16[32,24,128]{2,1,0:T(8,128)(2,1)} %get-tuple-element.89), calls=%async_computation.1 | async-start | bytes 393216 | tf_op jit(solution)/shard_map/all_to_all | solution.py:637

commit v3 on v2

v3 whole, which is shorter than its diff:
```python
import functools
import math

import jax
import jax.numpy as jnp
from jax import lax
from jax.experimental import pallas as pl
from jax.experimental.pallas import tpu as pltpu
from jax.sharding import PartitionSpec as P


HALO = 16
EPS = 1e-05
AXES = ("band", "rep")
F32 = jnp.float32
BF16 = jnp.bfloat16
CH = 8
HBM = pl.BlockSpec(memory_space=pltpu.HBM)
ANY = pl.BlockSpec(memory_space=pl.ANY)
SMEM = pl.BlockSpec(memory_space=pltpu.SMEM)
VMEM = pl.BlockSpec(memory_space=pltpu.VMEM)


def nt(a, b):
    return lax.dot_general(a, b, (((1,), (1,)), ((), ())), preferred_element_type=F32)


def nn(a, b):
    return jnp.dot(a, b, preferred_element_type=F32)


def eye(n):
    rows = lax.broadcasted_iota(jnp.int32, (n, n), 0)
    cols = lax.broadcasted_iota(jnp.int32, (n, n), 1)
    return (rows == cols).astype(BF16)


def column(row, width):
    return jnp.transpose(jnp.broadcast_to(row, (width, row.shape[1])))


def lanes(parts):
    return jnp.concatenate(parts, axis=1)


def widen(block, times):
    return lanes([block] * times)


def parity():
    place = lax.axis_index("band") * lax.axis_size("rep") + lax.axis_index("rep")
    return lax.rem(place, 2)


def swap(x, far):
    n = lax.axis_size("band") * lax.axis_size("rep")
    pairs = []
    for c in range(n // 2):
        a, b = (2 * c, 2 * c + 1) if not far else (2 * c + 1, (2 * c + 2) % n)
        pairs += [(a, b), (b, a)]
    return lax.ppermute(x, AXES, pairs)


def rim_at(nb, far):
    odd = parity()
    return (odd if far else 1 - odd) * (HALO + nb)


def rows_at(far):
    odd = parity()
    return (odd if far else 1 - odd) * HALO


def for_blocks(count, body, per=4):
    def step(it, c):
        for s in range(per):
            body(it * per + s)
        return c

    lax.fori_loop(0, count // per, step, 0)


def turn_rows(x, ext, out, base, one):
    blk = ext.shape[2]

    def turn(b):
        block = nt(one, x[pl.ds(b * blk, blk)]).astype(BF16)
        ext[HALO + base + b] = block
        out[b] = block

    for_blocks(HALO, turn, 8)


def half_of(x_hbm, x, base, sem):
    rows = x.shape[0]
    return pltpu.make_async_copy(
        x_hbm.at[pl.ds(pl.multiple_of(base * (rows // HALO), rows), rows)], x, sem
    )


def turn_kernel(x_hbm, ext, far, x, sem):
    base = rows_at(True)
    get = half_of(x_hbm, x, base, sem.at[0])
    get.start()
    one = eye(ext.shape[2])
    get.wait()
    turn_rows(x, ext, far, base, one)


def fetch_rims(near_hbm, far_hbm, rims, sem):
    copies = [
        pltpu.make_async_copy(far_hbm, rims.at[pl.ds(rows_at(True), HALO)], sem.at[0]),
        pltpu.make_async_copy(near_hbm, rims.at[pl.ds(rows_at(False), HALO)], sem.at[1]),
    ]
    for c in copies:
        c.start()
    return copies


def take_rim(rim, buf, at):
    def one(b):
        buf[at + b] = rim[b]

    for_blocks(HALO, one, 8)


def inner_tile(b, ext, tiles, offs, part):
    slot = jnp.where(b < HALO, 2, 1)
    left = lanes([ext[HALO + b], ext[HALO + b + offs[slot, b]]])
    part[b] = nt(left, lanes([tiles[b, 0], tiles[b, slot]]))


def inner0_kernel(
    nb, offs, ext_in, x_hbm, tiles_hbm, w_in_hbm, w_out_hbm,
    ext, near, part, w1t, w2t, w2, kept, x, tiles, w_in, w_out, sem, tsem,
):
    base = rows_at(False)
    per = nb // tsem.shape[0]

    def get_t(it):
        some = pl.ds(it * per, per)
        return pltpu.make_async_copy(tiles_hbm.at[some], tiles.at[some], tsem.at[it])

    get = half_of(x_hbm, x, base, sem.at[1])
    gets = [
        pltpu.make_async_copy(w_in_hbm, w_in, sem.at[2]),
        pltpu.make_async_copy(w_out_hbm, w_out, sem.at[3]),
    ]
    get.start()
    for it in range(nb // per):
        get_t(it).start()
    for c in gets:
        c.start()
    one = eye(tiles.shape[2])
    get.wait()
    turn_rows(x, ext, near, base, one)
    keep = pltpu.make_async_copy(ext.at[pl.ds(HALO, nb)], kept, sem.at[0])
    keep.start()

    def step(it, c):
        get_t(it).wait()
        for s in range(per):
            inner_tile(it * per + s, ext, tiles, offs, part)
        return c

    lax.fori_loop(0, nb // per, step, 0)
    for c in gets:
        c.wait()
    for layer in range(w_in.shape[0]):
        w1t[layer] = (0.5 * nt(one, w_in[layer])).astype(BF16)
        w2t[layer] = nt(one, w_out[layer]).astype(BF16)
        w2[layer] = (0.5 * w_out[layer].astype(F32)).astype(BF16)
    keep.wait()


def inner1_kernel(nb, offs, ext, tiles, cot, part, cott):
    for_blocks(nb, lambda b: inner_tile(b, ext, tiles, offs, part))
    blk = tiles.shape[2]
    one = eye(blk)

    def turn(b):
        cott[b] = nt(one, cot[pl.ds(b * blk, blk)]).astype(BF16)

    for_blocks(nb, turn)


def edge_slot(b):
    return jnp.where(b < HALO, 1, 2)


def forward_step(blocks, ext, part, tiles, offs, w1t, w2t, bias, gain):
    agg = []
    for b in blocks:
        slot = edge_slot(b)
        agg.append((part[b] + nt(ext[HALO + b + offs[slot, b]], tiles[b, slot])).astype(BF16))
    agg = lanes(agg)
    feats = lanes([ext[HALO + b] for b in blocks])
    joined = jnp.concatenate([feats, agg], axis=0)
    half = nn(w1t, joined) + widen(bias[...], CH)
    t = jnp.tanh(half)
    up = 1.0 + t
    act = (half * up).astype(BF16)
    slope = up * (1.0 + half * (1.0 - t))
    mix = nn(w2t, act)
    centred = mix - jnp.mean(mix, axis=0, keepdims=True)
    inv = lax.rsqrt(jnp.mean(centred * centred, axis=0, keepdims=True) + EPS)
    xhat = centred * inv
    after = (feats.astype(F32) + xhat * widen(gain[...], CH)).astype(BF16)
    return agg, act, slope, xhat, inv, after


def backward_step(grad, xhat, inv, slope, w1, w2, gain):
    wide = widen(gain[...], CH)
    prod = grad * xhat
    gx = grad * wide
    gmix = inv * (
        gx - jnp.mean(gx, axis=0, keepdims=True) - xhat * jnp.mean(prod * wide, axis=0, keepdims=True)
    )
    gmix = gmix.astype(BF16)
    gpre = nn(w2, gmix) * slope
    gpre_b = gpre.astype(BF16)
    gcat = nn(w1, gpre_b)
    width = grad.shape[0]
    return prod, gmix, gpre, gpre_b, gcat[:width], gcat[width:].astype(BF16)


def cut(wide, s, blk):
    return wide[:, s * blk : (s + 1) * blk]


def fold(wide, blk):
    total = cut(wide, 0, blk)
    for s in range(1, CH):
        total = total + cut(wide, s, blk)
    return total


def push_edge(blocks, gagg, acc, tiles, offs, blk):
    for s, b in enumerate(blocks):
        slot = edge_slot(b)
        acc[HALO + b + offs[slot, b]] += nn(cut(gagg, s, blk), tiles[b, slot])


def push_inner(b, gagg, acc, first, tiles, offs, blk):
    slot = jnp.where(b < HALO, 2, 1)
    both = nn(gagg, lanes([tiles[b, 0], tiles[b, slot]]))
    acc[first + b] += both[:, :blk]
    acc[first + b + offs[slot, b]] += both[:, blk:]


def clear(ref):
    def one(b):
        ref[b] = jnp.zeros(ref.shape[1:], ref.dtype)

    for_blocks(ref.shape[0], one)


def node0_kernel(
    nb, is_far, offs, rim, ext_in, part, tiles, w1t, w2t, bias, gain, *refs
):
    rim_out, ext, after_ext, agg, act, slope, xhat, inv, bcol, gcol = refs if is_far else refs[1:]
    blk = tiles.shape[2]
    bcol[...] = column(0.5 * bias[0:1], blk)
    gcol[...] = column(gain[0:1], blk)
    take_rim(rim, ext, rim_at(nb, is_far))
    base = rows_at(is_far)

    def step(it, c):
        local = [it * CH + s for s in range(CH)]
        agg_w, act_w, slope_w, xhat_w, inv_w, after = forward_step(
            [base + b for b in local], ext, part, tiles, offs, w1t[0], w2t[0], bcol, gcol
        )
        slope_w = slope_w.astype(BF16)
        xhat_b = xhat_w.astype(BF16)
        for s, b in enumerate(local):
            agg[b] = cut(agg_w, s, blk)
            act[b] = cut(act_w, s, blk)
            slope[b] = cut(slope_w, s, blk)
            xhat[b] = cut(xhat_b, s, blk)
            inv[b] = cut(inv_w, s, blk)
            after_ext[HALO + base + b] = cut(after, s, blk)
            rim_out[b] = cut(after, s, blk)
        return c

    lax.fori_loop(0, HALO // CH, step, 0)


def node1_kernel(
    nb, is_far, offs, rim, ext_in, part, tiles, cott, w1t, w2t, w_in, w2, bias, gain, *refs
):
    rim_out, ext, h2, agg, act, gmix, gpre, gagg, acc, gb, gg, bcol, gcol = refs if is_far else refs[3:]
    blk = tiles.shape[2]
    bcol[...] = column(0.5 * bias[1:2], blk)
    gcol[...] = column(gain[1:2], blk)
    if is_far:
        gb[...] = jnp.zeros_like(gb)
        gg[...] = jnp.zeros_like(gg)
        clear(acc)
    take_rim(rim, ext, rim_at(nb, is_far))
    base = rows_at(is_far)

    def step(it, c):
        local = [it * CH + s for s in range(CH)]
        blocks = [base + b for b in local]
        agg_w, act_w, slope, xhat, inv, after = forward_step(
            blocks, ext, part, tiles, offs, w1t[1], w2t[1], bcol, gcol
        )
        grad = lanes([cott[b] for b in blocks]).astype(F32)
        prod, gmix_w, gpre_f, gpre_w, gh, gagg_w = backward_step(
            grad, xhat, inv, slope, w_in[1], w2[1], gcol
        )
        gg[...] += fold(prod, blk)
        gb[...] += fold(gpre_f, blk)
        rest = grad + gh
        for s, b in enumerate(local):
            agg[b] = cut(agg_w, s, blk)
            act[b] = cut(act_w, s, blk)
            h2[b] = cut(after, s, blk)
            gmix[b] = cut(gmix_w, s, blk)
            gpre[b] = cut(gpre_w, s, blk)
            gagg[b] = cut(gagg_w, s, blk)
            acc[HALO + base + b] += cut(rest, s, blk)
        push_edge(blocks, gagg_w, acc, tiles, offs, blk)
        return c

    lax.fori_loop(0, HALO // CH, step, 0)
    at = rim_at(nb, is_far)

    def give(b):
        rim_out[b] = acc[at + b].astype(BF16)

    for_blocks(HALO, give, 8)


def outer_step(local, feats, first, agg, act, gmix, gpre, gw):
    width = feats.shape[1]
    gpre_w = lanes([gpre[b] for b in local])
    gw[0:width] += nt(lanes([feats[first + b] for b in local]), gpre_w)
    gw[width : 2 * width] += nt(lanes([agg[b] for b in local]), gpre_w)
    gw[2 * width :] += nt(lanes([act[b] for b in local]), lanes([gmix[b] for b in local]))


def row_sum(block):
    return jnp.sum(jnp.transpose(block), axis=0, keepdims=True)


def weights_kernel(offs, acc_in, tiles, ext, gb, gg, *refs):
    halves, (acc, gw, gv, h2_hbm, sem) = (refs[:6], refs[6:12]), refs[12:]
    blk = tiles.shape[2]
    puts = [
        pltpu.make_async_copy(half[0], h2_hbm.at[pl.ds(rows_at(is_far), HALO)], sem.at[i])
        for i, (is_far, half) in enumerate(zip((True, False), halves))
    ]
    for c in puts:
        c.start()
    gv[0:1] = row_sum(gb[...])
    gv[1:2] = row_sum(gg[...])
    gw[...] = jnp.zeros_like(gw)
    for is_far, (_, agg, act, gmix, gpre, gagg) in zip((True, False), halves):
        base = rows_at(is_far)
        for_blocks(HALO, lambda b: push_inner(base + b, gagg[b], acc, HALO, tiles, offs, blk))

        def outer(it, c):
            local = [it * CH + s for s in range(CH)]
            outer_step(local, ext, HALO + base, agg, act, gmix, gpre, gw)
            return c

        lax.fori_loop(0, HALO // CH, outer, 0)
    for c in puts:
        c.wait()


def output_kernel(nb, h_hbm, out_hbm, h, out, sem):
    blk = h.shape[2]
    per = nb // sem.shape[0]

    def get(it):
        some = pl.ds(it * per, per)
        return pltpu.make_async_copy(h_hbm.at[some], h.at[some], sem.at[it])

    def put(it):
        rows = pl.ds(pl.multiple_of(it * per * blk, per * blk), per * blk)
        return pltpu.make_async_copy(out.at[rows], out_hbm.at[rows], sem.at[it])

    for it in range(nb // per):
        get(it).start()
    one = eye(blk)

    def step(it, c):
        get(it).wait()
        for s in range(per):
            b = it * per + s
            out[pl.ds(pl.multiple_of(b * blk, blk), blk)] = nt(one, h[b]).astype(BF16)
        put(it).start()
        return c

    lax.fori_loop(0, nb // per, step, 0)
    for it in range(nb // per):
        put(it).wait()


def node2_kernel(nb, is_far, offs, rim, acc_in, tiles, w_in, w2, gain, kept, agg, act, slope, xhat, inv, *refs):
    if is_far:
        (near_in, gw1, gv1, *_, near_hbm, far_hbm, bundle_hbm, gagg_hbm, acc_hbm,
         acc, gb, gg, gw, gagg, gmix, gpre, gcol, rims, bundle, sem) = refs
    else:
        acc, gb, gg, gw, gagg_hbm, near_sum, gagg, gmix, gpre, gcol, sem = refs
    blk = tiles.shape[2]
    gcol[...] = column(gain[0:1], blk)
    if is_far:
        pass
    else:
        gb[...] = jnp.zeros_like(gb)
        gg[...] = jnp.zeros_like(gg)
        gw[...] = jnp.zeros_like(gw)
        clear(acc)
    base = rows_at(is_far)

    def step(it, c):
        local = [it * CH + s for s in range(CH)]
        blocks = [base + b for b in local]
        grad = lanes([acc_in[HALO + base + b] + rim[b].astype(F32) for b in local])
        xhat_w = lanes([xhat[b] for b in local]).astype(F32)
        slope_w = lanes([slope[b] for b in local]).astype(F32)
        inv_w = lanes([inv[b] for b in local])
        prod, gmix_w, gpre_f, gpre_w, gh, gagg_w = backward_step(
            grad, xhat_w, inv_w, slope_w, w_in[0], w2[0], gcol
        )
        gg[...] += fold(prod, blk)
        gb[...] += fold(gpre_f, blk)
        rest = grad + gh
        for s, b in enumerate(local):
            gmix[b] = cut(gmix_w, s, blk)
            gpre[b] = cut(gpre_w, s, blk)
            gagg[b] = cut(gagg_w, s, blk)
            acc[HALO + base + b] += cut(rest, s, blk)
        some = pl.ds(it * CH, CH)
        pltpu.make_async_copy(gagg.at[some], gagg_hbm.at[some], sem.at[1]).start()
        push_edge(blocks, gagg_w, acc, tiles, offs, blk)
        outer_step(local, kept, base, agg, act, gmix, gpre, gw)
        return c

    lax.fori_loop(0, HALO // CH, step, 0)
    at = rim_at(nb, is_far)
    if not is_far:

        def give(b):
            near_sum[b] = acc[at + b].astype(BF16)

        for_blocks(HALO, give, 8)
        pltpu.make_async_copy(gagg, gagg_hbm, sem.at[1]).wait()
        return
    put = pltpu.make_async_copy(acc.at[pl.ds(HALO, nb)], acc_hbm, sem.at[0])
    put.start()

    def rim_sum(b):
        rims[b] = acc[at + b].astype(BF16)

    for_blocks(HALO, rim_sum, 8)
    sent = [
        pltpu.make_async_copy(rims, far_hbm, sem.at[2]),
        pltpu.make_async_copy(near_in, near_hbm, sem.at[3]),
    ]
    for c in sent:
        c.start()
    devices = bundle.shape[0]
    rows = gw.shape[0]
    share = 2 * rows // devices
    vectors = jnp.concatenate([row_sum(gb[...]), row_sum(gg[...]), gv1[...]], axis=0)
    vectors = jnp.concatenate([vectors, jnp.zeros_like(vectors)], axis=0).astype(BF16)
    for p in range(devices):
        bundle[p, 0:8] = vectors
        first = p * share
        if first + share <= rows:
            mine = gw[first : first + share]
        elif first >= rows:
            mine = gw1[first - rows : first - rows + share]
        else:
            mine = jnp.concatenate([gw[first:rows], gw1[0 : first + share - rows]], axis=0)
        bundle[p, 8 : 8 + share] = mine.astype(BF16)
    out = pltpu.make_async_copy(bundle, bundle_hbm, sem.at[4])
    out.start()
    pltpu.make_async_copy(gagg, gagg_hbm, sem.at[1]).wait()
    for c in [*sent, put, out]:
        c.wait()


def total_kernel(scale, parts, mine_hbm, gbias, ggain, mine, sem):
    total = jnp.sum(parts[...].astype(F32), axis=0) * scale
    mine[...] = jnp.broadcast_to(total[8:][None], mine.shape).astype(BF16)
    put = pltpu.make_async_copy(mine, mine_hbm, sem.at[0])
    put.start()
    gbias[0:1] = total[0:1]
    ggain[0:1] = total[1:2]
    gbias[1:2] = total[2:3]
    ggain[1:2] = total[3:4]
    put.wait()


def final_kernel(
    nb, offs, near, far, acc_hbm, gagg_far, gagg_near, tiles_hbm, out_hbm,
    acc, gagg, tiles, halo, out, sem, tsem,
):
    blk = tiles.shape[2]
    per = nb // tsem.shape[0]
    get_a = pltpu.make_async_copy(acc_hbm, acc, sem.at[0])

    def get_t(it):
        some = pl.ds(it * per, per)
        return pltpu.make_async_copy(tiles_hbm.at[some], tiles.at[some], tsem.at[it])

    get_g = fetch_rims(gagg_near, gagg_far, gagg, sem.at[pl.ds(4, 2)])
    get_a.start()
    for it in range(nb // per):
        get_t(it).start()
    rims = fetch_rims(near, far, halo, sem.at[pl.ds(2, 2)])
    for c in get_g:
        c.wait()
    get_a.wait()

    def push(it, c):
        get_t(it).wait()
        for s in range(per):
            push_inner(it * per + s, gagg[it * per + s], acc, 0, tiles, offs, blk)
        return c

    lax.fori_loop(0, nb // per, push, 0)

    for c in rims:
        c.wait()

    def put(it):
        rows = pl.ds(it * per * blk, per * blk)
        return pltpu.make_async_copy(out.at[rows], out_hbm.at[rows], tsem.at[it])

    def step(it, c):
        for s in range(per):
            b = it * per + s
            out[pl.ds(b * blk, blk)] = jnp.transpose(acc[b] + halo[b].astype(F32))
        put(it).start()
        return c

    lax.fori_loop(0, nb // per, step, 0)
    for it in range(nb // per):
        put(it).wait()


def unpack_kernel(sums, out1_hbm, out2_hbm, out1, out2, sem):
    devices, share, _ = sums.shape
    _, upper, _ = out1.shape
    rows = upper + out2.shape[1]
    for p in range(devices):
        mine = sums[p].astype(F32)
        at = p * share
        while at < (p + 1) * share:
            layer, row = divmod(at, rows)
            end = min((p + 1) * share, layer * rows + (upper if row < upper else rows))
            piece = mine[at - p * share : end - p * share]
            if row < upper:
                out1[layer, row : row + end - at] = piece
            else:
                out2[layer, row - upper : row - upper + end - at] = piece
            at = end
    puts = [
        pltpu.make_async_copy(out1, out1_hbm, sem.at[0]),
        pltpu.make_async_copy(out2, out2_hbm, sem.at[1]),
    ]
    for p in puts:
        p.start()
    for p in puts:
        p.wait()


def call(body, args, outs, scratch=(), alias=None, far_args=(), any_args=(), flops=0, moved=0):
    args = [
        pltpu.with_memory_space_constraint(a, pltpu.HBM) if i in far_args else a
        for i, a in enumerate(args)
    ]
    return pl.pallas_call(
        body,
        in_specs=[
            HBM if i in far_args else ANY if i in any_args else SMEM if a.dtype == jnp.int32 else VMEM
            for i, a in enumerate(args)
        ],
        out_specs=[HBM if len(o) == 3 else VMEM for o in outs],
        out_shape=[
            pltpu.HBM(o[0], o[1]) if len(o) == 3 else jax.ShapeDtypeStruct(o[0], o[1]) for o in outs
        ],
        scratch_shapes=list(scratch),
        input_output_aliases=alias or {},
        compiler_params=pltpu.CompilerParams(vmem_limit_bytes=24 << 20),
        cost_estimate=pl.CostEstimate(flops=flops, bytes_accessed=moved, transcendentals=0),
    )(*args)


def dma(n):
    return pltpu.SemaphoreType.DMA((n,))


def per_device(feats, tile_vals, tile_offs, w_in, bias_in, w_out, gain, cot):
    nodes, width = feats.shape
    nb, slots, blk, _ = tile_vals.shape
    hid = w_out.shape[1]
    layers = w_in.shape[0]
    assert nb == 2 * HALO and width == blk and hid == width and layers == 2
    devices = lax.axis_size("band") * lax.axis_size("rep")
    block = (width, blk)
    full, _, ext = ((n, *block) for n in (nb, HALO, nb + 2 * HALO))
    whole = (2 * width + hid, hid)
    share = layers * whole[0] // devices
    assert share * devices == layers * whole[0]
    v = pltpu.VMEM
    part_of = functools.partial
    tile_flops = 2 * blk * blk * width
    mlp_flops = 2 * nodes * (2 * width * hid + hid * width)
    mib = 2 * nodes * width
    offs = tile_offs.T

    half = (HALO, *block)
    half_rows = (nodes // 2, width)

    h0, far = call(
        turn_kernel, (feats,), [(ext, BF16), (half, BF16)],
        [v(half_rows, BF16), dma(1)], far_args=(0,),
        flops=nb * tile_flops, moved=3 * mib,
    )
    far = swap(far, True)
    h0, near, part, w1t, w2t, w2, kept = call(
        part_of(inner0_kernel, nb), (offs, h0, feats, tile_vals, w_in, w_out),
        [(ext, BF16), (half, BF16), (full, F32), ((layers, hid, 2 * width), BF16), ((layers, width, hid), BF16),
         (w_out.shape, BF16), (full, BF16, True)],
        [v(half_rows, BF16), v(tile_vals.shape, BF16), v(w_in.shape, BF16), v(w_out.shape, BF16), dma(4), dma(8)],
        {1: 0}, far_args=(2, 3, 4, 5),
        flops=2 * nb * tile_flops, moved=6 * mib,
    )
    near = swap(near, False)

    def node0(is_far, rim, h, more):
        return call(
            part_of(node0_kernel, nb, is_far),
            (offs, rim, h, part, tile_vals, w1t, w2t, bias_in, gain, *more),
            [(half, BF16), (ext, BF16), (ext, BF16), *[(half, BF16)] * 4, ((HALO, 1, blk), F32)],
            [v(block, F32), v(block, F32)], {2: 1} if is_far else {2: 1, 9: 2},
            flops=(nb * tile_flops + mlp_flops) // 2, moved=6 * mib,
        )

    far, h0, h1, *saved_far = node0(True, far, h0, ())
    far = swap(far, True)
    near, h0, h1, *saved_near = node0(False, near, h0, (h1,))
    near = swap(near, False)
    part, cott = call(
        part_of(inner1_kernel, nb), (offs, h1, tile_vals, cot), [(full, F32), (full, BF16)],
        flops=2 * nb * tile_flops, moved=8 * mib,
    )

    def node1(is_far, rim, h, more):
        return call(
            part_of(node1_kernel, nb, is_far),
            (offs, rim, h, part, tile_vals, cott, w1t, w2t, w_in, w2, bias_in, gain, *more),
            [(half, BF16), (ext, BF16), *[(half, BF16)] * 6, (ext, F32), (block, F32), (block, F32)],
            [v(block, F32), v(block, F32)], {2: 1} if is_far else {2: 1, 12: 8, 13: 9, 14: 10},
            flops=nb * tile_flops + mlp_flops, moved=8 * mib,
        )

    far, h1, *made_far, acc, gb1, gg1 = node1(True, far, h1, ())
    far = swap(far, True)
    near, h1, *made_near, acc, gb1, gg1 = node1(False, near, h1, (acc, gb1, gg1))
    near = swap(near, False)
    acc, gw1, gv1, h2 = call(
        weights_kernel, (offs, acc, tile_vals, h1, gb1, gg1, *made_far, *made_near),
        [(ext, F32), (whole, F32), ((2, hid), F32), (full, BF16, True)],
        [dma(2)], {1: 0},
        flops=tile_flops, moved=mib,
    )

    def node2(is_far, rim, acc, saved, more, outs, scratch, alias):
        return call(
            part_of(node2_kernel, nb, is_far),
            (offs, rim, acc, tile_vals, w_in, w2, gain, kept, *saved, *more), outs, scratch, alias,
            flops=nb * tile_flops + mlp_flops, moved=8 * mib,
        )

    sums = [(ext, F32), (block, F32), (block, F32), (whole, F32)]
    work = [v(half, BF16), v(half, BF16), v(half, BF16), v(block, F32)]
    *state, gagg_near, near = node2(
        False, near, acc, saved_near, (), [*sums, (half, BF16, True), (half, BF16)], [*work, dma(2)], {}
    )
    near, far, bundle, gagg_far, acc, *_ = node2(
        True, far, acc, saved_far, (near, gw1, gv1, *state),
        [(half, BF16, True), (half, BF16, True), ((devices, 8 + share, hid), BF16, True), (half, BF16, True), (full, F32, True), *sums],
        [*work, v(half, BF16), v((devices, 8 + share, hid), BF16), dma(5)],
        {16 + i: 5 + i for i in range(4)},
    )

    parts = lax.all_to_all(bundle, AXES, 0, 0, tiled=True)
    near, far = swap(near, False), swap(far, True)
    (out_feats,) = call(
        part_of(output_kernel, nb), (h2,), [((nodes, width), BF16, True)],
        [v(full, BF16), v((nodes, width), BF16), dma(4)], far_args=(0,),
        flops=nb * tile_flops, moved=2 * mib,
    )
    mine, grad_bias, grad_gain = call(
        part_of(total_kernel, 1.0 / math.sqrt(nodes * devices)), (parts,),
        [((devices, share, hid), BF16, True), ((layers, hid), F32), ((layers, width), F32)],
        [v((devices, share, hid), BF16), dma(1)],
        flops=nodes * width, moved=mib,
    )
    sums = lax.all_to_all(mine, AXES, 0, 0, tiled=True)
    (grad_feats,) = call(
        part_of(final_kernel, nb), (offs, near, far, acc, gagg_far, gagg_near, tile_vals),
        [((nodes, width), F32, True)],
        [v(full, F32), v(full, BF16), v((nb, slots, blk, blk), BF16), v(full, BF16), v((nodes, width), F32), dma(6), dma(8)],
        far_args=(3, 4, 5, 6), any_args=(1, 2),
        flops=2 * nb * tile_flops, moved=9 * mib,
    )
    grad_w_in, grad_w_out = call(
        unpack_kernel, (sums,),
        [((layers, 2 * width, hid), F32, True), ((layers, hid, width), F32, True)],
        [v((layers, 2 * width, hid), F32), v((layers, hid, width), F32), dma(2)],
        flops=nodes * width, moved=mib,
    )
    return out_feats, grad_feats, grad_w_in, grad_bias, grad_w_out, grad_gain


def solution(mesh):
    placed = (
        P(AXES, None),
        P(AXES, None, None, None),
        P(AXES, None),
        P(),
        P(),
        P(),
        P(),
        P(AXES, None),
    )
    return jax.shard_map(
        per_device,
        mesh=mesh,
        in_specs=placed,
        out_specs=(P(AXES, None), P(AXES, None), P(), P(), P(), P()),
        check_vma=False,
    )
```

time: 101 us -> 97.7 us (0.967)
  waiting for transfers between devices: 31.7 us -> 21.9 us
  Pallas kernels: 42.3 us -> 48.5 us
  starting transfers between devices: 21.3 us -> 25.2 us
  local copies, waits for them, and re-layouts: 4.34 us -> 0.71 us
    ppermute x8, waiting for transfers between devices: 20.5 us -> 12.7 us  [swap(): return lax.ppermute(x, AXES, pairs)]
    pallas_call x10 -> x14, Pallas kernels: 42.3 us -> 48.5 us  [call(): pl.pallas_call(body, in_specs=[HBM if i in far_args else ANY if i in any_...]
    ppermute x8, starting transfers between devices: 8.33 us -> 12.3 us  [swap(): return lax.ppermute(x, AXES, pairs)]
    unnamed x22 -> x16, local copies, waits for them, and re-layouts: 4.34 us -> 0.71 us
    all_to_all x1, waiting for transfers between devices: 2.01 us -> 0.01 us  [per_device(): sums = lax.all_to_all(mine, AXES, 0, 0, tiled=True)]
  transfers between devices with their start and end apart: 10 -> 10, of which waited for: 5 -> 4; matrix products, arithmetic and copies ran while one was open for 0% -> 0% of each run, Pallas kernels for 21% -> 39%
where the time goes in v3:
time: 97.7 us; the launch traced here: 97.1 us
  Pallas kernels  48.5 us (50%)
  starting transfers between devices  25.2 us (26%)
  waiting for transfers between devices  21.9 us (22%)
    pallas_call x14, Pallas kernels, call(): pl.pallas_call(body, in_specs=[HBM if i in far_args else ANY if i in any_...  48.5 us
    ppermute x8, waiting for transfers between devices, swap(): return lax.ppermute(x, AXES, pairs)  12.7 us
    ppermute x8, starting transfers between devices, swap(): return lax.ppermute(x, AXES, pairs)  12.3 us
    all_to_all x1, waiting for transfers between devices, per_device(): parts = lax.all_to_all(bundle, AXES, 0, 0, tiled=True)  9.19 us
    all_to_all x1, starting transfers between devices, per_device(): sums = lax.all_to_all(mine, AXES, 0, 0, tiled=True)  6.74 us
    all_to_all x1, starting transfers between devices, per_device(): parts = lax.all_to_all(bundle, AXES, 0, 0, tiled=True)  6.23 us
  transfers between devices with their start and end apart: 10, of which 4 were waited for; matrix products, arithmetic and copies ran while one was open for 0% of the time, Pallas kernels for 39%

profile of v3, /device:TPU:1, one launch (start us, length us, event | category | flops | bytes accessed | tf_op | source)
XLA Modules:
  0.0 97.1 jit_solution(4150432222304316027)
XLA Ops:
  0.6 1.7 %shard_map.127 = (bf16[64,128,128]{2,1,0:T(8,128)(2,1)S(1)}, bf16[16,128,128]{2,1,0:T(8,128)(2,1)S(1)}) custom-call(bf16[4096,128]{1,0:T(8,128)(2,1)} %x_hbm.3), custom_call_target="tpu_custom_call" | custom-call | flops 134217728 | bytes 3145728 | tf_op jit(solution)/shard_map/pallas_call | solution.py:579
  2.3 2.7 %collective-permute-start.1 = (bf16[16,128,128]{2,1,0:T(8,128)(2,1)S(1)}, bf16[16,128,128]{2,1,0:T(8,128)(2,1)S(1)}, u32[]{:S(2)}, u32[]{:S(2)}) collective-permute-start(bf16[16,128,128]{2,1,0:T(8,128)(2,1)S(1)} %get-tuple-element.76), channel_id=1, source_target_pairs={{1,2},{2,1},{3,4},{4,3},{5,6},{6,5},{7,8},{8,7},{9,10},{10,9},{11,... | collective-permute-start | bytes 1572872 | tf_op jit(solution)/shard_map/ppermute | solution.py:61
  5.0 0.7 copy-done.4
  5.7 5.5 %shard_map.128 = (bf16[64,128,128]{2,1,0:T(8,128)(2,1)S(1)}, bf16[16,128,128]{2,1,0:T(8,128)(2,1)S(1)}, f32[32,128,128]{2,1,0:T(8,128)S(1)}, bf16[2,128,256]{2,1...) custom-call(s32[3,32]{1,0:T(4,128)S(1)} %bitcast.1, ...), custom_call_target="tpu_custom_call", output_to_operand_aliasing={{0}: (1, {})} | custom-call | flops 268435456 | bytes 6291456 | tf_op jit(solution)/shard_map/pallas_call | solution.py:579
  11.2 3.9 %collective-permute-start = (bf16[16,128,128]{2,1,0:T(8,128)(2,1)S(1)}, bf16[16,128,128]{2,1,0:T(8,128)(2,1)S(1)}, u32[]{:S(2)}, u32[]{:S(2)}) collective-permute-start(bf16[16,128,128]{2,1,0:T(8,128)(2,1)S(1)} %get-tuple-element.75), channel_id=1, source_target_pairs={{0,1},{1,0},{2,3},{3,2},{4,5},{5,4},{6,7},{7,6},{8,9},{9,8},{10,11... | collective-permute-start | bytes 1572872 | tf_op jit(solution)/shard_map/ppermute | solution.py:61
  15.1 2.4 %collective-permute-done.1.rim = bf16[16,128,128]{2,1,0:T(8,128)(2,1)S(1)} collective-permute-done((bf16[16,128,128]{2,1,0:T(8,128)(2,1)S(1)}, bf16[16,128,128]{2,1,0:T(8,128)(2,1)S(1)}, u32[]{:S(2)}, u32[]{:S(2)}) %collective-permute-start.1) | collective-permute-done | bytes 524320 | tf_op jit(solution)/shard_map/ppermute | solution.py:61
  17.5 2.2 %shard_map.129 = (bf16[16,128,128]{2,1,0:T(8,128)(2,1)S(1)}, bf16[64,128,128]{2,1,0:T(8,128)(2,1)S(1)}, bf16[64,128,128]{2,1,0:T(8,128)(2,1)S(1)}, bf16[16,128,1...) custom-call(s32[3,32]{1,0:T(4,128)S(1)} %bitcast.2, ...), custom_call_target="tpu_custom_call", output_to_operand_aliasing={{1}: (2, {})} | custom-call | flops 268435456 | bytes 6291456 | tf_op jit(solution)/shard_map/pallas_call | solution.py:579
  19.8 1.8 %collective-permute-start.3 = (bf16[16,128,128]{2,1,0:T(8,128)(2,1)S(1)}, bf16[16,128,128]{2,1,0:T(8,128)(2,1)S(1)}, u32[]{:S(2)}, u32[]{:S(2)}) collective-permute-start(bf16[16,128,128]{2,1,0:T(8,128)(2,1)S(1)} %get-tuple-element.84), channel_id=1, source_target_pairs={{1,2},{2,1},{3,4},{4,3},{5,6},{6,5},{7,8},{8,7},{9,10},{10,9},{11,... | collective-permute-start | bytes 1572872 | tf_op jit(solution)/shard_map/ppermute | solution.py:61
  21.6 0.0 collective-permute-done.rim
  21.6 2.2 %shard_map.130 = (bf16[16,128,128]{2,1,0:T(8,128)(2,1)S(1)}, bf16[64,128,128]{2,1,0:T(8,128)(2,1)S(1)}, bf16[64,128,128]{2,1,0:T(8,128)(2,1)S(1)}, bf16[16,128,1...) custom-call(s32[3,32]{1,0:T(4,128)S(1)} %bitcast.3, ...), custom_call_target="tpu_custom_call", output_to_operand_aliasing={{1}: (2, {}), {2}: (9, {})} | custom-call | flops 268435456 | bytes 6291456 | tf_op jit(solution)/shard_map/pallas_call | solution.py:579
  23.8 2.0 %collective-permute-start.2 = (bf16[16,128,128]{2,1,0:T(8,128)(2,1)S(1)}, bf16[16,128,128]{2,1,0:T(8,128)(2,1)S(1)}, u32[]{:S(2)}, u32[]{:S(2)}) collective-permute-start(bf16[16,128,128]{2,1,0:T(8,128)(2,1)S(1)} %get-tuple-element.83), channel_id=1, source_target_pairs={{0,1},{1,0},{2,3},{3,2},{4,5},{5,4},{6,7},{7,6},{8,9},{9,8},{10,11... | collective-permute-start | bytes 1572872 | tf_op jit(solution)/shard_map/ppermute | solution.py:61
  25.8 4.1 %shard_map.131 = (f32[32,128,128]{2,1,0:T(8,128)S(1)}, bf16[32,128,128]{2,1,0:T(8,128)(2,1)S(1)}) custom-call(s32[3,32]{1,0:T(4,128)S(1)} %bitcast.4, bf16[64,128,128]{2,1,0:T(8,128)(2,1)S(1)} %get-tuple-element.85.ext.ext_in, bf16[32,3,128,128]{3,2,1,0:T(8,128)(2,1)S(1)} %copy-done, bf16[4096,128]{1,0:T(8,128)(2,1)S(1)} %copy-done.3), custom_call_target="tpu_custom_call" | custom-call | flops 268435456 | bytes 8388608 | tf_op jit(solution)/shard_map/pallas_call | solution.py:579
  29.9 4.1 %collective-permute-done.3.rim = bf16[16,128,128]{2,1,0:T(8,128)(2,1)S(1)} collective-permute-done((bf16[16,128,128]{2,1,0:T(8,128)(2,1)S(1)}, bf16[16,128,128]{2,1,0:T(8,128)(2,1)S(1)}, u32[]{:S(2)}, u32[]{:S(2)}) %collective-permute-start.3) | collective-permute-done | bytes 524320 | tf_op jit(solution)/shard_map/ppermute | solution.py:61
  34.0 4.1 %shard_map.132 = (bf16[16,128,128]{2,1,0:T(8,128)(2,1)S(1)}, bf16[64,128,128]{2,1,0:T(8,128)(2,1)S(1)}, bf16[16,128,128]{2,1,0:T(8,128)(2,1)S(1)}, bf16[16,128,1...) custom-call(s32[3,32]{1,0:T(4,128)S(1)} %bitcast.5, ...), custom_call_target="tpu_custom_call", output_to_operand_aliasing={{1}: (2, {})} | custom-call | flops 536870912 | bytes 8388608 | tf_op jit(solution)/shard_map/pallas_call | solution.py:579
  38.1 0.0 collective-permute-done.2.rim
  38.1 3.8 %shard_map.133 = (bf16[16,128,128]{2,1,0:T(8,128)(2,1)S(1)}, bf16[64,128,128]{2,1,0:T(8,128)(2,1)S(1)}, bf16[16,128,128]{2,1,0:T(8,128)(2,1)S(1)}, bf16[16,128,1...) custom-call(s32[3,32]{1,0:T(4,128)S(1)} %bitcast.6, ...), custom_call_target="tpu_custom_call", output_to_operand_aliasing={{1}: (2, {}), {8}: (12, {}), {9}: (13, {}), {10}: (14, {})} | custom-call | flops 536870912 | bytes 8388608 | tf_op jit(solution)/shard_map/pallas_call | solution.py:579
  41.9 0.1 collective-permute-start.5
  42.0 0.1 collective-permute-start.4
  42.0 0.0 copy-start.1
  42.1 4.1 %shard_map.134 = (f32[64,128,128]{2,1,0:T(8,128)S(1)}, f32[384,128]{1,0:T(8,128)S(1)}, f32[2,128]{1,0:T(2,128)S(1)}, bf16[32,128,128]{2,1,0:T(8,128)(2,1)}) custom-call(s32[3,32]{1,0:T(4,128)S(1)} %bitcast.7, f32[64,128,128]{2,1,0:T(8,128)S(1)} %get-tuple-element.93.acc_in, bf16[32,3,128,128]{3,2,1,0:T(8,128)(2,1)S(1)} %copy-done, ...), custom_call_target="tpu_custom_call", output_to_operand_aliasing={{0}: (1, {})} | custom-call | flops 4194304 | bytes 1048576 | tf_op jit(solution)/shard_map/pallas_call | solution.py:579
  46.2 3.8 %shard_map.136 = (f32[64,128,128]{2,1,0:T(8,128)S(1)}, f32[128,128]{1,0:T(8,128)S(1)}, f32[128,128]{1,0:T(8,128)S(1)}, f32[384,128]{1,0:T(8,128)S(1)}, bf16[16,1...) custom-call(s32[3,32]{1,0:T(4,128)S(1)} %bitcast.8, bf16[16,128,128]{2,1,0:T(8,128)(2,1)S(1)} %collective-permute-done.5.rim, ...), custom_call_target="tpu_custom_call" | custom-call | flops 536870912 | bytes 8388608 | tf_op jit(solution)/shard_map/pallas_call | solution.py:579
  50.1 6.2 %collective-permute-done.4.rim = bf16[16,128,128]{2,1,0:T(8,128)(2,1)S(1)} collective-permute-done((bf16[16,128,128]{2,1,0:T(8,128)(2,1)S(1)}, bf16[16,128,128]{2,1,0:T(8,128)(2,1)S(1)}, u32[]{:S(2)}, u32[]{:S(2)}) %collective-permute-start.4) | collective-permute-done | bytes 524320 | tf_op jit(solution)/shard_map/ppermute | solution.py:61
  56.3 4.6 %shard_map.137 = (bf16[16,128,128]{2,1,0:T(8,128)(2,1)}, bf16[16,128,128]{2,1,0:T(8,128)(2,1)}, bf16[32,32,128]{2,1,0:T(8,128)(2,1)}, bf16[16,128,128]{2,1,0:T(8...) custom-call(s32[3,32]{1,0:T(4,128)S(1)} %bitcast.9, ...), custom_call_target="tpu_custom_call", output_to_operand_aliasing={{5}: (16, {}), {6}: (17, {}), {7}: (18, {}), {8}: (19, {})} | custom-call | flops 536870912 | bytes 8388608 | tf_op jit(solution)/shard_map/pallas_call | solution.py:579
  60.9 6.2 %all-to-all-start = ((bf16[32,32,128]{2,1,0:T(8,128)(2,1)}), bf16[32,32,128]{2,1,0:T(8,128)(2,1)S(1)}, u32[]{:S(2)}, u32[]{:S(2)}) async-start(bf16[32,32,128]{2,1,0:T(8,128)(2,1)} %get-tuple-element.136), calls=%async_computation | async-start | bytes 524288 | tf_op jit(solution)/shard_map/all_to_all | solution.py:695
  67.1 0.3 collective-permute-start.6
  67.5 1.5 %collective-permute-start.7 = (bf16[16,128,128]{2,1,0:T(8,128)(2,1)}, bf16[16,128,128]{2,1,0:T(8,128)(2,1)S(1)}, u32[]{:S(2)}, u32[]{:S(2)}) collective-permute-start(bf16[16,128,128]{2,1,0:T(8,128)(2,1)} %get-tuple-element.132), channel_id=1, source_target_pairs={{1,2},{2,1},{3,4},{4,3},{5,6},{6,5},{7,8},{8,7},{9,10},{10,9},{11,... | collective-permute-start | bytes 1572872 | tf_op jit(solution)/shard_map/ppermute | solution.py:61
  69.0 9.2 %all-to-all-done.parts = bf16[32,32,128]{2,1,0:T(8,128)(2,1)S(1)} async-done(((bf16[32,32,128]{2,1,0:T(8,128)(2,1)}), bf16[32,32,128]{2,1,0:T(8,128)(2,1)S(1)}, u32[]{:S(2)}, u32[]{:S(2)}) %all-to-all-start) | async-done | bytes 262176 | tf_op jit(solution)/shard_map/all_to_all | solution.py:695
  78.1 1.3 %shard_map.139 = (bf16[32,24,128]{2,1,0:T(8,128)(2,1)}, f32[2,128]{1,0:T(2,128)}, f32[2,128]{1,0:T(2,128)}) custom-call(bf16[32,32,128]{2,1,0:T(8,128)(2,1)S(1)} %all-to-all-done.parts), custom_call_target="tpu_custom_call" | custom-call | flops 524288 | bytes 1048576 | tf_op jit(solution)/shard_map/pallas_call | solution.py:579
  79.5 6.7 %all-to-all-start.1 = ((bf16[32,24,128]{2,1,0:T(8,128)(2,1)}), bf16[32,24,128]{2,1,0:T(8,128)(2,1)S(1)}, u32[]{:S(2)}, u32[]{:S(2)}) async-start(bf16[32,24,128]{2,1,0:T(8,128)(2,1)} %get-tuple-element.137), calls=%async_computation.1 | async-start | bytes 393216 | tf_op jit(solution)/shard_map/all_to_all | solution.py:708
  86.2 2.9 %shard_map.135 = bf16[4096,128]{1,0:T(8,128)(2,1)} custom-call(bf16[32,128,128]{2,1,0:T(8,128)(2,1)} %get-tuple-element.109.h_hbm), custom_call_target="tpu_custom_call" | custom-call | flops 134217728 | bytes 2097152 | tf_op jit(solution)/shard_map/pallas_call | solution.py:579
  89.2 7.2 %shard_map.138 = f32[4096,128]{1,0:T(8,128)} custom-call(s32[3,32]{1,0:T(4,128)S(1)} %bitcast.10, bf16[16,128,128]{2,1,0:T(8,128)(2,1)S(1)} %collective-permute-done.6.near, bf16[16,128,128]{2,1,0:T(8,128)(2,1)S(1)} %collective-permute-done.7.far, f32[32,128,128]{2,1,0:T(8,128)} %get-tuple-element.133.acc_hbm, ...), custom_call_target="tpu_custom_call" | custom-call | flops 268435456 | bytes 9437184 | tf_op jit(solution)/shard_map/pallas_call | solution.py:579
  96.4 0.8 shard_map.140
  (18 shorter events, 0.0 us)
Async XLA Ops:
  2.3 15.2 %collective-permute-start.1 = (bf16[16,128,128]{2,1,0:T(8,128)(2,1)S(1)}, bf16[16,128,128]{2,1,0:T(8,128)(2,1)S(1)}, u32[]{:S(2)}, u32[]{:S(2)}) collective-permute-start(bf16[16,128,128]{2,1,0:T(8,128)(2,1)S(1)} %get-tuple-element.76), channel_id=1, source_target_pairs={{1,2},{2,1},{3,4},{4,3},{5,6},{6,5},{7,8},{8,7},{9,10},{10,9},{11,... | collective-permute-start | bytes 1572872 | tf_op jit(solution)/shard_map/ppermute | solution.py:61
  5.0 0.7 copy-start.4
  5.7 11.8 %copy-start = (bf16[32,3,128,128]{3,2,1,0:T(8,128)(2,1)S(1)}, bf16[32,3,128,128]{3,2,1,0:T(8,128)(2,1)}, u32[]{:S(2)}) copy-start(bf16[32,3,128,128]{3,2,1,0:T(8,128)(2,1)} %tiles_hbm.3) | copy-start | bytes 9437188
  5.7 11.8 %copy-start.6 = (f32[2,128]{1,0:T(2,128)S(1)}, f32[2,128]{1,0:T(2,128)}, u32[]{:S(2)}) copy-start(f32[2,128]{1,0:T(2,128)} %gain.11) | copy-start | bytes 3076
  5.7 11.8 %copy-start.7 = (f32[2,128]{1,0:T(2,128)S(1)}, f32[2,128]{1,0:T(2,128)}, u32[]{:S(2)}) copy-start(f32[2,128]{1,0:T(2,128)} %bias.7) | copy-start | bytes 3076
  11.2 10.3 %collective-permute-start = (bf16[16,128,128]{2,1,0:T(8,128)(2,1)S(1)}, bf16[16,128,128]{2,1,0:T(8,128)(2,1)S(1)}, u32[]{:S(2)}, u32[]{:S(2)}) collective-permute-start(bf16[16,128,128]{2,1,0:T(8,128)(2,1)S(1)} %get-tuple-element.75), channel_id=1, source_target_pairs={{0,1},{1,0},{2,3},{3,2},{4,5},{5,4},{6,7},{7,6},{8,9},{9,8},{10,11... | collective-permute-start | bytes 1572872 | tf_op jit(solution)/shard_map/ppermute | solution.py:61
  19.8 14.3 %collective-permute-start.3 = (bf16[16,128,128]{2,1,0:T(8,128)(2,1)S(1)}, bf16[16,128,128]{2,1,0:T(8,128)(2,1)S(1)}, u32[]{:S(2)}, u32[]{:S(2)}) collective-permute-start(bf16[16,128,128]{2,1,0:T(8,128)(2,1)S(1)} %get-tuple-element.84), channel_id=1, source_target_pairs={{1,2},{2,1},{3,4},{4,3},{5,6},{6,5},{7,8},{8,7},{9,10},{10,9},{11,... | collective-permute-start | bytes 1572872 | tf_op jit(solution)/shard_map/ppermute | solution.py:61
  21.6 4.2 %copy-start.3 = (bf16[4096,128]{1,0:T(8,128)(2,1)S(1)}, bf16[4096,128]{1,0:T(8,128)(2,1)}, u32[]{:S(2)}) copy-start(bf16[4096,128]{1,0:T(8,128)(2,1)} %cot.1) | copy-start | bytes 3145732
  21.6 4.2 %copy-start.5 = (s32[32,3]{0,1:T(4,128)S(1)}, s32[32,3]{0,1:T(4,128)}, u32[]{:S(2)}) copy-start(s32[32,3]{0,1:T(4,128)} %param.10) | copy-start | bytes 1156
  23.8 14.3 %collective-permute-start.2 = (bf16[16,128,128]{2,1,0:T(8,128)(2,1)S(1)}, bf16[16,128,128]{2,1,0:T(8,128)(2,1)S(1)}, u32[]{:S(2)}, u32[]{:S(2)}) collective-permute-start(bf16[16,128,128]{2,1,0:T(8,128)(2,1)S(1)} %get-tuple-element.83), channel_id=1, source_target_pairs={{0,1},{1,0},{2,3},{3,2},{4,5},{5,4},{6,7},{7,6},{8,9},{9,8},{10,11... | collective-permute-start | bytes 1572872 | tf_op jit(solution)/shard_map/ppermute | solution.py:61
  25.8 8.3 %copy-start.2 = (bf16[2,256,128]{2,1,0:T(8,128)(2,1)S(1)}, bf16[2,256,128]{2,1,0:T(8,128)(2,1)}, u32[]{:S(2)}) copy-start(bf16[2,256,128]{2,1,0:T(8,128)(2,1)} %w_in.7) | copy-start | bytes 393220
  41.9 4.3 %collective-permute-start.5 = (bf16[16,128,128]{2,1,0:T(8,128)(2,1)S(1)}, bf16[16,128,128]{2,1,0:T(8,128)(2,1)S(1)}, u32[]{:S(2)}, u32[]{:S(2)}) collective-permute-start(bf16[16,128,128]{2,1,0:T(8,128)(2,1)S(1)} %get-tuple-element.118), channel_id=1, source_target_pairs={{0,1},{1,0},{2,3},{3,2},{4,5},{5,4},{6,7},{7,6},{8,9},{9,8},{10,11... | collective-permute-start | bytes 1572872 | tf_op jit(solution)/shard_map/ppermute | solution.py:61
  42.0 14.3 %collective-permute-start.4 = (bf16[16,128,128]{2,1,0:T(8,128)(2,1)S(1)}, bf16[16,128,128]{2,1,0:T(8,128)(2,1)S(1)}, u32[]{:S(2)}, u32[]{:S(2)}) collective-permute-start(bf16[16,128,128]{2,1,0:T(8,128)(2,1)S(1)} %get-tuple-element.110), channel_id=1, source_target_pairs={{1,2},{2,1},{3,4},{4,3},{5,6},{6,5},{7,8},{8,7},{9,10},{10,9},{11,... | collective-permute-start | bytes 1572872 | tf_op jit(solution)/shard_map/ppermute | solution.py:61
  42.0 4.2 %copy-start.1 = (bf16[32,128,128]{2,1,0:T(8,128)(2,1)S(1)}, bf16[32,128,128]{2,1,0:T(8,128)(2,1)}, u32[]{:S(2)}) copy-start(bf16[32,128,128]{2,1,0:T(8,128)(2,1)} %get-tuple-element.112.kept) | copy-start | bytes 3145732
  60.9 17.2 %all-to-all-start = ((bf16[32,32,128]{2,1,0:T(8,128)(2,1)}), bf16[32,32,128]{2,1,0:T(8,128)(2,1)S(1)}, u32[]{:S(2)}, u32[]{:S(2)}) async-start(bf16[32,32,128]{2,1,0:T(8,128)(2,1)} %get-tuple-element.136), calls=%async_computation | async-start | bytes 524288 | tf_op jit(solution)/shard_map/all_to_all | solution.py:695
  67.1 22.0 %collective-permute-start.6 = (bf16[16,128,128]{2,1,0:T(8,128)(2,1)}, bf16[16,128,128]{2,1,0:T(8,128)(2,1)S(1)}, u32[]{:S(2)}, u32[]{:S(2)}) collective-permute-start(bf16[16,128,128]{2,1,0:T(8,128)(2,1)} %get-tuple-element.131), channel_id=1, source_target_pairs={{0,1},{1,0},{2,3},{3,2},{4,5},{5,4},{6,7},{7,6},{8,9},{9,8},{10,11... | collective-permute-start | bytes 1572872 | tf_op jit(solution)/shard_map/ppermute | solution.py:61
  67.5 21.7 %collective-permute-start.7 = (bf16[16,128,128]{2,1,0:T(8,128)(2,1)}, bf16[16,128,128]{2,1,0:T(8,128)(2,1)S(1)}, u32[]{:S(2)}, u32[]{:S(2)}) collective-permute-start(bf16[16,128,128]{2,1,0:T(8,128)(2,1)} %get-tuple-element.132), channel_id=1, source_target_pairs={{1,2},{2,1},{3,4},{4,3},{5,6},{6,5},{7,8},{8,7},{9,10},{10,9},{11,... | collective-permute-start | bytes 1572872 | tf_op jit(solution)/shard_map/ppermute | solution.py:61
  79.5 16.9 %all-to-all-start.1 = ((bf16[32,24,128]{2,1,0:T(8,128)(2,1)}), bf16[32,24,128]{2,1,0:T(8,128)(2,1)S(1)}, u32[]{:S(2)}, u32[]{:S(2)}) async-start(bf16[32,24,128]{2,1,0:T(8,128)(2,1)} %get-tuple-element.137), calls=%async_computation.1 | async-start | bytes 393216 | tf_op jit(solution)/shard_map/all_to_all | solution.py:708

commit v4 on v3

--- a/solution.py
+++ b/solution.py
@@ -14,7 +14,8 @@
 AXES = ("band", "rep")
 F32 = jnp.float32
 BF16 = jnp.bfloat16
-CH = 8
+OUTER = 8
+CH = 4
 HBM = pl.BlockSpec(memory_space=pltpu.HBM)
 ANY = pl.BlockSpec(memory_space=pl.ANY)
 SMEM = pl.BlockSpec(memory_space=pltpu.SMEM)
@@ -71,6 +72,14 @@
     return (odd if far else 1 - odd) * HALO
 
 
+def pipelined(count, *stages):
+    held = {}
+    for t in range(count + len(stages) - 1):
+        for i, stage in enumerate(stages):
+            if 0 <= t - i < count:
+                held[t - i] = stage(t - i, *held.get(t - i, ()))
+
+
 def for_blocks(count, body, per=4):
     def step(it, c):
         for s in range(per):
@@ -100,11 +109,27 @@
 
 def turn_kernel(x_hbm, ext, far, x, sem):
     base = rows_at(True)
-    get = half_of(x_hbm, x, base, sem.at[0])
-    get.start()
-    one = eye(ext.shape[2])
-    get.wait()
-    turn_rows(x, ext, far, base, one)
+    blk = ext.shape[2]
+    pieces = sem.shape[0]
+    per = HALO // pieces
+
+    def get(i):
+        rows = per * blk
+        return pltpu.make_async_copy(
+            x_hbm.at[pl.ds(pl.multiple_of((base + i * per) * blk, rows), rows)],
+            x.at[pl.ds(i * rows, rows)],
+            sem.at[i],
+        )
+
+    for i in range(pieces):
+        get(i).start()
+    one = eye(blk)
+    for i in range(pieces):
+        get(i).wait()
+        for b in range(i * per, (i + 1) * per):
+            block = nt(one, x[b * blk : (b + 1) * blk]).astype(BF16)
+            ext[HALO + base + b] = block
+            far[b] = block
 
 
 def fetch_rims(near_hbm, far_hbm, rims, sem):
@@ -131,8 +156,8 @@
 
 
 def inner0_kernel(
-    nb, offs, ext_in, x_hbm, tiles_hbm, w_in_hbm, w_out_hbm,
-    ext, near, part, w1t, w2t, w2, kept, x, tiles, w_in, w_out, sem, tsem,
+    nb, offs, ext_in, x_hbm, tiles_hbm, w_in_hbm, w_out_hbm, bias, gain,
+    ext, near, part, w1t, w2t, w2, bcols, gcols, kept, x, tiles, w_in, w_out, sem, tsem,
 ):
     base = rows_at(False)
     per = nb // tsem.shape[0]
@@ -170,10 +195,12 @@
         w1t[layer] = (0.5 * nt(one, w_in[layer])).astype(BF16)
         w2t[layer] = nt(one, w_out[layer]).astype(BF16)
         w2[layer] = (0.5 * w_out[layer].astype(F32)).astype(BF16)
+        bcols[layer] = column(0.5 * bias[layer : layer + 1], bcols.shape[2])
+        gcols[layer] = column(gain[layer : layer + 1], gcols.shape[2])
     keep.wait()
 
 
-def inner1_kernel(nb, offs, ext, tiles, cot, part, cott):
+def inner1_kernel(nb, offs, ext, tiles, cot, part, cott, acc1, acc0):
     for_blocks(nb, lambda b: inner_tile(b, ext, tiles, offs, part))
     blk = tiles.shape[2]
     one = eye(blk)
@@ -182,34 +209,42 @@
         cott[b] = nt(one, cot[pl.ds(b * blk, blk)]).astype(BF16)
 
     for_blocks(nb, turn)
+    clear(acc1)
+    clear(acc0)
 
 
 def edge_slot(b):
     return jnp.where(b < HALO, 1, 2)
 
 
-def forward_step(blocks, ext, part, tiles, offs, w1t, w2t, bias, gain):
+def join_step(blocks, ext, part, tiles, offs, w1t, bias):
     agg = []
     for b in blocks:
         slot = edge_slot(b)
         agg.append((part[b] + nt(ext[HALO + b + offs[slot, b]], tiles[b, slot])).astype(BF16))
     agg = lanes(agg)
     feats = lanes([ext[HALO + b] for b in blocks])
-    joined = jnp.concatenate([feats, agg], axis=0)
-    half = nn(w1t, joined) + widen(bias[...], CH)
+    half = nn(w1t, jnp.concatenate([feats, agg], axis=0)) + widen(bias[...], CH)
+    return feats, agg, half
+
+
+def mix_step(half, w2t):
     t = jnp.tanh(half)
     up = 1.0 + t
     act = (half * up).astype(BF16)
     slope = up * (1.0 + half * (1.0 - t))
-    mix = nn(w2t, act)
+    return act, slope, nn(w2t, act)
+
+
+def norm_step(feats, mix, gain):
     centred = mix - jnp.mean(mix, axis=0, keepdims=True)
     inv = lax.rsqrt(jnp.mean(centred * centred, axis=0, keepdims=True) + EPS)
     xhat = centred * inv
     after = (feats.astype(F32) + xhat * widen(gain[...], CH)).astype(BF16)
-    return agg, act, slope, xhat, inv, after
-
-
-def backward_step(grad, xhat, inv, slope, w1, w2, gain):
+    return xhat, inv, after
+
+
+def unmix_step(grad, xhat, inv, w2, gain):
     wide = widen(gain[...], CH)
     prod = grad * xhat
     gx = grad * wide
@@ -217,11 +252,19 @@
         gx - jnp.mean(gx, axis=0, keepdims=True) - xhat * jnp.mean(prod * wide, axis=0, keepdims=True)
     )
     gmix = gmix.astype(BF16)
-    gpre = nn(w2, gmix) * slope
+    return prod, gmix, nn(w2, gmix)
+
+
+def unjoin_step(gact, slope, w1):
+    gpre = gact * slope
     gpre_b = gpre.astype(BF16)
     gcat = nn(w1, gpre_b)
-    width = grad.shape[0]
-    return prod, gmix, gpre, gpre_b, gcat[:width], gcat[width:].astype(BF16)
+    width = gact.shape[0]
+    return gpre, gpre_b, gcat[:width], gcat[width:].astype(BF16)
+
+
+def chunk(base, it):
+    return [base + it * CH + s for s in range(CH)]
 
 
 def cut(wide, s, blk):
@@ -256,74 +299,81 @@
 
 
 def node0_kernel(
-    nb, is_far, offs, rim, ext_in, part, tiles, w1t, w2t, bias, gain, *refs
+    nb, is_far, offs, rim, ext_in, part, tiles, w1t, w2t, bcols, gcols, *refs
 ):
-    rim_out, ext, after_ext, agg, act, slope, xhat, inv, bcol, gcol = refs if is_far else refs[1:]
+    rim_out, ext, after_ext, agg, act, slope, xhat, inv = refs if is_far else refs[1:]
+    bcol, gcol = bcols.at[0], gcols.at[0]
     blk = tiles.shape[2]
-    bcol[...] = column(0.5 * bias[0:1], blk)
-    gcol[...] = column(gain[0:1], blk)
     take_rim(rim, ext, rim_at(nb, is_far))
     base = rows_at(is_far)
 
-    def step(it, c):
-        local = [it * CH + s for s in range(CH)]
-        agg_w, act_w, slope_w, xhat_w, inv_w, after = forward_step(
-            [base + b for b in local], ext, part, tiles, offs, w1t[0], w2t[0], bcol, gcol
-        )
-        slope_w = slope_w.astype(BF16)
-        xhat_b = xhat_w.astype(BF16)
-        for s, b in enumerate(local):
+    def join(it):
+        return join_step(chunk(base, it), ext, part, tiles, offs, w1t[0], bcol)
+
+    def mixing(it, feats, agg_w, half):
+        for s, b in enumerate(chunk(0, it)):
             agg[b] = cut(agg_w, s, blk)
+        return feats, *mix_step(half, w2t[0])
+
+    def norm(it, feats, act_w, slope_w, mix):
+        xhat_w, inv_w, after = norm_step(feats, mix, gcol)
+        slope_w, xhat_w = slope_w.astype(BF16), xhat_w.astype(BF16)
+        for s, b in enumerate(chunk(0, it)):
             act[b] = cut(act_w, s, blk)
             slope[b] = cut(slope_w, s, blk)
-            xhat[b] = cut(xhat_b, s, blk)
+            xhat[b] = cut(xhat_w, s, blk)
             inv[b] = cut(inv_w, s, blk)
             after_ext[HALO + base + b] = cut(after, s, blk)
             rim_out[b] = cut(after, s, blk)
-        return c
-
-    lax.fori_loop(0, HALO // CH, step, 0)
+
+    pipelined(HALO // CH, join, mixing, norm)
 
 
 def node1_kernel(
-    nb, is_far, offs, rim, ext_in, part, tiles, cott, w1t, w2t, w_in, w2, bias, gain, *refs
+    nb, is_far, offs, rim, ext_in, part, tiles, cott, w1t, w2t, w_in, w2, bcols, gcols, *refs
 ):
-    rim_out, ext, h2, agg, act, gmix, gpre, gagg, acc, gb, gg, bcol, gcol = refs if is_far else refs[3:]
+    rim_out, ext, h2, agg, act, gmix, gpre, gagg, acc, gb, gg = refs[1:] if is_far else refs[3:]
+    bcol, gcol = bcols.at[1], gcols.at[1]
     blk = tiles.shape[2]
-    bcol[...] = column(0.5 * bias[1:2], blk)
-    gcol[...] = column(gain[1:2], blk)
     if is_far:
         gb[...] = jnp.zeros_like(gb)
         gg[...] = jnp.zeros_like(gg)
-        clear(acc)
     take_rim(rim, ext, rim_at(nb, is_far))
     base = rows_at(is_far)
 
-    def step(it, c):
-        local = [it * CH + s for s in range(CH)]
-        blocks = [base + b for b in local]
-        agg_w, act_w, slope, xhat, inv, after = forward_step(
-            blocks, ext, part, tiles, offs, w1t[1], w2t[1], bcol, gcol
-        )
-        grad = lanes([cott[b] for b in blocks]).astype(F32)
-        prod, gmix_w, gpre_f, gpre_w, gh, gagg_w = backward_step(
-            grad, xhat, inv, slope, w_in[1], w2[1], gcol
-        )
+    def join(it):
+        return join_step(chunk(base, it), ext, part, tiles, offs, w1t[1], bcol)
+
+    def mixing(it, feats, agg_w, half):
+        for s, b in enumerate(chunk(0, it)):
+            agg[b] = cut(agg_w, s, blk)
+        return feats, *mix_step(half, w2t[1])
+
+    def turn(it, feats, act_w, slope, mix):
+        xhat, inv, after = norm_step(feats, mix, gcol)
+        grad = lanes([cott[b] for b in chunk(base, it)]).astype(F32)
+        prod, gmix_w, gact = unmix_step(grad, xhat, inv, w2[1], gcol)
         gg[...] += fold(prod, blk)
-        gb[...] += fold(gpre_f, blk)
-        rest = grad + gh
-        for s, b in enumerate(local):
-            agg[b] = cut(agg_w, s, blk)
+        for s, b in enumerate(chunk(0, it)):
             act[b] = cut(act_w, s, blk)
             h2[b] = cut(after, s, blk)
             gmix[b] = cut(gmix_w, s, blk)
+        return slope, gact
+
+    def unjoin(it, slope, gact):
+        gpre_f, gpre_w, gh, gagg_w = unjoin_step(gact, slope, w_in[1])
+        gb[...] += fold(gpre_f, blk)
+        grad = lanes([cott[b] for b in chunk(base, it)]).astype(F32)
+        return gpre_w, grad + gh, gagg_w
+
+    def push(it, gpre_w, rest, gagg_w):
+        for s, b in enumerate(chunk(0, it)):
             gpre[b] = cut(gpre_w, s, blk)
             gagg[b] = cut(gagg_w, s, blk)
             acc[HALO + base + b] += cut(rest, s, blk)
-        push_edge(blocks, gagg_w, acc, tiles, offs, blk)
-        return c
-
-    lax.fori_loop(0, HALO // CH, step, 0)
+        push_edge(chunk(base, it), gagg_w, acc, tiles, offs, blk)
+
+    pipelined(HALO // CH, join, mixing, turn, unjoin, push)
     at = rim_at(nb, is_far)
 
     def give(b):
@@ -361,11 +411,11 @@
         for_blocks(HALO, lambda b: push_inner(base + b, gagg[b], acc, HALO, tiles, offs, blk))
 
         def outer(it, c):
-            local = [it * CH + s for s in range(CH)]
+            local = [it * OUTER + s for s in range(OUTER)]
             outer_step(local, ext, HALO + base, agg, act, gmix, gpre, gw)
             return c
 
-        lax.fori_loop(0, HALO // CH, outer, 0)
+        lax.fori_loop(0, HALO // OUTER, outer, 0)
     for c in puts:
         c.wait()
 
@@ -399,70 +449,64 @@
         put(it).wait()
 
 
-def node2_kernel(nb, is_far, offs, rim, acc_in, tiles, w_in, w2, gain, kept, agg, act, slope, xhat, inv, *refs):
+def node2_kernel(nb, is_far, offs, rim, acc_in, tiles, w_in, w2, gcols, kept, agg, act, slope, xhat, inv, *refs):
     if is_far:
-        (near_in, gw1, gv1, *_, near_hbm, far_hbm, bundle_hbm, gagg_hbm, acc_hbm,
-         acc, gb, gg, gw, gagg, gmix, gpre, gcol, rims, bundle, sem) = refs
+        (gw1, gv1, *_, far_hbm, bundle_hbm, gagg_hbm, acc_hbm,
+         acc, gb, gg, gw, gagg, gmix, gpre, rims, bundle, sem) = refs
     else:
-        acc, gb, gg, gw, gagg_hbm, near_sum, gagg, gmix, gpre, gcol, sem = refs
-    blk = tiles.shape[2]
-    gcol[...] = column(gain[0:1], blk)
-    if is_far:
-        pass
-    else:
+        _, acc, gb, gg, gw, gagg_hbm, near_hbm, gagg, gmix, gpre, rims, sem = refs
         gb[...] = jnp.zeros_like(gb)
         gg[...] = jnp.zeros_like(gg)
         gw[...] = jnp.zeros_like(gw)
-        clear(acc)
+    blk = tiles.shape[2]
+    gcol = gcols.at[0]
     base = rows_at(is_far)
 
-    def step(it, c):
-        local = [it * CH + s for s in range(CH)]
-        blocks = [base + b for b in local]
+    def unmix(it):
+        local = chunk(0, it)
         grad = lanes([acc_in[HALO + base + b] + rim[b].astype(F32) for b in local])
         xhat_w = lanes([xhat[b] for b in local]).astype(F32)
-        slope_w = lanes([slope[b] for b in local]).astype(F32)
         inv_w = lanes([inv[b] for b in local])
-        prod, gmix_w, gpre_f, gpre_w, gh, gagg_w = backward_step(
-            grad, xhat_w, inv_w, slope_w, w_in[0], w2[0], gcol
-        )
+        prod, gmix_w, gact = unmix_step(grad, xhat_w, inv_w, w2[0], gcol)
         gg[...] += fold(prod, blk)
-        gb[...] += fold(gpre_f, blk)
-        rest = grad + gh
         for s, b in enumerate(local):
             gmix[b] = cut(gmix_w, s, blk)
+        return gact, grad
+
+    def unjoin(it, gact, grad):
+        slope_w = lanes([slope[b] for b in chunk(0, it)]).astype(F32)
+        gpre_f, gpre_w, gh, gagg_w = unjoin_step(gact, slope_w, w_in[0])
+        gb[...] += fold(gpre_f, blk)
+        return gpre_w, grad + gh, gagg_w
+
+    def push(it, gpre_w, rest, gagg_w):
+        for s, b in enumerate(chunk(0, it)):
             gpre[b] = cut(gpre_w, s, blk)
             gagg[b] = cut(gagg_w, s, blk)
             acc[HALO + base + b] += cut(rest, s, blk)
         some = pl.ds(it * CH, CH)
         pltpu.make_async_copy(gagg.at[some], gagg_hbm.at[some], sem.at[1]).start()
-        push_edge(blocks, gagg_w, acc, tiles, offs, blk)
-        outer_step(local, kept, base, agg, act, gmix, gpre, gw)
-        return c
-
-    lax.fori_loop(0, HALO // CH, step, 0)
+        push_edge(chunk(base, it), gagg_w, acc, tiles, offs, blk)
+        if (it + 1) * CH % OUTER == 0:
+            wide = list(range((it + 1) * CH - OUTER, (it + 1) * CH))
+            outer_step(wide, kept, base, agg, act, gmix, gpre, gw)
+
+    pipelined(HALO // CH, unmix, unjoin, push)
     at = rim_at(nb, is_far)
-    if not is_far:
-
-        def give(b):
-            near_sum[b] = acc[at + b].astype(BF16)
-
-        for_blocks(HALO, give, 8)
-        pltpu.make_async_copy(gagg, gagg_hbm, sem.at[1]).wait()
-        return
-    put = pltpu.make_async_copy(acc.at[pl.ds(HALO, nb)], acc_hbm, sem.at[0])
-    put.start()
 
     def rim_sum(b):
         rims[b] = acc[at + b].astype(BF16)
 
+    if is_far:
+        put = pltpu.make_async_copy(acc.at[pl.ds(HALO, nb)], acc_hbm, sem.at[0])
+        put.start()
     for_blocks(HALO, rim_sum, 8)
-    sent = [
-        pltpu.make_async_copy(rims, far_hbm, sem.at[2]),
-        pltpu.make_async_copy(near_in, near_hbm, sem.at[3]),
-    ]
-    for c in sent:
-        c.start()
+    sent = pltpu.make_async_copy(rims, far_hbm if is_far else near_hbm, sem.at[2])
+    sent.start()
+    if not is_far:
+        pltpu.make_async_copy(gagg, gagg_hbm, sem.at[1]).wait()
+        sent.wait()
+        return
     devices = bundle.shape[0]
     rows = gw.shape[0]
     share = 2 * rows // devices
@@ -478,10 +522,10 @@
         else:
             mine = jnp.concatenate([gw[first:rows], gw1[0 : first + share - rows]], axis=0)
         bundle[p, 8 : 8 + share] = mine.astype(BF16)
-    out = pltpu.make_async_copy(bundle, bundle_hbm, sem.at[4])
+    out = pltpu.make_async_copy(bundle, bundle_hbm, sem.at[3])
     out.start()
     pltpu.make_async_copy(gagg, gagg_hbm, sem.at[1]).wait()
-    for c in [*sent, put, out]:
+    for c in [sent, put, out]:
         c.wait()
 
 
@@ -621,14 +665,14 @@
 
     h0, far = call(
         turn_kernel, (feats,), [(ext, BF16), (half, BF16)],
-        [v(half_rows, BF16), dma(1)], far_args=(0,),
+        [v(half_rows, BF16), dma(4)], far_args=(0,),
         flops=nb * tile_flops, moved=3 * mib,
     )
     far = swap(far, True)
-    h0, near, part, w1t, w2t, w2, kept = call(
-        part_of(inner0_kernel, nb), (offs, h0, feats, tile_vals, w_in, w_out),
+    h0, near, part, w1t, w2t, w2, bcols, gcols, kept = call(
+        part_of(inner0_kernel, nb), (offs, h0, feats, tile_vals, w_in, w_out, bias_in, gain),
         [(ext, BF16), (half, BF16), (full, F32), ((layers, hid, 2 * width), BF16), ((layers, width, hid), BF16),
-         (w_out.shape, BF16), (full, BF16, True)],
+         (w_out.shape, BF16), ((layers, *block), F32), ((layers, *block), F32), (full, BF16, True)],
         [v(half_rows, BF16), v(tile_vals.shape, BF16), v(w_in.shape, BF16), v(w_out.shape, BF16), dma(4), dma(8)],
         {1: 0}, far_args=(2, 3, 4, 5),
         flops=2 * nb * tile_flops, moved=6 * mib,
@@ -638,9 +682,9 @@
     def node0(is_far, rim, h, more):
         return call(
             part_of(node0_kernel, nb, is_far),
-            (offs, rim, h, part, tile_vals, w1t, w2t, bias_in, gain, *more),
+            (offs, rim, h, part, tile_vals, w1t, w2t, bcols, gcols, *more),
             [(half, BF16), (ext, BF16), (ext, BF16), *[(half, BF16)] * 4, ((HALO, 1, blk), F32)],
-            [v(block, F32), v(block, F32)], {2: 1} if is_far else {2: 1, 9: 2},
+            alias={2: 1} if is_far else {2: 1, 9: 2},
             flops=(nb * tile_flops + mlp_flops) // 2, moved=6 * mib,
         )
 
@@ -648,21 +692,21 @@
     far = swap(far, True)
     near, h0, h1, *saved_near = node0(False, near, h0, (h1,))
     near = swap(near, False)
-    part, cott = call(
-        part_of(inner1_kernel, nb), (offs, h1, tile_vals, cot), [(full, F32), (full, BF16)],
+    part, cott, acc1, acc0 = call(
+        part_of(inner1_kernel, nb), (offs, h1, tile_vals, cot), [(full, F32), (full, BF16), (ext, F32), (ext, F32)],
         flops=2 * nb * tile_flops, moved=8 * mib,
     )
 
     def node1(is_far, rim, h, more):
         return call(
             part_of(node1_kernel, nb, is_far),
-            (offs, rim, h, part, tile_vals, cott, w1t, w2t, w_in, w2, bias_in, gain, *more),
+            (offs, rim, h, part, tile_vals, cott, w1t, w2t, w_in, w2, bcols, gcols, *more),
             [(half, BF16), (ext, BF16), *[(half, BF16)] * 6, (ext, F32), (block, F32), (block, F32)],
-            [v(block, F32), v(block, F32)], {2: 1} if is_far else {2: 1, 12: 8, 13: 9, 14: 10},
+            alias={2: 1, 12: 8} if is_far else {2: 1, 12: 8, 13: 9, 14: 10},
             flops=nb * tile_flops + mlp_flops, moved=8 * mib,
         )
 
-    far, h1, *made_far, acc, gb1, gg1 = node1(True, far, h1, ())
+    far, h1, *made_far, acc, gb1, gg1 = node1(True, far, h1, (acc1,))
     far = swap(far, True)
     near, h1, *made_near, acc, gb1, gg1 = node1(False, near, h1, (acc, gb1, gg1))
     near = swap(near, False)
@@ -676,20 +720,20 @@
     def node2(is_far, rim, acc, saved, more, outs, scratch, alias):
         return call(
             part_of(node2_kernel, nb, is_far),
-            (offs, rim, acc, tile_vals, w_in, w2, gain, kept, *saved, *more), outs, scratch, alias,
+            (offs, rim, acc, tile_vals, w_in, w2, gcols, kept, *saved, *more), outs, scratch, alias,
             flops=nb * tile_flops + mlp_flops, moved=8 * mib,
         )
 
     sums = [(ext, F32), (block, F32), (block, F32), (whole, F32)]
-    work = [v(half, BF16), v(half, BF16), v(half, BF16), v(block, F32)]
+    work = [v(half, BF16)] * 4
     *state, gagg_near, near = node2(
-        False, near, acc, saved_near, (), [*sums, (half, BF16, True), (half, BF16)], [*work, dma(2)], {}
-    )
-    near, far, bundle, gagg_far, acc, *_ = node2(
-        True, far, acc, saved_far, (near, gw1, gv1, *state),
-        [(half, BF16, True), (half, BF16, True), ((devices, 8 + share, hid), BF16, True), (half, BF16, True), (full, F32, True), *sums],
-        [*work, v(half, BF16), v((devices, 8 + share, hid), BF16), dma(5)],
-        {16 + i: 5 + i for i in range(4)},
+        False, near, acc, saved_near, (acc0,), [*sums, (half, BF16, True), (half, BF16, True)], [*work, dma(3)], {13: 0}
+    )
+    far, bundle, gagg_far, acc, *_ = node2(
+        True, far, acc, saved_far, (gw1, gv1, *state),
+        [(half, BF16, True), ((devices, 8 + share, hid), BF16, True), (half, BF16, True), (full, F32, True), *sums],
+        [*work, v((devices, 8 + share, hid), BF16), dma(4)],
+        {15 + i: 4 + i for i in range(4)},
     )
 
     parts = lax.all_to_all(bundle, AXES, 0, 0, tiled=True)

time: 97.7 us -> 95.8 us (0.981)
  Pallas kernels: 48.5 us -> 46.7 us
  waiting for transfers between devices: 21.9 us -> 20.3 us
  local copies, waits for them, and re-layouts: 0.71 us -> 2.06 us
    pallas_call x14, Pallas kernels: 48.5 us -> 46.7 us  [call(): pl.pallas_call(body, in_specs=[HBM if i in far_args else ANY if i in any_...]
    ppermute x8, waiting for transfers between devices: 12.7 us -> 11.1 us  [swap(): return lax.ppermute(x, AXES, pairs)]
    unnamed x16 -> x18, local copies, waits for them, and re-layouts: 0.71 us -> 2.06 us
where the time goes in v4:
time: 95.8 us; the launch traced here: 95.3 us
  Pallas kernels  46.7 us (49%)
  starting transfers between devices  25.2 us (26%)
  waiting for transfers between devices  20.3 us (21%)
  local copies, waits for them, and re-layouts  2.06 us (2%)
  between operations  1 us (1%)
    pallas_call x14, Pallas kernels, call(): pl.pallas_call(body, in_specs=[HBM if i in far_args else ANY if i in any_...  46.7 us
    ppermute x8, starting transfers between devices, swap(): return lax.ppermute(x, AXES, pairs)  12.3 us
    ppermute x8, waiting for transfers between devices, swap(): return lax.ppermute(x, AXES, pairs)  11.1 us
    all_to_all x1, waiting for transfers between devices, per_device(): parts = lax.all_to_all(bundle, AXES, 0, 0, tiled=True)  9.18 us
    all_to_all x1, starting transfers between devices, per_device(): sums = lax.all_to_all(mine, AXES, 0, 0, tiled=True)  6.74 us
    all_to_all x1, starting transfers between devices, per_device(): parts = lax.all_to_all(bundle, AXES, 0, 0, tiled=True)  6.21 us
    unnamed x18, local copies, waits for them, and re-layouts  2.06 us
  transfers between devices with their start and end apart: 10, of which 4 were waited for; matrix products, arithmetic and copies ran while one was open for 0% of the time, Pallas kernels for 39%

profile of v4, /device:TPU:1, one launch (start us, length us, event | category | flops | bytes accessed | tf_op | source)
XLA Modules:
  0.0 95.3 jit_solution(5061640891142579955)
XLA Ops:
  0.6 1.8 %shard_map.127 = (bf16[64,128,128]{2,1,0:T(8,128)(2,1)S(1)}, bf16[16,128,128]{2,1,0:T(8,128)(2,1)S(1)}) custom-call(bf16[4096,128]{1,0:T(8,128)(2,1)} %x_hbm.3), custom_call_target="tpu_custom_call" | custom-call | flops 134217728 | bytes 3145728 | tf_op jit(solution)/shard_map/pallas_call | solution.py:623
  2.4 2.7 %collective-permute-start.1 = (bf16[16,128,128]{2,1,0:T(8,128)(2,1)S(1)}, bf16[16,128,128]{2,1,0:T(8,128)(2,1)S(1)}, u32[]{:S(2)}, u32[]{:S(2)}) collective-permute-start(bf16[16,128,128]{2,1,0:T(8,128)(2,1)S(1)} %get-tuple-element.79), channel_id=1, source_target_pairs={{1,2},{2,1},{3,4},{4,3},{5,6},{6,5},{7,8},{8,7},{9,10},{10,9},{11,... | collective-permute-start | bytes 1572872 | tf_op jit(solution)/shard_map/ppermute | solution.py:62
  5.1 0.7 copy-done.4
  5.8 0.7 copy-done.6
  6.5 0.7 copy-done.7
  7.2 5.6 %shard_map.128 = (bf16[64,128,128]{2,1,0:T(8,128)(2,1)S(1)}, bf16[16,128,128]{2,1,0:T(8,128)(2,1)S(1)}, f32[32,128,128]{2,1,0:T(8,128)S(1)}, bf16[2,128,256]{2,1...) custom-call(s32[3,32]{1,0:T(4,128)S(1)} %bitcast.1, ...), custom_call_target="tpu_custom_call", output_to_operand_aliasing={{0}: (1, {})} | custom-call | flops 268435456 | bytes 6291456 | tf_op jit(solution)/shard_map/pallas_call | solution.py:623
  12.7 3.9 %collective-permute-start = (bf16[16,128,128]{2,1,0:T(8,128)(2,1)S(1)}, bf16[16,128,128]{2,1,0:T(8,128)(2,1)S(1)}, u32[]{:S(2)}, u32[]{:S(2)}) collective-permute-start(bf16[16,128,128]{2,1,0:T(8,128)(2,1)S(1)} %get-tuple-element.78), channel_id=1, source_target_pairs={{0,1},{1,0},{2,3},{3,2},{4,5},{5,4},{6,7},{7,6},{8,9},{9,8},{10,11... | collective-permute-start | bytes 1572872 | tf_op jit(solution)/shard_map/ppermute | solution.py:62
  16.6 1.0 %collective-permute-done.1.rim = bf16[16,128,128]{2,1,0:T(8,128)(2,1)S(1)} collective-permute-done((bf16[16,128,128]{2,1,0:T(8,128)(2,1)S(1)}, bf16[16,128,128]{2,1,0:T(8,128)(2,1)S(1)}, u32[]{:S(2)}, u32[]{:S(2)}) %collective-permute-start.1) | collective-permute-done | bytes 524320 | tf_op jit(solution)/shard_map/ppermute | solution.py:62
  17.6 2.1 %shard_map.129 = (bf16[16,128,128]{2,1,0:T(8,128)(2,1)S(1)}, bf16[64,128,128]{2,1,0:T(8,128)(2,1)S(1)}, bf16[64,128,128]{2,1,0:T(8,128)(2,1)S(1)}, bf16[16,128,1...) custom-call(s32[3,32]{1,0:T(4,128)S(1)} %bitcast.2, ...), custom_call_target="tpu_custom_call", output_to_operand_aliasing={{1}: (2, {})} | custom-call | flops 268435456 | bytes 6291456 | tf_op jit(solution)/shard_map/pallas_call | solution.py:623
  19.7 1.8 %collective-permute-start.3 = (bf16[16,128,128]{2,1,0:T(8,128)(2,1)S(1)}, bf16[16,128,128]{2,1,0:T(8,128)(2,1)S(1)}, u32[]{:S(2)}, u32[]{:S(2)}) collective-permute-start(bf16[16,128,128]{2,1,0:T(8,128)(2,1)S(1)} %get-tuple-element.89), channel_id=1, source_target_pairs={{1,2},{2,1},{3,4},{4,3},{5,6},{6,5},{7,8},{8,7},{9,10},{10,9},{11,... | collective-permute-start | bytes 1572872 | tf_op jit(solution)/shard_map/ppermute | solution.py:62
  21.6 2.1 %shard_map.130 = (bf16[16,128,128]{2,1,0:T(8,128)(2,1)S(1)}, bf16[64,128,128]{2,1,0:T(8,128)(2,1)S(1)}, bf16[64,128,128]{2,1,0:T(8,128)(2,1)S(1)}, bf16[16,128,1...) custom-call(s32[3,32]{1,0:T(4,128)S(1)} %bitcast.3, ...), custom_call_target="tpu_custom_call", output_to_operand_aliasing={{1}: (2, {}), {2}: (9, {})} | custom-call | flops 268435456 | bytes 6291456 | tf_op jit(solution)/shard_map/pallas_call | solution.py:623
  23.7 2.0 %collective-permute-start.2 = (bf16[16,128,128]{2,1,0:T(8,128)(2,1)S(1)}, bf16[16,128,128]{2,1,0:T(8,128)(2,1)S(1)}, u32[]{:S(2)}, u32[]{:S(2)}) collective-permute-start(bf16[16,128,128]{2,1,0:T(8,128)(2,1)S(1)} %get-tuple-element.88), channel_id=1, source_target_pairs={{0,1},{1,0},{2,3},{3,2},{4,5},{5,4},{6,7},{7,6},{8,9},{9,8},{10,11... | collective-permute-start | bytes 1572872 | tf_op jit(solution)/shard_map/ppermute | solution.py:62
  25.6 4.7 %shard_map.131 = (f32[32,128,128]{2,1,0:T(8,128)S(1)}, bf16[32,128,128]{2,1,0:T(8,128)(2,1)S(1)}, f32[64,128,128]{2,1,0:T(8,128)S(1)}, f32[64,128,128]{2,1,0:T(8,128)S(1)}) custom-call(s32[3,32]{1,0:T(4,128)S(1)} %bitcast.4, bf16[64,128,128]{2,1,0:T(8,128)(2,1)S(1)} %get-tuple-element.90.ext.ext_in, bf16[32,3,128,128]{3,2,1,0:T(8,128)(2,1)S(1)} %copy-done, ...), custom_call_target="tpu_custom_call" | custom-call | flops 268435456 | bytes 8388608 | tf_op jit(solution)/shard_map/pallas_call | solution.py:623
  30.4 3.7 %collective-permute-done.3.rim = bf16[16,128,128]{2,1,0:T(8,128)(2,1)S(1)} collective-permute-done((bf16[16,128,128]{2,1,0:T(8,128)(2,1)S(1)}, bf16[16,128,128]{2,1,0:T(8,128)(2,1)S(1)}, u32[]{:S(2)}, u32[]{:S(2)}) %collective-permute-start.3) | collective-permute-done | bytes 524320 | tf_op jit(solution)/shard_map/ppermute | solution.py:62
  34.0 3.3 %shard_map.132 = (bf16[16,128,128]{2,1,0:T(8,128)(2,1)S(1)}, bf16[64,128,128]{2,1,0:T(8,128)(2,1)S(1)}, bf16[16,128,128]{2,1,0:T(8,128)(2,1)S(1)}, bf16[16,128,1...) custom-call(s32[3,32]{1,0:T(4,128)S(1)} %bitcast.5, ...), custom_call_target="tpu_custom_call", output_to_operand_aliasing={{1}: (2, {}), {8}: (12, {})} | custom-call | flops 536870912 | bytes 8388608 | tf_op jit(solution)/shard_map/pallas_call | solution.py:623
  37.3 3.3 %shard_map.133 = (bf16[16,128,128]{2,1,0:T(8,128)(2,1)S(1)}, bf16[64,128,128]{2,1,0:T(8,128)(2,1)S(1)}, bf16[16,128,128]{2,1,0:T(8,128)(2,1)S(1)}, bf16[16,128,1...) custom-call(s32[3,32]{1,0:T(4,128)S(1)} %bitcast.6, ...), custom_call_target="tpu_custom_call", output_to_operand_aliasing={{1}: (2, {}), {8}: (12, {}), {9}: (13, {}), {10}: (14, {})} | custom-call | flops 536870912 | bytes 8388608 | tf_op jit(solution)/shard_map/pallas_call | solution.py:623
  40.6 0.1 collective-permute-start.4
  40.7 0.1 collective-permute-start.6
  40.8 0.0 copy-start.1
  40.8 4.1 %shard_map.134 = (f32[64,128,128]{2,1,0:T(8,128)S(1)}, f32[384,128]{1,0:T(8,128)S(1)}, f32[2,128]{1,0:T(2,128)S(1)}, bf16[32,128,128]{2,1,0:T(8,128)(2,1)}) custom-call(s32[3,32]{1,0:T(4,128)S(1)} %bitcast.7, f32[64,128,128]{2,1,0:T(8,128)S(1)} %get-tuple-element.99.acc_in, bf16[32,3,128,128]{3,2,1,0:T(8,128)(2,1)S(1)} %copy-done, ...), custom_call_target="tpu_custom_call", output_to_operand_aliasing={{0}: (1, {})} | custom-call | flops 4194304 | bytes 1048576 | tf_op jit(solution)/shard_map/pallas_call | solution.py:623
  44.9 3.6 %shard_map.136 = (f32[64,128,128]{2,1,0:T(8,128)S(1)}, f32[128,128]{1,0:T(8,128)S(1)}, f32[128,128]{1,0:T(8,128)S(1)}, f32[384,128]{1,0:T(8,128)S(1)}, bf16[16,1...) custom-call(s32[3,32]{1,0:T(4,128)S(1)} %bitcast.8, ...), custom_call_target="tpu_custom_call", output_to_operand_aliasing={{0}: (13, {})} | custom-call | flops 536870912 | bytes 8388608 | tf_op jit(solution)/shard_map/pallas_call | solution.py:623
  48.5 6.4 %collective-permute-done.6.rim = bf16[16,128,128]{2,1,0:T(8,128)(2,1)S(1)} collective-permute-done((bf16[16,128,128]{2,1,0:T(8,128)(2,1)S(1)}, bf16[16,128,128]{2,1,0:T(8,128)(2,1)S(1)}, u32[]{:S(2)}, u32[]{:S(2)}) %collective-permute-start.6) | collective-permute-done | bytes 524320 | tf_op jit(solution)/shard_map/ppermute | solution.py:62
  55.0 3.9 %shard_map.137 = (bf16[16,128,128]{2,1,0:T(8,128)(2,1)}, bf16[32,32,128]{2,1,0:T(8,128)(2,1)}, bf16[16,128,128]{2,1,0:T(8,128)(2,1)}, f32[32,128,128]{2,1,0:T(8,...) custom-call(s32[3,32]{1,0:T(4,128)S(1)} %bitcast.9, ...), custom_call_target="tpu_custom_call", output_to_operand_aliasing={{4}: (15, {}), {5}: (16, {}), {6}: (17, {}), {7}: (18, {})} | custom-call | flops 536870912 | bytes 8388608 | tf_op jit(solution)/shard_map/pallas_call | solution.py:623
  58.9 6.2 %all-to-all-start = ((bf16[32,32,128]{2,1,0:T(8,128)(2,1)}), bf16[32,32,128]{2,1,0:T(8,128)(2,1)S(1)}, u32[]{:S(2)}, u32[]{:S(2)}) async-start(bf16[32,32,128]{2,1,0:T(8,128)(2,1)} %get-tuple-element.142), calls=%async_computation | async-start | bytes 524288 | tf_op jit(solution)/shard_map/all_to_all | solution.py:739
  65.1 0.3 collective-permute-start.5
  65.5 1.5 %collective-permute-start.7 = (bf16[16,128,128]{2,1,0:T(8,128)(2,1)}, bf16[16,128,128]{2,1,0:T(8,128)(2,1)S(1)}, u32[]{:S(2)}, u32[]{:S(2)}) collective-permute-start(bf16[16,128,128]{2,1,0:T(8,128)(2,1)} %get-tuple-element.138), channel_id=1, source_target_pairs={{1,2},{2,1},{3,4},{4,3},{5,6},{6,5},{7,8},{8,7},{9,10},{10,9},{11,... | collective-permute-start | bytes 1572872 | tf_op jit(solution)/shard_map/ppermute | solution.py:62
  66.9 9.2 %all-to-all-done.parts = bf16[32,32,128]{2,1,0:T(8,128)(2,1)S(1)} async-done(((bf16[32,32,128]{2,1,0:T(8,128)(2,1)}), bf16[32,32,128]{2,1,0:T(8,128)(2,1)S(1)}, u32[]{:S(2)}, u32[]{:S(2)}) %all-to-all-start) | async-done | bytes 262176 | tf_op jit(solution)/shard_map/all_to_all | solution.py:739
  76.1 1.3 %shard_map.139 = (bf16[32,24,128]{2,1,0:T(8,128)(2,1)}, f32[2,128]{1,0:T(2,128)}, f32[2,128]{1,0:T(2,128)}) custom-call(bf16[32,32,128]{2,1,0:T(8,128)(2,1)S(1)} %all-to-all-done.parts), custom_call_target="tpu_custom_call" | custom-call | flops 524288 | bytes 1048576 | tf_op jit(solution)/shard_map/pallas_call | solution.py:623
  77.4 6.7 %all-to-all-start.1 = ((bf16[32,24,128]{2,1,0:T(8,128)(2,1)}), bf16[32,24,128]{2,1,0:T(8,128)(2,1)S(1)}, u32[]{:S(2)}, u32[]{:S(2)}) async-start(bf16[32,24,128]{2,1,0:T(8,128)(2,1)} %get-tuple-element.143), calls=%async_computation.1 | async-start | bytes 393216 | tf_op jit(solution)/shard_map/all_to_all | solution.py:752
  84.2 2.9 %shard_map.135 = bf16[4096,128]{1,0:T(8,128)(2,1)} custom-call(bf16[32,128,128]{2,1,0:T(8,128)(2,1)} %get-tuple-element.115.h_hbm), custom_call_target="tpu_custom_call" | custom-call | flops 134217728 | bytes 2097152 | tf_op jit(solution)/shard_map/pallas_call | solution.py:623
  87.1 7.2 %shard_map.138 = f32[4096,128]{1,0:T(8,128)} custom-call(s32[3,32]{1,0:T(4,128)S(1)} %bitcast.10, bf16[16,128,128]{2,1,0:T(8,128)(2,1)S(1)} %collective-permute-done.5.near, bf16[16,128,128]{2,1,0:T(8,128)(2,1)S(1)} %collective-permute-done.7.far, f32[32,128,128]{2,1,0:T(8,128)} %get-tuple-element.139.acc_hbm, ...), custom_call_target="tpu_custom_call" | custom-call | flops 268435456 | bytes 9437184 | tf_op jit(solution)/shard_map/pallas_call | solution.py:623
  94.3 0.8 shard_map.140
  (20 shorter events, 0.0 us)
Async XLA Ops:
  2.4 15.2 %collective-permute-start.1 = (bf16[16,128,128]{2,1,0:T(8,128)(2,1)S(1)}, bf16[16,128,128]{2,1,0:T(8,128)(2,1)S(1)}, u32[]{:S(2)}, u32[]{:S(2)}) collective-permute-start(bf16[16,128,128]{2,1,0:T(8,128)(2,1)S(1)} %get-tuple-element.79), channel_id=1, source_target_pairs={{1,2},{2,1},{3,4},{4,3},{5,6},{6,5},{7,8},{8,7},{9,10},{10,9},{11,... | collective-permute-start | bytes 1572872 | tf_op jit(solution)/shard_map/ppermute | solution.py:62
  5.1 0.7 copy-start.4
  5.8 0.7 copy-start.6
  6.5 0.7 copy-start.7
  7.2 10.4 %copy-start = (bf16[32,3,128,128]{3,2,1,0:T(8,128)(2,1)S(1)}, bf16[32,3,128,128]{3,2,1,0:T(8,128)(2,1)}, u32[]{:S(2)}) copy-start(bf16[32,3,128,128]{3,2,1,0:T(8,128)(2,1)} %tiles_hbm.3) | copy-start | bytes 9437188
  12.7 8.8 %collective-permute-start = (bf16[16,128,128]{2,1,0:T(8,128)(2,1)S(1)}, bf16[16,128,128]{2,1,0:T(8,128)(2,1)S(1)}, u32[]{:S(2)}, u32[]{:S(2)}) collective-permute-start(bf16[16,128,128]{2,1,0:T(8,128)(2,1)S(1)} %get-tuple-element.78), channel_id=1, source_target_pairs={{0,1},{1,0},{2,3},{3,2},{4,5},{5,4},{6,7},{7,6},{8,9},{9,8},{10,11... | collective-permute-start | bytes 1572872 | tf_op jit(solution)/shard_map/ppermute | solution.py:62
  19.7 14.3 %collective-permute-start.3 = (bf16[16,128,128]{2,1,0:T(8,128)(2,1)S(1)}, bf16[16,128,128]{2,1,0:T(8,128)(2,1)S(1)}, u32[]{:S(2)}, u32[]{:S(2)}) collective-permute-start(bf16[16,128,128]{2,1,0:T(8,128)(2,1)S(1)} %get-tuple-element.89), channel_id=1, source_target_pairs={{1,2},{2,1},{3,4},{4,3},{5,6},{6,5},{7,8},{8,7},{9,10},{10,9},{11,... | collective-permute-start | bytes 1572872 | tf_op jit(solution)/shard_map/ppermute | solution.py:62
  21.5 4.1 %copy-start.3 = (bf16[4096,128]{1,0:T(8,128)(2,1)S(1)}, bf16[4096,128]{1,0:T(8,128)(2,1)}, u32[]{:S(2)}) copy-start(bf16[4096,128]{1,0:T(8,128)(2,1)} %cot.1) | copy-start | bytes 3145732
  21.6 4.1 %copy-start.5 = (s32[32,3]{0,1:T(4,128)S(1)}, s32[32,3]{0,1:T(4,128)}, u32[]{:S(2)}) copy-start(s32[32,3]{0,1:T(4,128)} %param.10) | copy-start | bytes 1156
  23.7 13.6 %collective-permute-start.2 = (bf16[16,128,128]{2,1,0:T(8,128)(2,1)S(1)}, bf16[16,128,128]{2,1,0:T(8,128)(2,1)S(1)}, u32[]{:S(2)}, u32[]{:S(2)}) collective-permute-start(bf16[16,128,128]{2,1,0:T(8,128)(2,1)S(1)} %get-tuple-element.88), channel_id=1, source_target_pairs={{0,1},{1,0},{2,3},{3,2},{4,5},{5,4},{6,7},{7,6},{8,9},{9,8},{10,11... | collective-permute-start | bytes 1572872 | tf_op jit(solution)/shard_map/ppermute | solution.py:62
  25.6 8.4 %copy-start.2 = (bf16[2,256,128]{2,1,0:T(8,128)(2,1)S(1)}, bf16[2,256,128]{2,1,0:T(8,128)(2,1)}, u32[]{:S(2)}) copy-start(bf16[2,256,128]{2,1,0:T(8,128)(2,1)} %w_in.7) | copy-start | bytes 393220
  40.6 4.3 %collective-permute-start.4 = (bf16[16,128,128]{2,1,0:T(8,128)(2,1)S(1)}, bf16[16,128,128]{2,1,0:T(8,128)(2,1)S(1)}, u32[]{:S(2)}, u32[]{:S(2)}) collective-permute-start(bf16[16,128,128]{2,1,0:T(8,128)(2,1)S(1)} %get-tuple-element.116), channel_id=1, source_target_pairs={{0,1},{1,0},{2,3},{3,2},{4,5},{5,4},{6,7},{7,6},{8,9},{9,8},{10,11... | collective-permute-start | bytes 1572872 | tf_op jit(solution)/shard_map/ppermute | solution.py:62
  40.7 14.3 %collective-permute-start.6 = (bf16[16,128,128]{2,1,0:T(8,128)(2,1)S(1)}, bf16[16,128,128]{2,1,0:T(8,128)(2,1)S(1)}, u32[]{:S(2)}, u32[]{:S(2)}) collective-permute-start(bf16[16,128,128]{2,1,0:T(8,128)(2,1)S(1)} %get-tuple-element.126), channel_id=1, source_target_pairs={{1,2},{2,1},{3,4},{4,3},{5,6},{6,5},{7,8},{8,7},{9,10},{10,9},{11,... | collective-permute-start | bytes 1572872 | tf_op jit(solution)/shard_map/ppermute | solution.py:62
  40.8 4.1 %copy-start.1 = (bf16[32,128,128]{2,1,0:T(8,128)(2,1)S(1)}, bf16[32,128,128]{2,1,0:T(8,128)(2,1)}, u32[]{:S(2)}) copy-start(bf16[32,128,128]{2,1,0:T(8,128)(2,1)} %get-tuple-element.118.kept) | copy-start | bytes 3145732
  55.0 10.1 %copy-start.8 = (bf16[16,128,128]{2,1,0:T(8,128)(2,1)S(1)}, bf16[16,128,128]{2,1,0:T(8,128)(2,1)}, u32[]{:S(2)}) copy-start(bf16[16,128,128]{2,1,0:T(8,128)(2,1)} %get-tuple-element.125) | copy-start | bytes 1572868
  58.9 17.2 %all-to-all-start = ((bf16[32,32,128]{2,1,0:T(8,128)(2,1)}), bf16[32,32,128]{2,1,0:T(8,128)(2,1)S(1)}, u32[]{:S(2)}, u32[]{:S(2)}) async-start(bf16[32,32,128]{2,1,0:T(8,128)(2,1)} %get-tuple-element.142), calls=%async_computation | async-start | bytes 524288 | tf_op jit(solution)/shard_map/all_to_all | solution.py:739
  65.1 22.0 %collective-permute-start.5 = (bf16[16,128,128]{2,1,0:T(8,128)(2,1)S(1)}, bf16[16,128,128]{2,1,0:T(8,128)(2,1)S(1)}, u32[]{:S(2)}, u32[]{:S(2)}) collective-permute-start(bf16[16,128,128]{2,1,0:T(8,128)(2,1)S(1)} %copy-done.8), channel_id=1, source_target_pairs={{0,1},{1,0},{2,3},{3,2},{4,5},{5,4},{6,7},{7,6},{8,9},{9,8},{10,11... | collective-permute-start | bytes 1572872 | tf_op jit(solution)/shard_map/ppermute | solution.py:62
  65.5 21.7 %collective-permute-start.7 = (bf16[16,128,128]{2,1,0:T(8,128)(2,1)}, bf16[16,128,128]{2,1,0:T(8,128)(2,1)S(1)}, u32[]{:S(2)}, u32[]{:S(2)}) collective-permute-start(bf16[16,128,128]{2,1,0:T(8,128)(2,1)} %get-tuple-element.138), channel_id=1, source_target_pairs={{1,2},{2,1},{3,4},{4,3},{5,6},{6,5},{7,8},{8,7},{9,10},{10,9},{11,... | collective-permute-start | bytes 1572872 | tf_op jit(solution)/shard_map/ppermute | solution.py:62
  77.4 16.9 %all-to-all-start.1 = ((bf16[32,24,128]{2,1,0:T(8,128)(2,1)}), bf16[32,24,128]{2,1,0:T(8,128)(2,1)S(1)}, u32[]{:S(2)}, u32[]{:S(2)}) async-start(bf16[32,24,128]{2,1,0:T(8,128)(2,1)} %get-tuple-element.143), calls=%async_computation.1 | async-start | bytes 393216 | tf_op jit(solution)/shard_map/all_to_all | solution.py:752

commit v5 on v4

--- a/solution.py
+++ b/solution.py
@@ -67,6 +67,14 @@
     return (odd if far else 1 - odd) * (HALO + nb)
 
 
+def quarter(nb, nearest):
+    odd = parity()
+    q = HALO // 2
+    if nearest:
+        return odd * (HALO + q), odd * q, q + odd * (nb + q)
+    return q + odd * (HALO - q), q - odd * q, odd * (nb + HALO + q)
+
+
 def rows_at(far):
     odd = parity()
     return (odd if far else 1 - odd) * HALO
@@ -107,16 +115,18 @@
     )
 
 
-def turn_kernel(x_hbm, ext, far, x, sem):
-    base = rows_at(True)
+def turn_kernel(nb, x_hbm, ext, near_border, outer, x, sem):
     blk = ext.shape[2]
+    q = HALO // 2
+    starts = [quarter(nb, True)[0], quarter(nb, False)[0]]
     pieces = sem.shape[0]
     per = HALO // pieces
 
     def get(i):
         rows = per * blk
+        first = starts[i * per // q] + i * per % q
         return pltpu.make_async_copy(
-            x_hbm.at[pl.ds(pl.multiple_of((base + i * per) * blk, rows), rows)],
+            x_hbm.at[pl.ds(pl.multiple_of(first * blk, rows), rows)],
             x.at[pl.ds(i * rows, rows)],
             sem.at[i],
         )
@@ -128,8 +138,11 @@
         get(i).wait()
         for b in range(i * per, (i + 1) * per):
             block = nt(one, x[b * blk : (b + 1) * blk]).astype(BF16)
-            ext[HALO + base + b] = block
-            far[b] = block
+            ext[HALO + starts[b // q] + b % q] = block
+            if b < q:
+                near_border[b] = block
+            else:
+                outer[b - q] = block
 
 
 def fetch_rims(near_hbm, far_hbm, rims, sem):
@@ -146,7 +159,7 @@
     def one(b):
         buf[at + b] = rim[b]
 
-    for_blocks(HALO, one, 8)
+    for_blocks(rim.shape[0], one, 8)
 
 
 def inner_tile(b, ext, tiles, offs, part):
@@ -299,46 +312,54 @@
 
 
 def node0_kernel(
-    nb, is_far, offs, rim, ext_in, part, tiles, w1t, w2t, bcols, gcols, *refs
+    nb, kind, offs, rim, ext_in, part, tiles, w1t, w2t, bcols, gcols, *refs
 ):
-    rim_out, ext, after_ext, agg, act, slope, xhat, inv = refs if is_far else refs[1:]
+    rim_out, ext, after_ext, agg, act, slope, xhat, inv = refs[{"outer": 0, "nearest": 6, "near": 1}[kind] :]
     bcol, gcol = bcols.at[0], gcols.at[0]
     blk = tiles.shape[2]
-    take_rim(rim, ext, rim_at(nb, is_far))
-    base = rows_at(is_far)
+    if kind == "near":
+        base, local, at = rows_at(False), 0, rim_at(nb, False)
+    else:
+        base, local, _ = quarter(nb, kind == "nearest")
+        at = quarter(nb, kind == "outer")[2]
+    take_rim(rim, ext, at)
 
     def join(it):
         return join_step(chunk(base, it), ext, part, tiles, offs, w1t[0], bcol)
 
     def mixing(it, feats, agg_w, half):
-        for s, b in enumerate(chunk(0, it)):
+        for s, b in enumerate(chunk(local, it)):
             agg[b] = cut(agg_w, s, blk)
         return feats, *mix_step(half, w2t[0])
 
     def norm(it, feats, act_w, slope_w, mix):
         xhat_w, inv_w, after = norm_step(feats, mix, gcol)
         slope_w, xhat_w = slope_w.astype(BF16), xhat_w.astype(BF16)
-        for s, b in enumerate(chunk(0, it)):
+        for s, b in enumerate(chunk(local, it)):
             act[b] = cut(act_w, s, blk)
             slope[b] = cut(slope_w, s, blk)
             xhat[b] = cut(xhat_w, s, blk)
             inv[b] = cut(inv_w, s, blk)
-            after_ext[HALO + base + b] = cut(after, s, blk)
-            rim_out[b] = cut(after, s, blk)
-
-    pipelined(HALO // CH, join, mixing, norm)
+            after_ext[HALO + base + it * CH + s] = cut(after, s, blk)
+            rim_out[it * CH + s] = cut(after, s, blk)
+
+    pipelined(rim_out.shape[0] // CH, join, mixing, norm)
 
 
 def node1_kernel(
     nb, is_far, offs, rim, ext_in, part, tiles, cott, w1t, w2t, w_in, w2, bcols, gcols, *refs
 ):
-    rim_out, ext, h2, agg, act, gmix, gpre, gagg, acc, gb, gg = refs[1:] if is_far else refs[3:]
+    rim_out, ext, h2, agg, act, gmix, gpre, gagg, acc, gb, gg = refs[2:] if is_far else refs[3:]
     bcol, gcol = bcols.at[1], gcols.at[1]
     blk = tiles.shape[2]
     if is_far:
         gb[...] = jnp.zeros_like(gb)
         gg[...] = jnp.zeros_like(gg)
-    take_rim(rim, ext, rim_at(nb, is_far))
+    if is_far:
+        take_rim(rim, ext, quarter(nb, True)[2])
+        take_rim(refs[1], ext, quarter(nb, False)[2])
+    else:
+        take_rim(rim, ext, rim_at(nb, False))
     base = rows_at(is_far)
 
     def join(it):
@@ -663,12 +684,14 @@
     half = (HALO, *block)
     half_rows = (nodes // 2, width)
 
-    h0, far = call(
-        turn_kernel, (feats,), [(ext, BF16), (half, BF16)],
+    some = (HALO // 2, *block)
+    h0, border, outer = call(
+        part_of(turn_kernel, nb), (feats,), [(ext, BF16), (some, BF16), (some, BF16)],
         [v(half_rows, BF16), dma(4)], far_args=(0,),
         flops=nb * tile_flops, moved=3 * mib,
     )
-    far = swap(far, True)
+    border = swap(border, True)
+    outer = swap(outer, True)
     h0, near, part, w1t, w2t, w2, bcols, gcols, kept = call(
         part_of(inner0_kernel, nb), (offs, h0, feats, tile_vals, w_in, w_out, bias_in, gain),
         [(ext, BF16), (half, BF16), (full, F32), ((layers, hid, 2 * width), BF16), ((layers, width, hid), BF16),
@@ -679,18 +702,22 @@
     )
     near = swap(near, False)
 
-    def node0(is_far, rim, h, more):
+    def node0(kind, rim, h, more):
+        alias = {2: 1} | {9 + i: 2 + i for i in range(len(more))}
         return call(
-            part_of(node0_kernel, nb, is_far),
+            part_of(node0_kernel, nb, kind),
             (offs, rim, h, part, tile_vals, w1t, w2t, bcols, gcols, *more),
-            [(half, BF16), (ext, BF16), (ext, BF16), *[(half, BF16)] * 4, ((HALO, 1, blk), F32)],
-            alias={2: 1} if is_far else {2: 1, 9: 2},
-            flops=(nb * tile_flops + mlp_flops) // 2, moved=6 * mib,
+            [(rim.shape, BF16), (ext, BF16), (ext, BF16), *[(half, BF16)] * 4, ((HALO, 1, blk), F32)],
+            alias=alias,
+            flops=(nb * tile_flops + mlp_flops) // 4, moved=4 * mib,
         )
 
-    far, h0, h1, *saved_far = node0(True, far, h0, ())
-    far = swap(far, True)
-    near, h0, h1, *saved_near = node0(False, near, h0, (h1,))
+    next_outer, h0, *saved_far = node0("outer", border, h0, ())
+    next_outer = swap(next_outer, True)
+    border, h0, *saved_far = node0("nearest", outer, h0, saved_far)
+    border = swap(border, True)
+    near, h0, h1, *saved_near = node0("near", near, h0, saved_far[:1])
+    saved_far = saved_far[1:]
     near = swap(near, False)
     part, cott, acc1, acc0 = call(
         part_of(inner1_kernel, nb), (offs, h1, tile_vals, cot), [(full, F32), (full, BF16), (ext, F32), (ext, F32)],
@@ -706,7 +733,7 @@
             flops=nb * tile_flops + mlp_flops, moved=8 * mib,
         )
 
-    far, h1, *made_far, acc, gb1, gg1 = node1(True, far, h1, (acc1,))
+    far, h1, *made_far, acc, gb1, gg1 = node1(True, border, h1, (acc1, next_outer))
     far = swap(far, True)
     near, h1, *made_near, acc, gb1, gg1 = node1(False, near, h1, (acc, gb1, gg1))
     near = swap(near, False)

time: 95.8 us -> 105 us (1.096)
  waiting for transfers between devices: 20.3 us -> 33.2 us
  starting transfers between devices: 25.2 us -> 20.8 us
    ppermute x8 -> x10, waiting for transfers between devices: 11.1 us -> 24 us  [swap(): return lax.ppermute(x, AXES, pairs)]
    ppermute x8 -> x10, starting transfers between devices: 12.3 us -> 9.17 us  [swap(): return lax.ppermute(x, AXES, pairs)]
    all_to_all x1, starting transfers between devices: 6.21 us -> 4.89 us  [per_device(): parts = lax.all_to_all(bundle, AXES, 0, 0, tiled=True)]
    pallas_call x14 -> x15, Pallas kernels: 46.7 us -> 47.6 us  [call(): pl.pallas_call(body, in_specs=[HBM if i in far_args else ANY if i in any_...]
  transfers between devices with their start and end apart: 10 -> 12, of which waited for: 4 -> 6; matrix products, arithmetic and copies ran while one was open for 0% -> 0% of each run, Pallas kernels for 39% -> 29%
where the time goes in v5:
time: 105 us
  Pallas kernels  47.6 us (45%)
  waiting for transfers between devices  33.2 us (32%)
  starting transfers between devices  20.8 us (20%)
  local copies, waits for them, and re-layouts  2.06 us (2%)
    pallas_call x15, Pallas kernels, call(): pl.pallas_call(body, in_specs=[HBM if i in far_args else ANY if i in any_...  47.6 us
    ppermute x10, waiting for transfers between devices, swap(): return lax.ppermute(x, AXES, pairs)  24 us
    all_to_all x1, waiting for transfers between devices, per_device(): parts = lax.all_to_all(bundle, AXES, 0, 0, tiled=True)  9.19 us
    ppermute x10, starting transfers between devices, swap(): return lax.ppermute(x, AXES, pairs)  9.17 us
    all_to_all x1, starting transfers between devices, per_device(): sums = lax.all_to_all(mine, AXES, 0, 0, tiled=True)  6.74 us
    all_to_all x1, starting transfers between devices, per_device(): parts = lax.all_to_all(bundle, AXES, 0, 0, tiled=True)  4.89 us
  transfers between devices with their start and end apart: 12, of which 6 were waited for; matrix products, arithmetic and copies ran while one was open for 0% of the time, Pallas kernels for 29%

profile of v5, /device:TPU:1, one launch (start us, length us, event | category | flops | bytes accessed | tf_op | source)
XLA Modules:
  0.0 104.6 jit_solution(10975800846013473718)
XLA Ops:
  0.6 1.8 %shard_map.127 = (bf16[64,128,128]{2,1,0:T(8,128)(2,1)S(1)}, bf16[8,128,128]{2,1,0:T(8,128)(2,1)S(1)}, bf16[8,128,128]{2,1,0:T(8,128)(2,1)S(1)}) custom-call(bf16[4096,128]{1,0:T(8,128)(2,1)} %x_hbm.3), custom_call_target="tpu_custom_call" | custom-call | flops 134217728 | bytes 3145728 | tf_op jit(solution)/shard_map/pallas_call | solution.py:644
  2.5 0.7 copy-done.4
  3.1 0.7 copy-done.6
  3.8 0.7 copy-done.7
  4.5 5.6 %shard_map.128 = (bf16[64,128,128]{2,1,0:T(8,128)(2,1)S(1)}, bf16[16,128,128]{2,1,0:T(8,128)(2,1)S(1)}, f32[32,128,128]{2,1,0:T(8,128)S(1)}, bf16[2,128,256]{2,1...) custom-call(s32[3,32]{1,0:T(4,128)S(1)} %bitcast.1, ...), custom_call_target="tpu_custom_call", output_to_operand_aliasing={{0}: (1, {})} | custom-call | flops 268435456 | bytes 6291456 | tf_op jit(solution)/shard_map/pallas_call | solution.py:644
  10.1 2.7 %collective-permute-start.2 = (bf16[8,128,128]{2,1,0:T(8,128)(2,1)S(1)}, bf16[8,128,128]{2,1,0:T(8,128)(2,1)S(1)}, u32[]{:S(2)}, u32[]{:S(2)}) collective-permute-start(bf16[8,128,128]{2,1,0:T(8,128)(2,1)S(1)} %get-tuple-element.89), channel_id=1, source_target_pairs={{1,2},{2,1},{3,4},{4,3},{5,6},{6,5},{7,8},{8,7},{9,10},{10,9},{11,... | collective-permute-start | bytes 786440 | tf_op jit(solution)/shard_map/ppermute | solution.py:62
  12.9 8.9 %collective-permute-done.2.rim = bf16[8,128,128]{2,1,0:T(8,128)(2,1)S(1)} collective-permute-done((bf16[8,128,128]{2,1,0:T(8,128)(2,1)S(1)}, bf16[8,128,128]{2,1,0:T(8,128)(2,1)S(1)}, u32[]{:S(2)}, u32[]{:S(2)}) %collective-permute-start.2) | collective-permute-done | bytes 262176 | tf_op jit(solution)/shard_map/ppermute | solution.py:62
  21.8 1.5 %shard_map.129 = (bf16[8,128,128]{2,1,0:T(8,128)(2,1)S(1)}, bf16[64,128,128]{2,1,0:T(8,128)(2,1)S(1)}, bf16[64,128,128]{2,1,0:T(8,128)(2,1)S(1)}, bf16[16,128,12...) custom-call(s32[3,32]{1,0:T(4,128)S(1)} %bitcast.2, ...), custom_call_target="tpu_custom_call", output_to_operand_aliasing={{1}: (2, {})} | custom-call | flops 134217728 | bytes 4194304 | tf_op jit(solution)/shard_map/pallas_call | solution.py:644
  23.2 1.3 %collective-permute-done.1.rim = bf16[8,128,128]{2,1,0:T(8,128)(2,1)S(1)} collective-permute-done((bf16[8,128,128]{2,1,0:T(8,128)(2,1)S(1)}, bf16[8,128,128]{2,1,0:T(8,128)(2,1)S(1)}, u32[]{:S(2)}, u32[]{:S(2)}) %collective-permute-start.1) | collective-permute-done | bytes 262176 | tf_op jit(solution)/shard_map/ppermute | solution.py:62
  24.6 1.5 %shard_map.130 = (bf16[8,128,128]{2,1,0:T(8,128)(2,1)S(1)}, bf16[64,128,128]{2,1,0:T(8,128)(2,1)S(1)}, bf16[64,128,128]{2,1,0:T(8,128)(2,1)S(1)}, bf16[16,128,12...) custom-call(s32[3,32]{1,0:T(4,128)S(1)} %bitcast.3, ...), custom_call_target="tpu_custom_call", output_to_operand_aliasing={{1}: (2, {}), {2}: (9, {}), {3}: (10, {}), {4}: (11, {}), {... | custom-call | flops 134217728 | bytes 4194304 | tf_op jit(solution)/shard_map/pallas_call | solution.py:644
  26.1 2.1 %shard_map.131 = (bf16[16,128,128]{2,1,0:T(8,128)(2,1)S(1)}, bf16[64,128,128]{2,1,0:T(8,128)(2,1)S(1)}, bf16[64,128,128]{2,1,0:T(8,128)(2,1)S(1)}, bf16[16,128,1...) custom-call(s32[3,32]{1,0:T(4,128)S(1)} %bitcast.4, ...), custom_call_target="tpu_custom_call", output_to_operand_aliasing={{1}: (2, {}), {2}: (9, {})} | custom-call | flops 134217728 | bytes 4194304 | tf_op jit(solution)/shard_map/pallas_call | solution.py:644
  28.2 2.1 %collective-permute-start.3 = (bf16[16,128,128]{2,1,0:T(8,128)(2,1)S(1)}, bf16[16,128,128]{2,1,0:T(8,128)(2,1)S(1)}, u32[]{:S(2)}, u32[]{:S(2)}) collective-permute-start(bf16[16,128,128]{2,1,0:T(8,128)(2,1)S(1)} %get-tuple-element.105), channel_id=1, source_target_pairs={{0,1},{1,0},{2,3},{3,2},{4,5},{5,4},{6,7},{7,6},{8,9},{9,8},{10,11... | collective-permute-start | bytes 1572872 | tf_op jit(solution)/shard_map/ppermute | solution.py:62
  30.3 0.5 collective-permute-start.4
  30.9 1.2 %collective-permute-start.5 = (bf16[8,128,128]{2,1,0:T(8,128)(2,1)S(1)}, bf16[8,128,128]{2,1,0:T(8,128)(2,1)S(1)}, u32[]{:S(2)}, u32[]{:S(2)}) collective-permute-start(bf16[8,128,128]{2,1,0:T(8,128)(2,1)S(1)} %get-tuple-element.112), channel_id=1, source_target_pairs={{1,2},{2,1},{3,4},{4,3},{5,6},{6,5},{7,8},{8,7},{9,10},{10,9},{11,... | collective-permute-start | bytes 786440 | tf_op jit(solution)/shard_map/ppermute | solution.py:62
  32.1 4.7 %shard_map.132 = (f32[32,128,128]{2,1,0:T(8,128)S(1)}, bf16[32,128,128]{2,1,0:T(8,128)(2,1)S(1)}, f32[64,128,128]{2,1,0:T(8,128)S(1)}, f32[64,128,128]{2,1,0:T(8,128)S(1)}) custom-call(s32[3,32]{1,0:T(4,128)S(1)} %bitcast.5, bf16[64,128,128]{2,1,0:T(8,128)(2,1)S(1)} %get-tuple-element.107.ext.ext_in, bf16[32,3,128,128]{3,2,1,0:T(8,128)(2,1)S(1)} %copy-done, ...), custom_call_target="tpu_custom_call" | custom-call | flops 268435456 | bytes 8388608 | tf_op jit(solution)/shard_map/pallas_call | solution.py:644
  36.8 3.0 %collective-permute-done.4.rim = bf16[8,128,128]{2,1,0:T(8,128)(2,1)S(1)} collective-permute-done((bf16[8,128,128]{2,1,0:T(8,128)(2,1)S(1)}, bf16[8,128,128]{2,1,0:T(8,128)(2,1)S(1)}, u32[]{:S(2)}, u32[]{:S(2)}) %collective-permute-start.4) | collective-permute-done | bytes 262176 | tf_op jit(solution)/shard_map/ppermute | solution.py:62
  39.8 4.8 %collective-permute-done.5.refs_1_ = bf16[8,128,128]{2,1,0:T(8,128)(2,1)S(1)} collective-permute-done((bf16[8,128,128]{2,1,0:T(8,128)(2,1)S(1)}, bf16[8,128,128]{2,1,0:T(8,128)(2,1)S(1)}, u32[]{:S(2)}, u32[]{:S(2)}) %collective-permute-start.5) | collective-permute-done | bytes 262176 | tf_op jit(solution)/shard_map/ppermute | solution.py:62
  44.6 3.3 %shard_map.133 = (bf16[16,128,128]{2,1,0:T(8,128)(2,1)S(1)}, bf16[64,128,128]{2,1,0:T(8,128)(2,1)S(1)}, bf16[16,128,128]{2,1,0:T(8,128)(2,1)S(1)}, bf16[16,128,1...) custom-call(s32[3,32]{1,0:T(4,128)S(1)} %bitcast.6, ...), custom_call_target="tpu_custom_call", output_to_operand_aliasing={{1}: (2, {}), {8}: (12, {})} | custom-call | flops 536870912 | bytes 8388608 | tf_op jit(solution)/shard_map/pallas_call | solution.py:644
  47.9 3.3 %shard_map.134 = (bf16[16,128,128]{2,1,0:T(8,128)(2,1)S(1)}, bf16[64,128,128]{2,1,0:T(8,128)(2,1)S(1)}, bf16[16,128,128]{2,1,0:T(8,128)(2,1)S(1)}, bf16[16,128,1...) custom-call(s32[3,32]{1,0:T(4,128)S(1)} %bitcast.7, ...), custom_call_target="tpu_custom_call", output_to_operand_aliasing={{1}: (2, {}), {8}: (12, {}), {9}: (13, {}), {10}: (14, {})} | custom-call | flops 536870912 | bytes 8388608 | tf_op jit(solution)/shard_map/pallas_call | solution.py:644
  51.5 0.4 collective-permute-start.8
  51.9 4.1 %shard_map.135 = (f32[64,128,128]{2,1,0:T(8,128)S(1)}, f32[384,128]{1,0:T(8,128)S(1)}, f32[2,128]{1,0:T(2,128)S(1)}, bf16[32,128,128]{2,1,0:T(8,128)(2,1)}) custom-call(s32[3,32]{1,0:T(4,128)S(1)} %bitcast.8, f32[64,128,128]{2,1,0:T(8,128)S(1)} %get-tuple-element.117.acc_in, bf16[32,3,128,128]{3,2,1,0:T(8,128)(2,1)S(1)} %copy-done, ...), custom_call_target="tpu_custom_call", output_to_operand_aliasing={{0}: (1, {})} | custom-call | flops 4194304 | bytes 1048576 | tf_op jit(solution)/shard_map/pallas_call | solution.py:644
  56.0 3.6 %shard_map.137 = (f32[64,128,128]{2,1,0:T(8,128)S(1)}, f32[128,128]{1,0:T(8,128)S(1)}, f32[128,128]{1,0:T(8,128)S(1)}, f32[384,128]{1,0:T(8,128)S(1)}, bf16[16,1...) custom-call(s32[3,32]{1,0:T(4,128)S(1)} %bitcast.9, ...), custom_call_target="tpu_custom_call", output_to_operand_aliasing={{0}: (13, {})} | custom-call | flops 536870912 | bytes 8388608 | tf_op jit(solution)/shard_map/pallas_call | solution.py:644
  59.6 6.1 %collective-permute-done.8.rim = bf16[16,128,128]{2,1,0:T(8,128)(2,1)S(1)} collective-permute-done((bf16[16,128,128]{2,1,0:T(8,128)(2,1)S(1)}, bf16[16,128,128]{2,1,0:T(8,128)(2,1)S(1)}, u32[]{:S(2)}, u32[]{:S(2)}) %collective-permute-start.8) | collective-permute-done | bytes 524320 | tf_op jit(solution)/shard_map/ppermute | solution.py:62
  65.7 3.9 %shard_map.138 = (bf16[16,128,128]{2,1,0:T(8,128)(2,1)}, bf16[32,32,128]{2,1,0:T(8,128)(2,1)}, bf16[16,128,128]{2,1,0:T(8,128)(2,1)}, f32[32,128,128]{2,1,0:T(8,...) custom-call(s32[3,32]{1,0:T(4,128)S(1)} %bitcast.10, ...), custom_call_target="tpu_custom_call", output_to_operand_aliasing={{4}: (15, {}), {5}: (16, {}), {6}: (17, {}), {7}: (18, {})} | custom-call | flops 536870912 | bytes 8388608 | tf_op jit(solution)/shard_map/pallas_call | solution.py:644
  69.6 4.9 %all-to-all-start = ((bf16[32,32,128]{2,1,0:T(8,128)(2,1)}), bf16[32,32,128]{2,1,0:T(8,128)(2,1)S(1)}, u32[]{:S(2)}, u32[]{:S(2)}) async-start(bf16[32,32,128]{2,1,0:T(8,128)(2,1)} %get-tuple-element.160), calls=%async_computation | async-start | bytes 524288 | tf_op jit(solution)/shard_map/all_to_all | solution.py:766
  74.8 1.5 %collective-permute-start.9 = (bf16[16,128,128]{2,1,0:T(8,128)(2,1)}, bf16[16,128,128]{2,1,0:T(8,128)(2,1)S(1)}, u32[]{:S(2)}, u32[]{:S(2)}) collective-permute-start(bf16[16,128,128]{2,1,0:T(8,128)(2,1)} %get-tuple-element.156), channel_id=1, source_target_pairs={{1,2},{2,1},{3,4},{4,3},{5,6},{6,5},{7,8},{8,7},{9,10},{10,9},{11,... | collective-permute-start | bytes 1572872 | tf_op jit(solution)/shard_map/ppermute | solution.py:62
  76.3 9.2 %all-to-all-done.parts = bf16[32,32,128]{2,1,0:T(8,128)(2,1)S(1)} async-done(((bf16[32,32,128]{2,1,0:T(8,128)(2,1)}), bf16[32,32,128]{2,1,0:T(8,128)(2,1)S(1)}, u32[]{:S(2)}, u32[]{:S(2)}) %all-to-all-start) | async-done | bytes 262176 | tf_op jit(solution)/shard_map/all_to_all | solution.py:766
  85.5 1.3 %shard_map.140 = (bf16[32,24,128]{2,1,0:T(8,128)(2,1)}, f32[2,128]{1,0:T(2,128)}, f32[2,128]{1,0:T(2,128)}) custom-call(bf16[32,32,128]{2,1,0:T(8,128)(2,1)S(1)} %all-to-all-done.parts), custom_call_target="tpu_custom_call" | custom-call | flops 524288 | bytes 1048576 | tf_op jit(solution)/shard_map/pallas_call | solution.py:644
  86.8 6.7 %all-to-all-start.1 = ((bf16[32,24,128]{2,1,0:T(8,128)(2,1)}), bf16[32,24,128]{2,1,0:T(8,128)(2,1)S(1)}, u32[]{:S(2)}, u32[]{:S(2)}) async-start(bf16[32,24,128]{2,1,0:T(8,128)(2,1)} %get-tuple-element.161), calls=%async_computation.1 | async-start | bytes 393216 | tf_op jit(solution)/shard_map/all_to_all | solution.py:779
  93.6 2.9 %shard_map.136 = bf16[4096,128]{1,0:T(8,128)(2,1)} custom-call(bf16[32,128,128]{2,1,0:T(8,128)(2,1)} %get-tuple-element.133.h_hbm), custom_call_target="tpu_custom_call" | custom-call | flops 134217728 | bytes 2097152 | tf_op jit(solution)/shard_map/pallas_call | solution.py:644
  96.5 7.2 %shard_map.139 = f32[4096,128]{1,0:T(8,128)} custom-call(s32[3,32]{1,0:T(4,128)S(1)} %bitcast.11, bf16[16,128,128]{2,1,0:T(8,128)(2,1)S(1)} %collective-permute-done.7.near, bf16[16,128,128]{2,1,0:T(8,128)(2,1)S(1)} %collective-permute-done.9.far, f32[32,128,128]{2,1,0:T(8,128)} %get-tuple-element.157.acc_hbm, ...), custom_call_target="tpu_custom_call" | custom-call | flops 268435456 | bytes 9437184 | tf_op jit(solution)/shard_map/pallas_call | solution.py:644
  103.7 0.8 shard_map.141
  (23 shorter events, 0.8 us)
Async XLA Ops:
  2.4 0.7 copy-start.4
  3.1 0.7 copy-start.6
  3.8 0.7 copy-start.7
  4.5 17.3 %copy-start = (bf16[32,3,128,128]{3,2,1,0:T(8,128)(2,1)S(1)}, bf16[32,3,128,128]{3,2,1,0:T(8,128)(2,1)}, u32[]{:S(2)}) copy-start(bf16[32,3,128,128]{3,2,1,0:T(8,128)(2,1)} %tiles_hbm.3) | copy-start | bytes 9437188
  10.1 16.0 %collective-permute-start = (bf16[16,128,128]{2,1,0:T(8,128)(2,1)S(1)}, bf16[16,128,128]{2,1,0:T(8,128)(2,1)S(1)}, u32[]{:S(2)}, u32[]{:S(2)}) collective-permute-start(bf16[16,128,128]{2,1,0:T(8,128)(2,1)S(1)} %get-tuple-element.87), channel_id=1, source_target_pairs={{0,1},{1,0},{2,3},{3,2},{4,5},{5,4},{6,7},{7,6},{8,9},{9,8},{10,11... | collective-permute-start | bytes 1572872 | tf_op jit(solution)/shard_map/ppermute | solution.py:62
  10.1 11.6 %collective-permute-start.2 = (bf16[8,128,128]{2,1,0:T(8,128)(2,1)S(1)}, bf16[8,128,128]{2,1,0:T(8,128)(2,1)S(1)}, u32[]{:S(2)}, u32[]{:S(2)}) collective-permute-start(bf16[8,128,128]{2,1,0:T(8,128)(2,1)S(1)} %get-tuple-element.89), channel_id=1, source_target_pairs={{1,2},{2,1},{3,4},{4,3},{5,6},{6,5},{7,8},{8,7},{9,10},{10,9},{11,... | collective-permute-start | bytes 786440 | tf_op jit(solution)/shard_map/ppermute | solution.py:62
  12.8 11.7 %collective-permute-start.1 = (bf16[8,128,128]{2,1,0:T(8,128)(2,1)S(1)}, bf16[8,128,128]{2,1,0:T(8,128)(2,1)S(1)}, u32[]{:S(2)}, u32[]{:S(2)}) collective-permute-start(bf16[8,128,128]{2,1,0:T(8,128)(2,1)S(1)} %get-tuple-element.88), channel_id=1, source_target_pairs={{1,2},{2,1},{3,4},{4,3},{5,6},{6,5},{7,8},{8,7},{9,10},{10,9},{11,... | collective-permute-start | bytes 786440 | tf_op jit(solution)/shard_map/ppermute | solution.py:62
  26.1 6.0 %copy-start.3 = (bf16[4096,128]{1,0:T(8,128)(2,1)S(1)}, bf16[4096,128]{1,0:T(8,128)(2,1)}, u32[]{:S(2)}) copy-start(bf16[4096,128]{1,0:T(8,128)(2,1)} %cot.1) | copy-start | bytes 3145732
  26.1 6.0 %copy-start.5 = (s32[32,3]{0,1:T(4,128)S(1)}, s32[32,3]{0,1:T(4,128)}, u32[]{:S(2)}) copy-start(s32[32,3]{0,1:T(4,128)} %param.10) | copy-start | bytes 1156
  28.2 19.6 %collective-permute-start.3 = (bf16[16,128,128]{2,1,0:T(8,128)(2,1)S(1)}, bf16[16,128,128]{2,1,0:T(8,128)(2,1)S(1)}, u32[]{:S(2)}, u32[]{:S(2)}) collective-permute-start(bf16[16,128,128]{2,1,0:T(8,128)(2,1)S(1)} %get-tuple-element.105), channel_id=1, source_target_pairs={{0,1},{1,0},{2,3},{3,2},{4,5},{5,4},{6,7},{7,6},{8,9},{9,8},{10,11... | collective-permute-start | bytes 1572872 | tf_op jit(solution)/shard_map/ppermute | solution.py:62
  30.3 9.4 %collective-permute-start.4 = (bf16[8,128,128]{2,1,0:T(8,128)(2,1)S(1)}, bf16[8,128,128]{2,1,0:T(8,128)(2,1)S(1)}, u32[]{:S(2)}, u32[]{:S(2)}) collective-permute-start(bf16[8,128,128]{2,1,0:T(8,128)(2,1)S(1)} %get-tuple-element.106), channel_id=1, source_target_pairs={{1,2},{2,1},{3,4},{4,3},{5,6},{6,5},{7,8},{8,7},{9,10},{10,9},{11,... | collective-permute-start | bytes 786440 | tf_op jit(solution)/shard_map/ppermute | solution.py:62
  30.9 13.7 %collective-permute-start.5 = (bf16[8,128,128]{2,1,0:T(8,128)(2,1)S(1)}, bf16[8,128,128]{2,1,0:T(8,128)(2,1)S(1)}, u32[]{:S(2)}, u32[]{:S(2)}) collective-permute-start(bf16[8,128,128]{2,1,0:T(8,128)(2,1)S(1)} %get-tuple-element.112), channel_id=1, source_target_pairs={{1,2},{2,1},{3,4},{4,3},{5,6},{6,5},{7,8},{8,7},{9,10},{10,9},{11,... | collective-permute-start | bytes 786440 | tf_op jit(solution)/shard_map/ppermute | solution.py:62
  32.1 12.5 %copy-start.2 = (bf16[2,256,128]{2,1,0:T(8,128)(2,1)S(1)}, bf16[2,256,128]{2,1,0:T(8,128)(2,1)}, u32[]{:S(2)}) copy-start(bf16[2,256,128]{2,1,0:T(8,128)(2,1)} %w_in.7) | copy-start | bytes 393220
  51.2 4.8 %collective-permute-start.6 = (bf16[16,128,128]{2,1,0:T(8,128)(2,1)S(1)}, bf16[16,128,128]{2,1,0:T(8,128)(2,1)S(1)}, u32[]{:S(2)}, u32[]{:S(2)}) collective-permute-start(bf16[16,128,128]{2,1,0:T(8,128)(2,1)S(1)} %get-tuple-element.134), channel_id=1, source_target_pairs={{0,1},{1,0},{2,3},{3,2},{4,5},{5,4},{6,7},{7,6},{8,9},{9,8},{10,11... | collective-permute-start | bytes 1572872 | tf_op jit(solution)/shard_map/ppermute | solution.py:62
  51.5 14.2 %collective-permute-start.8 = (bf16[16,128,128]{2,1,0:T(8,128)(2,1)S(1)}, bf16[16,128,128]{2,1,0:T(8,128)(2,1)S(1)}, u32[]{:S(2)}, u32[]{:S(2)}) collective-permute-start(bf16[16,128,128]{2,1,0:T(8,128)(2,1)S(1)} %get-tuple-element.144), channel_id=1, source_target_pairs={{1,2},{2,1},{3,4},{4,3},{5,6},{6,5},{7,8},{8,7},{9,10},{10,9},{11,... | collective-permute-start | bytes 1572872 | tf_op jit(solution)/shard_map/ppermute | solution.py:62
  51.9 4.1 %copy-start.1 = (bf16[32,128,128]{2,1,0:T(8,128)(2,1)S(1)}, bf16[32,128,128]{2,1,0:T(8,128)(2,1)}, u32[]{:S(2)}) copy-start(bf16[32,128,128]{2,1,0:T(8,128)(2,1)} %get-tuple-element.136.kept) | copy-start | bytes 3145732
  69.6 15.9 %all-to-all-start = ((bf16[32,32,128]{2,1,0:T(8,128)(2,1)}), bf16[32,32,128]{2,1,0:T(8,128)(2,1)S(1)}, u32[]{:S(2)}, u32[]{:S(2)}) async-start(bf16[32,32,128]{2,1,0:T(8,128)(2,1)} %get-tuple-element.160), calls=%async_computation | async-start | bytes 524288 | tf_op jit(solution)/shard_map/all_to_all | solution.py:766
  74.5 22.0 %collective-permute-start.7 = (bf16[16,128,128]{2,1,0:T(8,128)(2,1)}, bf16[16,128,128]{2,1,0:T(8,128)(2,1)S(1)}, u32[]{:S(2)}, u32[]{:S(2)}) collective-permute-start(bf16[16,128,128]{2,1,0:T(8,128)(2,1)} %get-tuple-element.143), channel_id=1, source_target_pairs={{0,1},{1,0},{2,3},{3,2},{4,5},{5,4},{6,7},{7,6},{8,9},{9,8},{10,11... | collective-permute-start | bytes 1572872 | tf_op jit(solution)/shard_map/ppermute | solution.py:62
  74.8 21.7 %collective-permute-start.9 = (bf16[16,128,128]{2,1,0:T(8,128)(2,1)}, bf16[16,128,128]{2,1,0:T(8,128)(2,1)S(1)}, u32[]{:S(2)}, u32[]{:S(2)}) collective-permute-start(bf16[16,128,128]{2,1,0:T(8,128)(2,1)} %get-tuple-element.156), channel_id=1, source_target_pairs={{1,2},{2,1},{3,4},{4,3},{5,6},{6,5},{7,8},{8,7},{9,10},{10,9},{11,... | collective-permute-start | bytes 1572872 | tf_op jit(solution)/shard_map/ppermute | solution.py:62
  86.8 16.9 %all-to-all-start.1 = ((bf16[32,24,128]{2,1,0:T(8,128)(2,1)}), bf16[32,24,128]{2,1,0:T(8,128)(2,1)S(1)}, u32[]{:S(2)}, u32[]{:S(2)}) async-start(bf16[32,24,128]{2,1,0:T(8,128)(2,1)} %get-tuple-element.161), calls=%async_computation.1 | async-start | bytes 393216 | tf_op jit(solution)/shard_map/all_to_all | solution.py:779

commit v6 on v5

--- a/solution.py
+++ b/solution.py
@@ -169,8 +169,8 @@
 
 
 def inner0_kernel(
-    nb, offs, ext_in, x_hbm, tiles_hbm, w_in_hbm, w_out_hbm, bias, gain,
-    ext, near, part, w1t, w2t, w2, bcols, gcols, kept, x, tiles, w_in, w_out, sem, tsem,
+    nb, offs, ext_in, x_hbm, tiles_hbm, w_in_hbm, w_out_hbm, bias_hbm, gain_hbm,
+    ext, near, part, w1t, w2t, w2, bcols, gcols, kept, x, tiles, w_in, w_out, bias, gain, sem, tsem,
 ):
     base = rows_at(False)
     per = nb // tsem.shape[0]
@@ -183,6 +183,8 @@
     gets = [
         pltpu.make_async_copy(w_in_hbm, w_in, sem.at[2]),
         pltpu.make_async_copy(w_out_hbm, w_out, sem.at[3]),
+        pltpu.make_async_copy(bias_hbm, bias, sem.at[4]),
+        pltpu.make_async_copy(gain_hbm, gain, sem.at[5]),
     ]
     get.start()
     for it in range(nb // per):
@@ -696,8 +698,8 @@
         part_of(inner0_kernel, nb), (offs, h0, feats, tile_vals, w_in, w_out, bias_in, gain),
         [(ext, BF16), (half, BF16), (full, F32), ((layers, hid, 2 * width), BF16), ((layers, width, hid), BF16),
          (w_out.shape, BF16), ((layers, *block), F32), ((layers, *block), F32), (full, BF16, True)],
-        [v(half_rows, BF16), v(tile_vals.shape, BF16), v(w_in.shape, BF16), v(w_out.shape, BF16), dma(4), dma(8)],
-        {1: 0}, far_args=(2, 3, 4, 5),
+        [v(half_rows, BF16), v(tile_vals.shape, BF16), v(w_in.shape, BF16), v(w_out.shape, BF16), v(bias_in.shape, F32), v(gain.shape, F32), dma(6), dma(8)],
+        {1: 0}, far_args=(2, 3, 4, 5, 6, 7),
         flops=2 * nb * tile_flops, moved=6 * mib,
     )
     near = swap(near, False)

time: 105 us -> 104 us (level)
  local copies, waits for them, and re-layouts: 2.06 us -> 0.7 us
    unnamed x16 -> x12, local copies, waits for them, and re-layouts: 2.06 us -> 0.7 us
where the time goes in v6:
time: 104 us; the launch traced here: 103 us
  Pallas kernels  47.4 us (46%)
  waiting for transfers between devices  33.2 us (32%)
  starting transfers between devices  20.8 us (20%)
    pallas_call x15, Pallas kernels, call(): pl.pallas_call(body, in_specs=[HBM if i in far_args else ANY if i in any_...  47.4 us
    ppermute x10, waiting for transfers between devices, swap(): return lax.ppermute(x, AXES, pairs)  24 us
    all_to_all x1, waiting for transfers between devices, per_device(): parts = lax.all_to_all(bundle, AXES, 0, 0, tiled=True)  9.19 us
    ppermute x10, starting transfers between devices, swap(): return lax.ppermute(x, AXES, pairs)  9.16 us
    all_to_all x1, starting transfers between devices, per_device(): sums = lax.all_to_all(mine, AXES, 0, 0, tiled=True)  6.74 us
    all_to_all x1, starting transfers between devices, per_device(): parts = lax.all_to_all(bundle, AXES, 0, 0, tiled=True)  4.88 us
  transfers between devices with their start and end apart: 12, of which 6 were waited for; matrix products, arithmetic and copies ran while one was open for 0% of the time, Pallas kernels for 29%

profile of v6, /device:TPU:1, one launch (start us, length us, event | category | flops | bytes accessed | tf_op | source)
XLA Modules:
  0.0 103.1 jit_solution(212203828258815358)
XLA Ops:
  0.6 1.8 %shard_map.127 = (bf16[64,128,128]{2,1,0:T(8,128)(2,1)S(1)}, bf16[8,128,128]{2,1,0:T(8,128)(2,1)S(1)}, bf16[8,128,128]{2,1,0:T(8,128)(2,1)S(1)}) custom-call(bf16[4096,128]{1,0:T(8,128)(2,1)} %x_hbm.3), custom_call_target="tpu_custom_call" | custom-call | flops 134217728 | bytes 3145728 | tf_op jit(solution)/shard_map/pallas_call | solution.py:646
  2.5 0.7 copy-done.4
  3.1 5.3 %shard_map.128 = (bf16[64,128,128]{2,1,0:T(8,128)(2,1)S(1)}, bf16[16,128,128]{2,1,0:T(8,128)(2,1)S(1)}, f32[32,128,128]{2,1,0:T(8,128)S(1)}, bf16[2,128,256]{2,1...) custom-call(s32[3,32]{1,0:T(4,128)S(1)} %bitcast.1, ...), custom_call_target="tpu_custom_call", output_to_operand_aliasing={{0}: (1, {})} | custom-call | flops 268435456 | bytes 6291456 | tf_op jit(solution)/shard_map/pallas_call | solution.py:646
  8.6 2.7 %collective-permute-start.2 = (bf16[8,128,128]{2,1,0:T(8,128)(2,1)S(1)}, bf16[8,128,128]{2,1,0:T(8,128)(2,1)S(1)}, u32[]{:S(2)}, u32[]{:S(2)}) collective-permute-start(bf16[8,128,128]{2,1,0:T(8,128)(2,1)S(1)} %get-tuple-element.89), channel_id=1, source_target_pairs={{1,2},{2,1},{3,4},{4,3},{5,6},{6,5},{7,8},{8,7},{9,10},{10,9},{11,... | collective-permute-start | bytes 786440 | tf_op jit(solution)/shard_map/ppermute | solution.py:62
  11.3 8.9 %collective-permute-done.2.rim = bf16[8,128,128]{2,1,0:T(8,128)(2,1)S(1)} collective-permute-done((bf16[8,128,128]{2,1,0:T(8,128)(2,1)S(1)}, bf16[8,128,128]{2,1,0:T(8,128)(2,1)S(1)}, u32[]{:S(2)}, u32[]{:S(2)}) %collective-permute-start.2) | collective-permute-done | bytes 262176 | tf_op jit(solution)/shard_map/ppermute | solution.py:62
  20.2 1.5 %shard_map.129 = (bf16[8,128,128]{2,1,0:T(8,128)(2,1)S(1)}, bf16[64,128,128]{2,1,0:T(8,128)(2,1)S(1)}, bf16[64,128,128]{2,1,0:T(8,128)(2,1)S(1)}, bf16[16,128,12...) custom-call(s32[3,32]{1,0:T(4,128)S(1)} %bitcast.2, ...), custom_call_target="tpu_custom_call", output_to_operand_aliasing={{1}: (2, {})} | custom-call | flops 134217728 | bytes 4194304 | tf_op jit(solution)/shard_map/pallas_call | solution.py:646
  21.6 1.3 %collective-permute-done.1.rim = bf16[8,128,128]{2,1,0:T(8,128)(2,1)S(1)} collective-permute-done((bf16[8,128,128]{2,1,0:T(8,128)(2,1)S(1)}, bf16[8,128,128]{2,1,0:T(8,128)(2,1)S(1)}, u32[]{:S(2)}, u32[]{:S(2)}) %collective-permute-start.1) | collective-permute-done | bytes 262176 | tf_op jit(solution)/shard_map/ppermute | solution.py:62
  23.0 1.5 %shard_map.130 = (bf16[8,128,128]{2,1,0:T(8,128)(2,1)S(1)}, bf16[64,128,128]{2,1,0:T(8,128)(2,1)S(1)}, bf16[64,128,128]{2,1,0:T(8,128)(2,1)S(1)}, bf16[16,128,12...) custom-call(s32[3,32]{1,0:T(4,128)S(1)} %bitcast.3, ...), custom_call_target="tpu_custom_call", output_to_operand_aliasing={{1}: (2, {}), {2}: (9, {}), {3}: (10, {}), {4}: (11, {}), {... | custom-call | flops 134217728 | bytes 4194304 | tf_op jit(solution)/shard_map/pallas_call | solution.py:646
  24.5 2.1 %shard_map.131 = (bf16[16,128,128]{2,1,0:T(8,128)(2,1)S(1)}, bf16[64,128,128]{2,1,0:T(8,128)(2,1)S(1)}, bf16[64,128,128]{2,1,0:T(8,128)(2,1)S(1)}, bf16[16,128,1...) custom-call(s32[3,32]{1,0:T(4,128)S(1)} %bitcast.4, ...), custom_call_target="tpu_custom_call", output_to_operand_aliasing={{1}: (2, {}), {2}: (9, {})} | custom-call | flops 134217728 | bytes 4194304 | tf_op jit(solution)/shard_map/pallas_call | solution.py:646
  26.6 2.1 %collective-permute-start.3 = (bf16[16,128,128]{2,1,0:T(8,128)(2,1)S(1)}, bf16[16,128,128]{2,1,0:T(8,128)(2,1)S(1)}, u32[]{:S(2)}, u32[]{:S(2)}) collective-permute-start(bf16[16,128,128]{2,1,0:T(8,128)(2,1)S(1)} %get-tuple-element.105), channel_id=1, source_target_pairs={{0,1},{1,0},{2,3},{3,2},{4,5},{5,4},{6,7},{7,6},{8,9},{9,8},{10,11... | collective-permute-start | bytes 1572872 | tf_op jit(solution)/shard_map/ppermute | solution.py:62
  28.8 0.5 collective-permute-start.4
  29.3 1.2 %collective-permute-start.5 = (bf16[8,128,128]{2,1,0:T(8,128)(2,1)S(1)}, bf16[8,128,128]{2,1,0:T(8,128)(2,1)S(1)}, u32[]{:S(2)}, u32[]{:S(2)}) collective-permute-start(bf16[8,128,128]{2,1,0:T(8,128)(2,1)S(1)} %get-tuple-element.112), channel_id=1, source_target_pairs={{1,2},{2,1},{3,4},{4,3},{5,6},{6,5},{7,8},{8,7},{9,10},{10,9},{11,... | collective-permute-start | bytes 786440 | tf_op jit(solution)/shard_map/ppermute | solution.py:62
  30.5 4.7 %shard_map.132 = (f32[32,128,128]{2,1,0:T(8,128)S(1)}, bf16[32,128,128]{2,1,0:T(8,128)(2,1)S(1)}, f32[64,128,128]{2,1,0:T(8,128)S(1)}, f32[64,128,128]{2,1,0:T(8,128)S(1)}) custom-call(s32[3,32]{1,0:T(4,128)S(1)} %bitcast.5, bf16[64,128,128]{2,1,0:T(8,128)(2,1)S(1)} %get-tuple-element.107.ext.ext_in, bf16[32,3,128,128]{3,2,1,0:T(8,128)(2,1)S(1)} %copy-done, ...), custom_call_target="tpu_custom_call" | custom-call | flops 268435456 | bytes 8388608 | tf_op jit(solution)/shard_map/pallas_call | solution.py:646
  35.2 3.0 %collective-permute-done.4.rim = bf16[8,128,128]{2,1,0:T(8,128)(2,1)S(1)} collective-permute-done((bf16[8,128,128]{2,1,0:T(8,128)(2,1)S(1)}, bf16[8,128,128]{2,1,0:T(8,128)(2,1)S(1)}, u32[]{:S(2)}, u32[]{:S(2)}) %collective-permute-start.4) | collective-permute-done | bytes 262176 | tf_op jit(solution)/shard_map/ppermute | solution.py:62
  38.2 4.8 %collective-permute-done.5.refs_1_ = bf16[8,128,128]{2,1,0:T(8,128)(2,1)S(1)} collective-permute-done((bf16[8,128,128]{2,1,0:T(8,128)(2,1)S(1)}, bf16[8,128,128]{2,1,0:T(8,128)(2,1)S(1)}, u32[]{:S(2)}, u32[]{:S(2)}) %collective-permute-start.5) | collective-permute-done | bytes 262176 | tf_op jit(solution)/shard_map/ppermute | solution.py:62
  43.0 3.3 %shard_map.133 = (bf16[16,128,128]{2,1,0:T(8,128)(2,1)S(1)}, bf16[64,128,128]{2,1,0:T(8,128)(2,1)S(1)}, bf16[16,128,128]{2,1,0:T(8,128)(2,1)S(1)}, bf16[16,128,1...) custom-call(s32[3,32]{1,0:T(4,128)S(1)} %bitcast.6, ...), custom_call_target="tpu_custom_call", output_to_operand_aliasing={{1}: (2, {}), {8}: (12, {})} | custom-call | flops 536870912 | bytes 8388608 | tf_op jit(solution)/shard_map/pallas_call | solution.py:646
  46.3 3.3 %shard_map.134 = (bf16[16,128,128]{2,1,0:T(8,128)(2,1)S(1)}, bf16[64,128,128]{2,1,0:T(8,128)(2,1)S(1)}, bf16[16,128,128]{2,1,0:T(8,128)(2,1)S(1)}, bf16[16,128,1...) custom-call(s32[3,32]{1,0:T(4,128)S(1)} %bitcast.7, ...), custom_call_target="tpu_custom_call", output_to_operand_aliasing={{1}: (2, {}), {8}: (12, {}), {9}: (13, {}), {10}: (14, {})} | custom-call | flops 536870912 | bytes 8388608 | tf_op jit(solution)/shard_map/pallas_call | solution.py:646
  49.6 0.3 collective-permute-start.6
  49.9 0.4 collective-permute-start.8
  50.3 4.1 %shard_map.135 = (f32[64,128,128]{2,1,0:T(8,128)S(1)}, f32[384,128]{1,0:T(8,128)S(1)}, f32[2,128]{1,0:T(2,128)S(1)}, bf16[32,128,128]{2,1,0:T(8,128)(2,1)}) custom-call(s32[3,32]{1,0:T(4,128)S(1)} %bitcast.8, f32[64,128,128]{2,1,0:T(8,128)S(1)} %get-tuple-element.117.acc_in, bf16[32,3,128,128]{3,2,1,0:T(8,128)(2,1)S(1)} %copy-done, ...), custom_call_target="tpu_custom_call", output_to_operand_aliasing={{0}: (1, {})} | custom-call | flops 4194304 | bytes 1048576 | tf_op jit(solution)/shard_map/pallas_call | solution.py:646
  54.4 3.6 %shard_map.137 = (f32[64,128,128]{2,1,0:T(8,128)S(1)}, f32[128,128]{1,0:T(8,128)S(1)}, f32[128,128]{1,0:T(8,128)S(1)}, f32[384,128]{1,0:T(8,128)S(1)}, bf16[16,1...) custom-call(s32[3,32]{1,0:T(4,128)S(1)} %bitcast.9, ...), custom_call_target="tpu_custom_call", output_to_operand_aliasing={{0}: (13, {})} | custom-call | flops 536870912 | bytes 8388608 | tf_op jit(solution)/shard_map/pallas_call | solution.py:646
  58.0 6.1 %collective-permute-done.8.rim = bf16[16,128,128]{2,1,0:T(8,128)(2,1)S(1)} collective-permute-done((bf16[16,128,128]{2,1,0:T(8,128)(2,1)S(1)}, bf16[16,128,128]{2,1,0:T(8,128)(2,1)S(1)}, u32[]{:S(2)}, u32[]{:S(2)}) %collective-permute-start.8) | collective-permute-done | bytes 524320 | tf_op jit(solution)/shard_map/ppermute | solution.py:62
  64.1 3.9 %shard_map.138 = (bf16[16,128,128]{2,1,0:T(8,128)(2,1)}, bf16[32,32,128]{2,1,0:T(8,128)(2,1)}, bf16[16,128,128]{2,1,0:T(8,128)(2,1)}, f32[32,128,128]{2,1,0:T(8,...) custom-call(s32[3,32]{1,0:T(4,128)S(1)} %bitcast.10, ...), custom_call_target="tpu_custom_call", output_to_operand_aliasing={{4}: (15, {}), {5}: (16, {}), {6}: (17, {}), {7}: (18, {})} | custom-call | flops 536870912 | bytes 8388608 | tf_op jit(solution)/shard_map/pallas_call | solution.py:646
  68.0 4.9 %all-to-all-start = ((bf16[32,32,128]{2,1,0:T(8,128)(2,1)}), bf16[32,32,128]{2,1,0:T(8,128)(2,1)S(1)}, u32[]{:S(2)}, u32[]{:S(2)}) async-start(bf16[32,32,128]{2,1,0:T(8,128)(2,1)} %get-tuple-element.160), calls=%async_computation | async-start | bytes 524288 | tf_op jit(solution)/shard_map/all_to_all | solution.py:768
  72.9 0.3 collective-permute-start.7
  73.3 1.5 %collective-permute-start.9 = (bf16[16,128,128]{2,1,0:T(8,128)(2,1)}, bf16[16,128,128]{2,1,0:T(8,128)(2,1)S(1)}, u32[]{:S(2)}, u32[]{:S(2)}) collective-permute-start(bf16[16,128,128]{2,1,0:T(8,128)(2,1)} %get-tuple-element.156), channel_id=1, source_target_pairs={{1,2},{2,1},{3,4},{4,3},{5,6},{6,5},{7,8},{8,7},{9,10},{10,9},{11,... | collective-permute-start | bytes 1572872 | tf_op jit(solution)/shard_map/ppermute | solution.py:62
  74.7 9.2 %all-to-all-done.parts = bf16[32,32,128]{2,1,0:T(8,128)(2,1)S(1)} async-done(((bf16[32,32,128]{2,1,0:T(8,128)(2,1)}), bf16[32,32,128]{2,1,0:T(8,128)(2,1)S(1)}, u32[]{:S(2)}, u32[]{:S(2)}) %all-to-all-start) | async-done | bytes 262176 | tf_op jit(solution)/shard_map/all_to_all | solution.py:768
  83.9 1.3 %shard_map.140 = (bf16[32,24,128]{2,1,0:T(8,128)(2,1)}, f32[2,128]{1,0:T(2,128)}, f32[2,128]{1,0:T(2,128)}) custom-call(bf16[32,32,128]{2,1,0:T(8,128)(2,1)S(1)} %all-to-all-done.parts), custom_call_target="tpu_custom_call" | custom-call | flops 524288 | bytes 1048576 | tf_op jit(solution)/shard_map/pallas_call | solution.py:646
  85.2 6.7 %all-to-all-start.1 = ((bf16[32,24,128]{2,1,0:T(8,128)(2,1)}), bf16[32,24,128]{2,1,0:T(8,128)(2,1)S(1)}, u32[]{:S(2)}, u32[]{:S(2)}) async-start(bf16[32,24,128]{2,1,0:T(8,128)(2,1)} %get-tuple-element.161), calls=%async_computation.1 | async-start | bytes 393216 | tf_op jit(solution)/shard_map/all_to_all | solution.py:781
  92.0 2.9 %shard_map.136 = bf16[4096,128]{1,0:T(8,128)(2,1)} custom-call(bf16[32,128,128]{2,1,0:T(8,128)(2,1)} %get-tuple-element.133.h_hbm), custom_call_target="tpu_custom_call" | custom-call | flops 134217728 | bytes 2097152 | tf_op jit(solution)/shard_map/pallas_call | solution.py:646
  94.9 7.2 %shard_map.139 = f32[4096,128]{1,0:T(8,128)} custom-call(s32[3,32]{1,0:T(4,128)S(1)} %bitcast.11, bf16[16,128,128]{2,1,0:T(8,128)(2,1)S(1)} %collective-permute-done.7.near, bf16[16,128,128]{2,1,0:T(8,128)(2,1)S(1)} %collective-permute-done.9.far, f32[32,128,128]{2,1,0:T(8,128)} %get-tuple-element.157.acc_hbm, ...), custom_call_target="tpu_custom_call" | custom-call | flops 268435456 | bytes 9437184 | tf_op jit(solution)/shard_map/pallas_call | solution.py:646
  102.1 0.8 shard_map.141
  (19 shorter events, 0.2 us)
Async XLA Ops:
  2.4 0.7 copy-start.4
  3.1 17.0 %copy-start = (bf16[32,3,128,128]{3,2,1,0:T(8,128)(2,1)S(1)}, bf16[32,3,128,128]{3,2,1,0:T(8,128)(2,1)}, u32[]{:S(2)}) copy-start(bf16[32,3,128,128]{3,2,1,0:T(8,128)(2,1)} %tiles_hbm.3) | copy-start | bytes 9437188
  8.5 16.0 %collective-permute-start = (bf16[16,128,128]{2,1,0:T(8,128)(2,1)S(1)}, bf16[16,128,128]{2,1,0:T(8,128)(2,1)S(1)}, u32[]{:S(2)}, u32[]{:S(2)}) collective-permute-start(bf16[16,128,128]{2,1,0:T(8,128)(2,1)S(1)} %get-tuple-element.87), channel_id=1, source_target_pairs={{0,1},{1,0},{2,3},{3,2},{4,5},{5,4},{6,7},{7,6},{8,9},{9,8},{10,11... | collective-permute-start | bytes 1572872 | tf_op jit(solution)/shard_map/ppermute | solution.py:62
  8.6 11.6 %collective-permute-start.2 = (bf16[8,128,128]{2,1,0:T(8,128)(2,1)S(1)}, bf16[8,128,128]{2,1,0:T(8,128)(2,1)S(1)}, u32[]{:S(2)}, u32[]{:S(2)}) collective-permute-start(bf16[8,128,128]{2,1,0:T(8,128)(2,1)S(1)} %get-tuple-element.89), channel_id=1, source_target_pairs={{1,2},{2,1},{3,4},{4,3},{5,6},{6,5},{7,8},{8,7},{9,10},{10,9},{11,... | collective-permute-start | bytes 786440 | tf_op jit(solution)/shard_map/ppermute | solution.py:62
  11.2 11.7 %collective-permute-start.1 = (bf16[8,128,128]{2,1,0:T(8,128)(2,1)S(1)}, bf16[8,128,128]{2,1,0:T(8,128)(2,1)S(1)}, u32[]{:S(2)}, u32[]{:S(2)}) collective-permute-start(bf16[8,128,128]{2,1,0:T(8,128)(2,1)S(1)} %get-tuple-element.88), channel_id=1, source_target_pairs={{1,2},{2,1},{3,4},{4,3},{5,6},{6,5},{7,8},{8,7},{9,10},{10,9},{11,... | collective-permute-start | bytes 786440 | tf_op jit(solution)/shard_map/ppermute | solution.py:62
  24.5 6.0 %copy-start.3 = (bf16[4096,128]{1,0:T(8,128)(2,1)S(1)}, bf16[4096,128]{1,0:T(8,128)(2,1)}, u32[]{:S(2)}) copy-start(bf16[4096,128]{1,0:T(8,128)(2,1)} %cot.1) | copy-start | bytes 3145732
  24.5 6.0 %copy-start.5 = (s32[32,3]{0,1:T(4,128)S(1)}, s32[32,3]{0,1:T(4,128)}, u32[]{:S(2)}) copy-start(s32[32,3]{0,1:T(4,128)} %param.10) | copy-start | bytes 1156
  26.6 19.6 %collective-permute-start.3 = (bf16[16,128,128]{2,1,0:T(8,128)(2,1)S(1)}, bf16[16,128,128]{2,1,0:T(8,128)(2,1)S(1)}, u32[]{:S(2)}, u32[]{:S(2)}) collective-permute-start(bf16[16,128,128]{2,1,0:T(8,128)(2,1)S(1)} %get-tuple-element.105), channel_id=1, source_target_pairs={{0,1},{1,0},{2,3},{3,2},{4,5},{5,4},{6,7},{7,6},{8,9},{9,8},{10,11... | collective-permute-start | bytes 1572872 | tf_op jit(solution)/shard_map/ppermute | solution.py:62
  28.8 9.4 %collective-permute-start.4 = (bf16[8,128,128]{2,1,0:T(8,128)(2,1)S(1)}, bf16[8,128,128]{2,1,0:T(8,128)(2,1)S(1)}, u32[]{:S(2)}, u32[]{:S(2)}) collective-permute-start(bf16[8,128,128]{2,1,0:T(8,128)(2,1)S(1)} %get-tuple-element.106), channel_id=1, source_target_pairs={{1,2},{2,1},{3,4},{4,3},{5,6},{6,5},{7,8},{8,7},{9,10},{10,9},{11,... | collective-permute-start | bytes 786440 | tf_op jit(solution)/shard_map/ppermute | solution.py:62
  29.3 13.7 %collective-permute-start.5 = (bf16[8,128,128]{2,1,0:T(8,128)(2,1)S(1)}, bf16[8,128,128]{2,1,0:T(8,128)(2,1)S(1)}, u32[]{:S(2)}, u32[]{:S(2)}) collective-permute-start(bf16[8,128,128]{2,1,0:T(8,128)(2,1)S(1)} %get-tuple-element.112), channel_id=1, source_target_pairs={{1,2},{2,1},{3,4},{4,3},{5,6},{6,5},{7,8},{8,7},{9,10},{10,9},{11,... | collective-permute-start | bytes 786440 | tf_op jit(solution)/shard_map/ppermute | solution.py:62
  30.5 12.5 %copy-start.2 = (bf16[2,256,128]{2,1,0:T(8,128)(2,1)S(1)}, bf16[2,256,128]{2,1,0:T(8,128)(2,1)}, u32[]{:S(2)}) copy-start(bf16[2,256,128]{2,1,0:T(8,128)(2,1)} %w_in.7) | copy-start | bytes 393220
  49.6 4.8 %collective-permute-start.6 = (bf16[16,128,128]{2,1,0:T(8,128)(2,1)S(1)}, bf16[16,128,128]{2,1,0:T(8,128)(2,1)S(1)}, u32[]{:S(2)}, u32[]{:S(2)}) collective-permute-start(bf16[16,128,128]{2,1,0:T(8,128)(2,1)S(1)} %get-tuple-element.134), channel_id=1, source_target_pairs={{0,1},{1,0},{2,3},{3,2},{4,5},{5,4},{6,7},{7,6},{8,9},{9,8},{10,11... | collective-permute-start | bytes 1572872 | tf_op jit(solution)/shard_map/ppermute | solution.py:62
  49.9 14.2 %collective-permute-start.8 = (bf16[16,128,128]{2,1,0:T(8,128)(2,1)S(1)}, bf16[16,128,128]{2,1,0:T(8,128)(2,1)S(1)}, u32[]{:S(2)}, u32[]{:S(2)}) collective-permute-start(bf16[16,128,128]{2,1,0:T(8,128)(2,1)S(1)} %get-tuple-element.144), channel_id=1, source_target_pairs={{1,2},{2,1},{3,4},{4,3},{5,6},{6,5},{7,8},{8,7},{9,10},{10,9},{11,... | collective-permute-start | bytes 1572872 | tf_op jit(solution)/shard_map/ppermute | solution.py:62
  50.3 4.1 %copy-start.1 = (bf16[32,128,128]{2,1,0:T(8,128)(2,1)S(1)}, bf16[32,128,128]{2,1,0:T(8,128)(2,1)}, u32[]{:S(2)}) copy-start(bf16[32,128,128]{2,1,0:T(8,128)(2,1)} %get-tuple-element.136.kept) | copy-start | bytes 3145732
  68.0 15.9 %all-to-all-start = ((bf16[32,32,128]{2,1,0:T(8,128)(2,1)}), bf16[32,32,128]{2,1,0:T(8,128)(2,1)S(1)}, u32[]{:S(2)}, u32[]{:S(2)}) async-start(bf16[32,32,128]{2,1,0:T(8,128)(2,1)} %get-tuple-element.160), calls=%async_computation | async-start | bytes 524288 | tf_op jit(solution)/shard_map/all_to_all | solution.py:768
  72.9 22.0 %collective-permute-start.7 = (bf16[16,128,128]{2,1,0:T(8,128)(2,1)}, bf16[16,128,128]{2,1,0:T(8,128)(2,1)S(1)}, u32[]{:S(2)}, u32[]{:S(2)}) collective-permute-start(bf16[16,128,128]{2,1,0:T(8,128)(2,1)} %get-tuple-element.143), channel_id=1, source_target_pairs={{0,1},{1,0},{2,3},{3,2},{4,5},{5,4},{6,7},{7,6},{8,9},{9,8},{10,11... | collective-permute-start | bytes 1572872 | tf_op jit(solution)/shard_map/ppermute | solution.py:62
  73.3 21.7 %collective-permute-start.9 = (bf16[16,128,128]{2,1,0:T(8,128)(2,1)}, bf16[16,128,128]{2,1,0:T(8,128)(2,1)S(1)}, u32[]{:S(2)}, u32[]{:S(2)}) collective-permute-start(bf16[16,128,128]{2,1,0:T(8,128)(2,1)} %get-tuple-element.156), channel_id=1, source_target_pairs={{1,2},{2,1},{3,4},{4,3},{5,6},{6,5},{7,8},{8,7},{9,10},{10,9},{11,... | collective-permute-start | bytes 1572872 | tf_op jit(solution)/shard_map/ppermute | solution.py:62
  85.2 16.9 %all-to-all-start.1 = ((bf16[32,24,128]{2,1,0:T(8,128)(2,1)}), bf16[32,24,128]{2,1,0:T(8,128)(2,1)S(1)}, u32[]{:S(2)}, u32[]{:S(2)}) async-start(bf16[32,24,128]{2,1,0:T(8,128)(2,1)} %get-tuple-element.161), calls=%async_computation.1 | async-start | bytes 393216 | tf_op jit(solution)/shard_map/all_to_all | solution.py:781
